TPU v7x, 32 devices: a whole 2x2x4 slice. The times are simulated.
32 devices in a mesh: seq: 8 (over z, y), dp: 4 (over x, core).
Axes of the slice: x: 2, y: 2, z: 4, core: 2. Of those that a mesh axis runs over, the one named last changes fastest.
Arguments:
- block_input: bfloat16 [4, 1024, 1536], P('dp', 'seq'), may hold values from -6 to 6
- query_proj: bfloat16 [4, 1024, 768], P('dp', 'seq'), may hold values from -8 to 8
- key_proj: bfloat16 [4, 1024, 768], P('dp', 'seq'), may hold values from -8 to 8
- value_proj: bfloat16 [4, 1024, 768], P('dp', 'seq'), may hold values from -6 to 6
- lengths: int32 [4], P('dp'), may hold values from 256 to 1024, as said below
- out_proj: bfloat16 [1536, 768], replicated, may hold values from -0.21875 to 0.21875
- kernel: float32 [31, 1536], replicated, may hold values from -1 to 1
- conv_bias: float32 [1536], replicated, may hold values from -3 to 3
- grad_output: bfloat16 [4, 1024, 1536], P('dp', 'seq'), may hold values from -6 to 6
Outputs:
- block_output: bfloat16 [4, 1024, 1536], P('dp', 'seq')
- grad_input: bfloat16 [4, 1024, 1536], P('dp', 'seq')
- grad_query: bfloat16 [4, 1024, 768], P('dp', 'seq')
- grad_out_proj: float32 [1536, 768], P('seq')
- grad_kernel: float32 [31, 1536], P(None, 'seq')
- grad_bias: float32 [1536], P('seq')
Inputs may be any that keep to these rules, and one draw needn't show every extreme that they name: `lengths`: frames at or after an utterance's length are padding; in every draw at least one utterance has all 1024 frames valid.
All inputs are finite; a program needn't handle non-finite values.
Results may differ from a plain program's by a relative error of at most 0.012.
The roundings to bfloat16 on the way count: a program that leaves them out, or rounds other values in their place, can miss the bound.
Values may be sent and summed in bfloat16 or wider, within the bound.
No kernel may reach another device: no remote copies, remote signals or barrier semaphores. Data moves between devices by JAX's collectives and lax.ppermute only.
A program may use at most 128 MiB of HBM per device.

v0:
```python
import math

import jax
import jax.numpy as jnp
from jax import lax
from jax.sharding import PartitionSpec as P

D = 1536
H = 8
HS = 96
KW = 31
HD = 768


def with_halo(x, sides, width):
    for axis, dim in sides:
        size, length = (lax.axis_size(axis), x.shape[dim])
        up = [(i, (i + 1) % size) for i in range(size - 1)]
        down = [(j, i) for i, j in up]
        last = lax.slice_in_dim(x, length - width, length, axis=dim)
        leading = lax.slice_in_dim(x, 0, width, axis=dim)
        before = lax.ppermute(last, axis, up)
        after = lax.ppermute(leading, axis, down)
        x = jnp.concatenate([before, x, after], axis=dim)
    return x


def forward_rows(query_one, key_one, value_one, key_valid, score_scale):
    row_total = query_one.shape[0]
    block_rows = math.gcd(row_total, 512)
    query_blocks = query_one.reshape(row_total // block_rows, block_rows, query_one.shape[1])

    def forward_one_block(query_block):
        scores = (
            lax.dot_general(
                query_block, key_one, (((1,), (1,)), ((), ())), preferred_element_type=jnp.float32
            )
            * score_scale
        )
        scores = jnp.where(key_valid[None, :], scores, -jnp.inf)
        row_top = jnp.max(scores, axis=-1, keepdims=True)
        log_total = row_top + jnp.log(jnp.sum(jnp.exp(scores - row_top), axis=-1, keepdims=True))
        weights = jnp.exp(scores - log_total).astype(jnp.bfloat16)
        return (jnp.dot(weights, value_one, preferred_element_type=jnp.float32), log_total[:, 0])

    outputs, log_totals = lax.map(forward_one_block, query_blocks)
    return (outputs.reshape(row_total, query_one.shape[1]), log_totals.reshape(row_total))


def backward_rows(
    query_one, key_one, value_one, grad_one, lse_one, delta_one, key_valid, score_scale
):
    row_total = query_one.shape[0]
    block_rows = math.gcd(row_total, 512)
    block_count = row_total // block_rows
    width = query_one.shape[1]

    def backward_one_block(items):
        query_block, grad_block, lse_block, delta_block = items
        scores = (
            lax.dot_general(
                query_block, key_one, (((1,), (1,)), ((), ())), preferred_element_type=jnp.float32
            )
            * score_scale
        )
        scores = jnp.where(key_valid[None, :], scores, -jnp.inf)
        probs = jnp.exp(scores - lse_block[:, None])
        grad_prob = lax.dot_general(
            grad_block, value_one, (((1,), (1,)), ((), ())), preferred_element_type=jnp.float32
        )
        grad_score = (probs * (grad_prob - delta_block[:, None])).astype(jnp.bfloat16)
        return jnp.dot(grad_score, key_one, preferred_element_type=jnp.float32) * score_scale

    results = lax.map(
        backward_one_block,
        (
            query_one.reshape(block_count, block_rows, width),
            grad_one.reshape(block_count, block_rows, width),
            lse_one.reshape(block_count, block_rows),
            delta_one.reshape(block_count, block_rows),
        ),
    )
    return results.reshape(row_total, width)


def on_device(
    block_input, query_proj, key_proj, value_proj, lengths, out_proj, kernel, conv_bias, grad_output
):
    frames_dev = block_input.shape[1]
    seq_count = lax.axis_size("seq")
    total_frames = frames_dev * seq_count
    first_frame = lax.axis_index("seq") * frames_dev
    utt_length = lengths[0]
    local_valid = first_frame + jnp.arange(frames_dev) < utt_length
    all_valid = jnp.arange(total_frames) < utt_length
    score_scale = 1.0 / math.sqrt(HS)
    halo_width = KW // 2
    group_size = seq_count // H
    sub_rows = frames_dev // group_size
    query_local = query_proj[0]

    def to_serving(matrix):
        return matrix.reshape(frames_dev, H, HS).transpose(1, 0, 2).reshape(seq_count, sub_rows, HS)

    def from_serving(returned):
        return returned.reshape(H, frames_dev, HS).transpose(1, 0, 2).reshape(frames_dev, HD)

    query_mine = lax.all_to_all(
        to_serving(query_local), "seq", split_axis=0, concat_axis=1, tiled=True
    )[0]
    key_send = jnp.repeat(
        key_proj[0].reshape(frames_dev, H, HS).transpose(1, 0, 2), group_size, axis=0
    )
    value_send = jnp.repeat(
        value_proj[0].reshape(frames_dev, H, HS).transpose(1, 0, 2), group_size, axis=0
    )
    key_mine, value_mine = (
        lax.all_to_all(key_send, "seq", split_axis=0, concat_axis=1, tiled=True),
        lax.all_to_all(value_send, "seq", split_axis=0, concat_axis=1, tiled=True),
    )
    key_mine = key_mine[0]
    value_mine = value_mine[0]
    head_out, head_lse = forward_rows(query_mine, key_mine, value_mine, all_valid, score_scale)
    head_attended = head_out.astype(jnp.bfloat16)
    attended = from_serving(
        lax.all_to_all(head_attended[None], "seq", split_axis=1, concat_axis=0, tiled=True)
    )
    projected = lax.dot_general(
        attended, out_proj, (((1,), (1,)), ((), ())), preferred_element_type=jnp.float32
    )
    mixed_rows = (block_input[0].astype(jnp.float32) + projected).astype(jnp.bfloat16)
    masked = jnp.where(local_valid[:, None], mixed_rows, jnp.zeros_like(mixed_rows))
    padded = with_halo(masked, (("seq", 0),), halo_width).astype(jnp.float32)
    conv_rows = jnp.broadcast_to(conv_bias, (frames_dev, D))
    for tap in range(KW):
        conv_rows = conv_rows + kernel[tap] * padded[tap : tap + frames_dev]
    gate_rows = jax.nn.sigmoid(conv_rows)
    block_output = jnp.where(
        local_valid[:, None], mixed_rows.astype(jnp.float32) + conv_rows * gate_rows, 0.0
    ).astype(jnp.bfloat16)
    grad_rows = jnp.where(local_valid[:, None], grad_output[0].astype(jnp.float32), 0.0)
    grad_conv = grad_rows * gate_rows * (1.0 + conv_rows * (1.0 - gate_rows))
    kernel_local = jnp.stack(
        [jnp.sum(grad_conv * padded[tap : tap + frames_dev], axis=0) for tap in range(KW)]
    )
    bias_local = jnp.sum(grad_conv, axis=0)
    grad_padded = with_halo(grad_conv, (("seq", 0),), halo_width)
    grad_masked = jnp.zeros((frames_dev, D), jnp.float32)
    for tap in range(KW):
        begin = 2 * halo_width - tap
        grad_masked = grad_masked + kernel[tap] * grad_padded[begin : begin + frames_dev]
    grad_input = (grad_rows + jnp.where(local_valid[:, None], grad_masked, 0.0)).astype(
        jnp.bfloat16
    )
    grad_attn = jnp.dot(grad_input, out_proj, preferred_element_type=jnp.float32).astype(
        jnp.bfloat16
    )
    grad_mine = lax.all_to_all(
        to_serving(grad_attn), "seq", split_axis=0, concat_axis=1, tiled=True
    )[0]
    delta_mine = jnp.sum(grad_mine.astype(jnp.float32) * head_attended.astype(jnp.float32), axis=-1)
    grad_q_mine = backward_rows(
        query_mine, key_mine, value_mine, grad_mine, head_lse, delta_mine, all_valid, score_scale
    ).astype(jnp.bfloat16)
    grad_query = from_serving(
        lax.all_to_all(grad_q_mine[None], "seq", split_axis=1, concat_axis=0, tiled=True)
    )
    term_block = lax.dot_general(
        grad_input, attended, (((0,), (0,)), ((), ())), preferred_element_type=jnp.float32
    )
    partial_rows = lax.psum_scatter(term_block, "seq", scatter_dimension=0, tiled=True)
    summed = lax.psum(partial_rows.astype(jnp.bfloat16), "dp").astype(jnp.float32)
    kernel_total, bias_total = lax.psum((kernel_local, bias_local), ("seq", "dp"))
    shard_width = D // seq_count
    offset = lax.axis_index("seq") * shard_width
    grad_kernel = lax.dynamic_slice_in_dim(kernel_total, offset, shard_width, 1)
    grad_bias = lax.dynamic_slice_in_dim(bias_total, offset, shard_width, 0)
    return (block_output[None], grad_input[None], grad_query[None], summed, grad_kernel, grad_bias)


def solution(mesh):
    placed = (
        P("dp", "seq", None),
        P("dp", "seq", None),
        P("dp", "seq", None),
        P("dp", "seq", None),
        P("dp"),
        P(),
        P(),
        P(),
        P("dp", "seq", None),
    )
    return jax.shard_map(
        on_device,
        mesh=mesh,
        in_specs=placed,
        out_specs=(
            P("dp", "seq", None),
            P("dp", "seq", None),
            P("dp", "seq", None),
            P("seq", None),
            P(None, "seq"),
            P("seq"),
        ),
        check_vma=False,
    )
```

profile of v0, /device:TPU:0, one launch (start us, length us, event | category | flops | bytes accessed | tf_op | source)
XLA Modules:
  0.0 321.5 jit_solution(12944451114000263372)
XLA Ops:
  8.0 1.9 copy.76
  9.9 7.3 %all-to-all-start = ((bf16[8,128,96]{1,2,0:T(8,128)(2,1)}), bf16[8,128,96]{1,2,0:T(8,128)(2,1)S(1)}, u32[]{:S(2)}, u32[]{:S(2)}) async-start(bf16[8,128,96]{1,2,0:T(8,128)(2,1)} %bitcast.3), calls=%async_computation | async-start | bytes 393216 | tf_op jit(solution)/shard_map/all_to_all | solution.py:108
  17.2 1.7 copy.78
  18.9 6.2 %all-to-all-done = bf16[8,128,96]{1,2,0:T(8,128)(2,1)S(1)} async-done(((bf16[8,128,96]{1,2,0:T(8,128)(2,1)}), bf16[8,128,96]{1,2,0:T(8,128)(2,1)S(1)}, u32[]{:S(2)}, u32[]{:S(2)}) %all-to-all-start) | async-done | bytes 196640 | tf_op jit(solution)/shard_map/all_to_all | solution.py:108
  25.1 3.4 %all-to-all-start.1 = ((bf16[8,128,96]{1,2,0:T(8,128)(2,1)}), bf16[8,128,96]{1,2,0:T(8,128)(2,1)S(1)}, u32[]{:S(2)}, u32[]{:S(2)}) async-start(bf16[8,128,96]{1,2,0:T(8,128)(2,1)} %bitcast.5), calls=%async_computation.1 | async-start | bytes 393216 | tf_op jit(solution)/shard_map/all_to_all | solution.py:118
  28.5 1.7 copy.80
  30.3 6.0 %all-to-all-done.1 = bf16[8,128,96]{1,2,0:T(8,128)(2,1)S(1)} async-done(((bf16[8,128,96]{1,2,0:T(8,128)(2,1)}), bf16[8,128,96]{1,2,0:T(8,128)(2,1)S(1)}, u32[]{:S(2)}, u32[]{:S(2)}) %all-to-all-start.1) | async-done | bytes 196640 | tf_op jit(solution)/shard_map/all_to_all | solution.py:118
  36.3 3.4 %all-to-all-start.2 = ((bf16[8,128,96]{1,2,0:T(8,128)(2,1)}), bf16[8,128,96]{1,2,0:T(8,128)(2,1)S(1)}, u32[]{:S(2)}, u32[]{:S(2)}) async-start(bf16[8,128,96]{1,2,0:T(8,128)(2,1)} %bitcast.7), calls=%async_computation.2 | async-start | bytes 393216 | tf_op jit(solution)/shard_map/all_to_all | solution.py:119
  40.0 7.3 %all-to-all-done.2 = bf16[8,128,96]{1,2,0:T(8,128)(2,1)S(1)} async-done(((bf16[8,128,96]{1,2,0:T(8,128)(2,1)}), bf16[8,128,96]{1,2,0:T(8,128)(2,1)S(1)}, u32[]{:S(2)}, u32[]{:S(2)}) %all-to-all-start.2) | async-done | bytes 196640 | tf_op jit(solution)/shard_map/all_to_all | solution.py:119
  47.6 4.6 %while.24 = (s32[]{:T(128)}, bf16[2,512,96]{1,2,0:T(8,128)(2,1)S(1)}, f32[2,512]{1,0:T(2,128)S(1)}, bf16[2,512,96]{2,1,0:T(8,128)(2,1)S(1)}, bf16[1024,96]{1,0:T...) while((s32[]{:T(128)}, ...), condition=%wide.region_3.4_spmd.clone, body=%wide.region_0.3_spmd.clone.sunk | while | flops 204997120 | bytes 7164021 | solution.py:46
  53.2 2.6 reshape.122
  56.3 3.7 %reduce.63 = bf16[1024,96]{1,0:T(8,128)(2,1)} reduce(bf16[1024,1,96]{2,1,0:T(2,128)(2,1)} %bitcast.115, bf16[]{:T(256)} %broadcast.73), dimensions={1}, to_apply=%bitcast.66.reduce_sub_computation | reduce | bytes 393218
  60.1 2.1 reshape.155
  62.1 3.4 %all-to-all-start.3 = ((bf16[8,2,6144]{2,1,0:T(2,128)(2,1)}), bf16[8,2,6144]{2,1,0:T(2,128)(2,1)S(1)}, u32[]{:S(2)}, u32[]{:S(2)}) async-start(bf16[8,2,6144]{2,1,0:T(2,128)(2,1)} %reshape.155), calls=%async_computation.3 | async-start | bytes 393216 | tf_op jit(solution)/shard_map/all_to_all | solution.py:126
  66.8 2.5 slice_reduce_fusion.30
  69.3 3.9 %all-to-all-done.3 = bf16[8,2,6144]{2,1,0:T(2,128)(2,1)S(1)} async-done(((bf16[8,2,6144]{2,1,0:T(2,128)(2,1)}), bf16[8,2,6144]{2,1,0:T(2,128)(2,1)S(1)}, u32[]{:S(2)}, u32[]{:S(2)}) %all-to-all-start.3) | async-done | bytes 196640 | tf_op jit(solution)/shard_map/all_to_all | solution.py:126
  75.9 2.7 broadcast_select_fusion
  78.6 1.9 collective-permute-start
  81.9 1.6 slice_reduce_fusion.29
  83.5 3.0 collective-permute-done.1
  86.9 7.5 %multiply_reduce_fusion = (f32[1536]{0:T(1024)}, f32[1536]{0:T(1024)}, f32[1536]{0:T(1024)}, f32[1536]{0:T(1024)}, f32[1536]{0:T(1024)}, /*index=5*/f32[1536]{0:...) fusion(f32[158,1536]{1,0:T(8,128)S(1)} %maximum_convert_fusion,, ...), kind=kLoop, calls=%fused_computation.190 | loop fusion | flops 21206016 | bytes 26652800 | tf_op jit(solution)/shard_map/reduce_sum | solution.py:144
  95.7 5.0 %collective-permute-start.3 = (f32[15,1536]{1,0:T(8,128)S(1)}, f32[15,1536]{1,0:T(8,128)S(1)}, u32[]{:S(2)}, u32[]{:S(2)}) collective-permute-start(f32[15,1536]{1,0:T(8,128)S(1)} %get-tuple-element.306), channel_id=1, source_target_pairs={{0,4},{4,8},{8,12},{12,16},{16,20},{20,24},{24,28},{1,5},{5,9},{9,... | collective-permute-start | bytes 276488 | tf_op jit(solution)/shard_map/ppermute | solution.py:22
  101.2 1.5 collective-permute-done.3
  102.7 3.7 %fusion.37 = bf16[128,1536]{1,0:T(8,128)(2,1)S(1)} fusion(f32[128,1536]{1,0:T(8,128)S(1)} %get-tuple-element.299, f32[15,1536]{1,0:T(8,128)S(1)} %collective-permute-done.3, f32[15,1536]{1,0:T(8,128)S(1)} %collective-permute-done.2, bf16[1,128,1536]{2,1,0:T(8,128)(2,1)S(1)} %copy-done.11, f32[1536]{0:T(1024)S(1)} %get-tuple-element.265, ...), kind=kLoop, calls=%fused_computation.100 | loop fusion | flops 18874368 | bytes 1947776 | tf_op jit(solution)/shard_map/convert_element_type | solution.py:152
  107.2 2.9 fusion.130
  111.1 2.1 reshape.121
  113.2 1.5 convolution_convert_fusion
  115.5 6.7 %all-to-all-start.4 = ((bf16[8,128,96]{1,2,0:T(8,128)(2,1)}), bf16[8,128,96]{1,2,0:T(8,128)(2,1)S(1)}, u32[]{:S(2)}, u32[]{:S(2)}) async-start(bf16[8,128,96]{1,2,0:T(8,128)(2,1)} %bitcast.121), calls=%async_computation.4 | async-start | bytes 393216 | tf_op jit(solution)/shard_map/all_to_all | solution.py:158
  122.4 3.0 multiply_reduce_fusion.18
  128.9 3.5 %stack.127 = f32[31,1536]{1,0:T(8,128)} concatenate(f32[1,1536]{1,0:T(1,128)} %stack.96, f32[1,1536]{1,0:T(1,128)} %stack.97, f32[1,1536]{1,0:T(1,128)} %stack.98, f32[1,1536]{1,0:T(1,128)} %stack.99, f32[1,1536]{1,0:T(1,128)} %stack.100, f32[1,1536]{1,0:T(1,128)S(1)} %stack.101, f32[1,1536]{1,0:T(1,128)S(1)} %stack.102, f32[1,1536]{1,0:T(1,128)S(1)} %stack.103, ...), dimensions={0} | concatenate | bytes 380928 | tf_op jit(solution)/shard_map/stack | solution.py:143
  132.4 1.5 all-to-all-done.4
  136.5 12.9 %while.25 = (s32[]{:T(128)}, bf16[2,512,96]{1,2,0:T(8,128)(2,1)}, bf16[2,512,96]{2,1,0:T(8,128)(2,1)S(1)}, bf16[1024,96]{1,0:T(8,128)(2,1)S(1)}, f32[2,512]{1,0:...) while((s32[]{:T(128)}, bf16[2,512,96]{1,2,0:T(8,128)(2,1)}, ...), condition=%wide.region_6.7_spmd.clone, body=%wide.region_5.6_spmd.clone.sunk | while | flops 305185792 | bytes 6241429 | solution.py:74
  138.0 1.8 fusion.162
  139.8 3.3 %fusion.163 = bf16[2,512,96]{1,2,0:T(8,128)(2,1)} fusion(bf16[2,512,96]{1,2,0:T(8,128)(2,1)} %get-tuple-element.455, s32[]{:T(128)S(6)} %copy.133, bf16[1024,96]{1,0:T(8,128)(2,1)S(1)} %get-tuple-element.467, f32[512,1024]{1,0:T(8,128)} %fusion.162, bf16[1024,96]{1,0:T(8,128)(2,1)S(1)} %get-tuple-element.470, f32[512]{0:T(512)S(1)} %bitcast.129, ...), kind=kOutput, calls=%fused_computation.17.clone.1 | convolution fusion | flops 204521472 | bytes 2955264 | tf_op jit(solution)/shard_map/while/body/eval_jaxpr/dot_general | solution.py:72
  144.4 1.8 fusion.162
  146.2 3.2 fusion.163
  149.5 1.9 copy.104
  151.3 2.7 reshape.123
  154.0 3.7 %reduce.64 = bf16[1024,96]{1,0:T(8,128)(2,1)} reduce(bf16[1024,1,96]{2,1,0:T(2,128)(2,1)} %bitcast.116, bf16[]{:T(256)} %broadcast.73), dimensions={1}, to_apply=%bitcast.68.reduce_sub_computation | reduce | bytes 393218
  157.7 2.1 reshape.157
  159.8 4.5 %all-to-all-start.5 = ((bf16[8,2,6144]{2,1,0:T(2,128)(2,1)}), bf16[8,2,6144]{2,1,0:T(2,128)(2,1)}, u32[]{:S(2)}, u32[]{:S(2)}) async-start(bf16[8,2,6144]{2,1,0:T(2,128)(2,1)} %reshape.157), calls=%async_computation.5 | async-start | bytes 393216 | tf_op jit(solution)/shard_map/all_to_all | solution.py:166
  164.3 48.2 %reduce-scatter.2.cloned.1.call-done = f32[192,768]{1,0:T(8,128)} async-done(((f32[1536,768]{1,0:T(8,128)}), f32[192,768]{1,0:T(8,128)}) %reduce-scatter.2.cloned.1.call-update) | async-done | bytes 589840 | tf_op jit(solution)/shard_map/reduce_scatter | solution.py:171
  212.5 1.8 convert_element_type.98
  215.4 40.3 %psum.23 = f32[1536]{0:T(1024)S(1)} all-reduce(f32[1536]{0:T(1024)S(1)} %copy-done.48), channel_id=1, replica_groups=mesh['seq'=8,'dp'=4] {'seq','dp'}, use_global_device_ids=true, to_apply=%region_42.43 | all-reduce | flops 1536 | bytes 12288 | tf_op jit(solution)/shard_map/psum | solution.py:173
  256.4 20.2 %all-reduce.5.cloned.1.call-done = f32[31,1536]{1,0:T(8,128)} async-done(((f32[31,1536]{1,0:T(8,128)}), f32[31,1536]{1,0:T(8,128)}) %all-reduce.5.cloned.1.call-update) | async-done | bytes 190480 | tf_op jit(solution)/shard_map/psum | solution.py:173
  276.6 1.5 constant_dynamic-slice_fusion.2
  280.6 31.7 %all-reduce.3.cloned.1.call-done = bf16[192,768]{1,0:T(8,128)(2,1)} async-done(((bf16[192,768]{1,0:T(8,128)(2,1)}), bf16[192,768]{1,0:T(8,128)(2,1)}) %all-reduce.3.cloned.1.call-update) | async-done | bytes 294928 | tf_op jit(solution)/shard_map/psum | solution.py:172
  312.3 1.8 convert_element_type.99
  (194 shorter events, 28.3 us)
Async XLA Ops:
  8.0 67.7 %copy-start = (bf16[1536,768]{1,0:T(8,128)(2,1)S(1)}, bf16[1536,768]{1,0:T(8,128)(2,1)}, u32[]{:S(2)}) copy-start(bf16[1536,768]{1,0:T(8,128)(2,1)} %param.18) | copy-start | bytes 7077892
  9.9 15.2 %all-to-all-start = ((bf16[8,128,96]{1,2,0:T(8,128)(2,1)}), bf16[8,128,96]{1,2,0:T(8,128)(2,1)S(1)}, u32[]{:S(2)}, u32[]{:S(2)}) async-start(bf16[8,128,96]{1,2,0:T(8,128)(2,1)} %bitcast.3), calls=%async_computation | async-start | bytes 393216 | tf_op jit(solution)/shard_map/all_to_all | solution.py:108
  25.1 11.1 %all-to-all-start.1 = ((bf16[8,128,96]{1,2,0:T(8,128)(2,1)}), bf16[8,128,96]{1,2,0:T(8,128)(2,1)S(1)}, u32[]{:S(2)}, u32[]{:S(2)}) async-start(bf16[8,128,96]{1,2,0:T(8,128)(2,1)} %bitcast.5), calls=%async_computation.1 | async-start | bytes 393216 | tf_op jit(solution)/shard_map/all_to_all | solution.py:118
  36.3 11.1 %all-to-all-start.2 = ((bf16[8,128,96]{1,2,0:T(8,128)(2,1)}), bf16[8,128,96]{1,2,0:T(8,128)(2,1)S(1)}, u32[]{:S(2)}, u32[]{:S(2)}) async-start(bf16[8,128,96]{1,2,0:T(8,128)(2,1)} %bitcast.7), calls=%async_computation.2 | async-start | bytes 393216 | tf_op jit(solution)/shard_map/all_to_all | solution.py:119
  52.2 14.0 %copy-start.49 = (f32[2,512]{1,0:T(2,128)}, f32[2,512]{1,0:T(2,128)S(1)}, u32[]{:S(2)}) copy-start(f32[2,512]{1,0:T(2,128)S(1)} %get-tuple-element.448) | copy-start | bytes 12292
  52.3 23.3 %copy-start.1 = (bf16[1024,96]{1,0:T(8,128)(2,1)}, bf16[1024,96]{1,0:T(8,128)(2,1)S(1)}, u32[]{:S(2)}) copy-start(bf16[1024,96]{1,0:T(8,128)(2,1)S(1)} %get-tuple-element.477) | copy-start | bytes 589828
  52.3 23.3 %copy-start.3 = (bf16[1024,96]{1,0:T(8,128)(2,1)}, bf16[1024,96]{1,0:T(8,128)(2,1)S(1)}, u32[]{:S(2)}) copy-start(bf16[1024,96]{1,0:T(8,128)(2,1)S(1)} %get-tuple-element.480) | copy-start | bytes 589828
  52.3 23.3 %copy-start.5 = (bf16[2,512,96]{2,1,0:T(8,128)(2,1)}, bf16[2,512,96]{2,1,0:T(8,128)(2,1)S(1)}, u32[]{:S(2)}) copy-start(bf16[2,512,96]{2,1,0:T(8,128)(2,1)S(1)} %get-tuple-element.481) | copy-start | bytes 589828
  62.1 11.1 %all-to-all-start.3 = ((bf16[8,2,6144]{2,1,0:T(2,128)(2,1)}), bf16[8,2,6144]{2,1,0:T(2,128)(2,1)S(1)}, u32[]{:S(2)}, u32[]{:S(2)}) async-start(bf16[8,2,6144]{2,1,0:T(2,128)(2,1)} %reshape.155), calls=%async_computation.3 | async-start | bytes 393216 | tf_op jit(solution)/shard_map/all_to_all | solution.py:126
  65.5 147.0 %reduce-scatter.2.cloned.1.call-start = ((), (), s32[]{:S(2)}) async-start(), calls=%async_computation.7 | async-start | bytes 5308416 | tf_op jit(solution)/shard_map/reduce_scatter | solution.py:171
  75.7 11.0 %copy-start.11 = (bf16[1,128,1536]{2,1,0:T(8,128)(2,1)S(1)}, bf16[1,128,1536]{2,1,0:T(8,128)(2,1)}, u32[]{:S(2)}) copy-start(bf16[1,128,1536]{2,1,0:T(8,128)(2,1)} %param.21) | copy-start | bytes 1179652
  75.7 11.0 %copy-start.13 = (f32[1536]{0:T(1024)S(1)}, f32[1536]{0:T(1024)}, u32[]{:S(2)}) copy-start(f32[1536]{0:T(1024)} %get-tuple-element.238) | copy-start | bytes 18436
  75.7 11.0 %copy-start.14 = (f32[1536]{0:T(1024)S(1)}, f32[1536]{0:T(1024)}, u32[]{:S(2)}) copy-start(f32[1536]{0:T(1024)} %get-tuple-element.239) | copy-start | bytes 18436
  75.7 11.0 %copy-start.15 = (f32[1536]{0:T(1024)S(1)}, f32[1536]{0:T(1024)}, u32[]{:S(2)}) copy-start(f32[1536]{0:T(1024)} %get-tuple-element.240) | copy-start | bytes 18436
  75.7 11.0 %copy-start.16 = (f32[1536]{0:T(1024)S(1)}, f32[1536]{0:T(1024)}, u32[]{:S(2)}) copy-start(f32[1536]{0:T(1024)} %get-tuple-element.241) | copy-start | bytes 18436
  75.7 11.0 %copy-start.17 = (f32[1536]{0:T(1024)S(1)}, f32[1536]{0:T(1024)}, u32[]{:S(2)}) copy-start(f32[1536]{0:T(1024)} %get-tuple-element.242) | copy-start | bytes 18436
  75.7 11.0 %copy-start.18 = (f32[1536]{0:T(1024)S(1)}, f32[1536]{0:T(1024)}, u32[]{:S(2)}) copy-start(f32[1536]{0:T(1024)} %get-tuple-element.243) | copy-start | bytes 18436
  75.7 11.0 %copy-start.19 = (f32[1536]{0:T(1024)S(1)}, f32[1536]{0:T(1024)}, u32[]{:S(2)}) copy-start(f32[1536]{0:T(1024)} %get-tuple-element.244) | copy-start | bytes 18436
  75.7 11.0 %copy-start.20 = (f32[1536]{0:T(1024)S(1)}, f32[1536]{0:T(1024)}, u32[]{:S(2)}) copy-start(f32[1536]{0:T(1024)} %get-tuple-element.245) | copy-start | bytes 18436
  75.8 11.0 %copy-start.21 = (f32[1536]{0:T(1024)S(1)}, f32[1536]{0:T(1024)}, u32[]{:S(2)}) copy-start(f32[1536]{0:T(1024)} %get-tuple-element.246) | copy-start | bytes 18436
  75.8 11.0 %copy-start.22 = (f32[1536]{0:T(1024)S(1)}, f32[1536]{0:T(1024)}, u32[]{:S(2)}) copy-start(f32[1536]{0:T(1024)} %get-tuple-element.247) | copy-start | bytes 18436
  75.8 11.0 %copy-start.23 = (f32[1536]{0:T(1024)S(1)}, f32[1536]{0:T(1024)}, u32[]{:S(2)}) copy-start(f32[1536]{0:T(1024)} %get-tuple-element.248) | copy-start | bytes 18436
  75.8 11.0 %copy-start.24 = (f32[1536]{0:T(1024)S(1)}, f32[1536]{0:T(1024)}, u32[]{:S(2)}) copy-start(f32[1536]{0:T(1024)} %get-tuple-element.249) | copy-start | bytes 18436
  75.8 11.0 %copy-start.25 = (f32[1536]{0:T(1024)S(1)}, f32[1536]{0:T(1024)}, u32[]{:S(2)}) copy-start(f32[1536]{0:T(1024)} %get-tuple-element.250) | copy-start | bytes 18436
  75.8 11.0 %copy-start.26 = (f32[1536]{0:T(1024)S(1)}, f32[1536]{0:T(1024)}, u32[]{:S(2)}) copy-start(f32[1536]{0:T(1024)} %get-tuple-element.251) | copy-start | bytes 18436
  75.8 11.0 %copy-start.27 = (f32[1536]{0:T(1024)S(1)}, f32[1536]{0:T(1024)}, u32[]{:S(2)}) copy-start(f32[1536]{0:T(1024)} %get-tuple-element.252) | copy-start | bytes 18436
  75.8 11.0 %copy-start.28 = (f32[1536]{0:T(1024)S(1)}, f32[1536]{0:T(1024)}, u32[]{:S(2)}) copy-start(f32[1536]{0:T(1024)} %get-tuple-element.253) | copy-start | bytes 18436
  75.8 11.0 %copy-start.29 = (f32[1536]{0:T(1024)S(1)}, f32[1536]{0:T(1024)}, u32[]{:S(2)}) copy-start(f32[1536]{0:T(1024)} %get-tuple-element.254) | copy-start | bytes 18436
  75.8 11.0 %copy-start.50 = (pred[128]{0:T(512)(128)(4,1)S(1)}, pred[128]{0:T(512)(128)(4,1)}, u32[]{:S(2)}) copy-start(pred[128]{0:T(512)(128)(4,1)} %add_compare_fusion) | copy-start | bytes 388
  75.9 11.0 %copy-start.52 = (f32[1536]{0:T(1024)S(1)}, f32[1536]{0:T(1024)}, u32[]{:S(2)}) copy-start(f32[1536]{0:T(1024)} %param.20) | copy-start | bytes 18436
  78.6 4.9 %collective-permute-start = (bf16[15,1536]{1,0:T(8,128)(2,1)S(1)}, bf16[15,1536]{1,0:T(8,128)(2,1)S(1)}, u32[]{:S(2)}, u32[]{:S(2)}) collective-permute-start(bf16[15,1536]{1,0:T(8,128)(2,1)S(1)} %get-tuple-element.307), channel_id=1, source_target_pairs={{0,4},{4,8},{8,12},{12,16},{16,20},{20,24},{24,28},{1,5},{5,9},{9,... | collective-permute-start | bytes 138248 | tf_op jit(solution)/shard_map/ppermute | solution.py:22
  80.6 6.0 %collective-permute-start.1 = (bf16[15,1536]{1,0:T(8,128)(2,1)S(1)}, bf16[15,1536]{1,0:T(8,128)(2,1)S(1)}, u32[]{:S(2)}, u32[]{:S(2)}) collective-permute-start(bf16[15,1536]{1,0:T(8,128)(2,1)S(1)} %get-tuple-element.308), channel_id=1, source_target_pairs={{4,0},{8,4},{12,8},{16,12},{20,16},{24,20},{28,24},{5,1},{9,5},{13... | collective-permute-start | bytes 138248 | tf_op jit(solution)/shard_map/ppermute | solution.py:23
  94.4 8.3 %copy-start.7 = (f32[128,1536]{1,0:T(8,128)}, f32[128,1536]{1,0:T(8,128)S(1)}, u32[]{:S(2)}) copy-start(f32[128,1536]{1,0:T(8,128)S(1)} %get-tuple-element.299) | copy-start | bytes 2359300
  94.4 6.7 %collective-permute-start.2 = (f32[15,1536]{1,0:T(8,128)S(1)}, f32[15,1536]{1,0:T(8,128)S(1)}, u32[]{:S(2)}, u32[]{:S(2)}) collective-permute-start(f32[15,1536]{1,0:T(8,128)S(1)} %get-tuple-element.305), channel_id=1, source_target_pairs={{4,0},{8,4},{12,8},{16,12},{20,16},{24,20},{28,24},{5,1},{9,5},{13... | collective-permute-start | bytes 276488 | tf_op jit(solution)/shard_map/ppermute | solution.py:23
  95.7 7.0 %collective-permute-start.3 = (f32[15,1536]{1,0:T(8,128)S(1)}, f32[15,1536]{1,0:T(8,128)S(1)}, u32[]{:S(2)}, u32[]{:S(2)}) collective-permute-start(f32[15,1536]{1,0:T(8,128)S(1)} %get-tuple-element.306), channel_id=1, source_target_pairs={{0,4},{4,8},{8,12},{12,16},{16,20},{20,24},{24,28},{1,5},{5,9},{9,... | collective-permute-start | bytes 276488 | tf_op jit(solution)/shard_map/ppermute | solution.py:22
  115.5 18.4 %all-to-all-start.4 = ((bf16[8,128,96]{1,2,0:T(8,128)(2,1)}), bf16[8,128,96]{1,2,0:T(8,128)(2,1)S(1)}, u32[]{:S(2)}, u32[]{:S(2)}) async-start(bf16[8,128,96]{1,2,0:T(8,128)(2,1)} %bitcast.121), calls=%async_computation.4 | async-start | bytes 393216 | tf_op jit(solution)/shard_map/all_to_all | solution.py:158
  122.1 3.6 %copy-start.31 = (f32[1536]{0:T(1024)S(1)}, f32[1536]{0:T(1024)}, u32[]{:S(2)}) copy-start(f32[1536]{0:T(1024)} %get-tuple-element.220) | copy-start | bytes 18436
  122.1 3.7 %copy-start.30 = (f32[1536]{0:T(1024)S(1)}, f32[1536]{0:T(1024)}, u32[]{:S(2)}) copy-start(f32[1536]{0:T(1024)} %get-tuple-element.221) | copy-start | bytes 18436
  122.2 154.4 %all-reduce.5.cloned.1.call-start = ((), (), s32[]{:S(2)}) async-start(), calls=%async_computation.9 | async-start | bytes 393216 | tf_op jit(solution)/shard_map/psum | solution.py:173
  125.4 11.2 %copy-start.2 = (bf16[1024,96]{1,0:T(8,128)(2,1)S(1)}, bf16[1024,96]{1,0:T(8,128)(2,1)}, u32[]{:S(2)}) copy-start(bf16[1024,96]{1,0:T(8,128)(2,1)} %copy-done.1) | copy-start | bytes 589828
  125.4 11.2 %copy-start.4 = (bf16[1024,96]{1,0:T(8,128)(2,1)S(1)}, bf16[1024,96]{1,0:T(8,128)(2,1)}, u32[]{:S(2)}) copy-start(bf16[1024,96]{1,0:T(8,128)(2,1)} %copy-done.3) | copy-start | bytes 589828
  125.4 11.2 %copy-start.6 = (bf16[2,512,96]{2,1,0:T(8,128)(2,1)S(1)}, bf16[2,512,96]{2,1,0:T(8,128)(2,1)}, u32[]{:S(2)}) copy-start(bf16[2,512,96]{2,1,0:T(8,128)(2,1)} %copy-done.5) | copy-start | bytes 589828
  149.4 64.9 %copy-start.9 = (f32[128,1536]{1,0:T(8,128)S(1)}, f32[128,1536]{1,0:T(8,128)}, u32[]{:S(2)}) copy-start(f32[128,1536]{1,0:T(8,128)} %get-tuple-element.300) | copy-start | bytes 2359300
  149.5 64.9 %copy-start.10 = (bf16[128,1536]{1,0:T(8,128)(2,1)S(1)}, bf16[128,1536]{1,0:T(8,128)(2,1)}, u32[]{:S(2)}) copy-start(bf16[128,1536]{1,0:T(8,128)(2,1)} %get-tuple-element.310) | copy-start | bytes 1179652
  149.5 64.9 %copy-start.51 = (pred[128]{0:T(512)(128)(4,1)S(1)}, pred[128]{0:T(512)(128)(4,1)}, u32[]{:S(2)}) copy-start(pred[128]{0:T(512)(128)(4,1)} %add_compare_fusion) | copy-start | bytes 388
  154.0 61.4 %copy-start.48 = (f32[1536]{0:T(1024)S(1)}, f32[1536]{0:T(1024)}, u32[]{:S(2)}) copy-start(f32[1536]{0:T(1024)} %get-tuple-element.235) | copy-start | bytes 18436
  159.8 118.3 %all-to-all-start.5 = ((bf16[8,2,6144]{2,1,0:T(2,128)(2,1)}), bf16[8,2,6144]{2,1,0:T(2,128)(2,1)}, u32[]{:S(2)}, u32[]{:S(2)}) async-start(bf16[8,2,6144]{2,1,0:T(2,128)(2,1)} %reshape.157), calls=%async_computation.5 | async-start | bytes 393216 | tf_op jit(solution)/shard_map/all_to_all | solution.py:166
  164.2 148.0 %all-reduce.3.cloned.1.call-start = ((), (), s32[]{:S(2)}) async-start(), calls=%async_computation.8 | async-start | bytes 589824 | tf_op jit(solution)/shard_map/psum | solution.py:172
  (19 other events, 60.0 us)
Sparse Core Ops, SparseCore 0:
  110.3 102.1 reduce-scatter.1
Sparse Core Ops, SparseCore 1:
  132.5 144.0 all-reduce.4
  279.3 32.9 all-reduce.2
where the time goes:
time: 324 us; the launch traced here: 322 us
  waiting for transfers between devices  130 us (40%)
  local copies, waits for them, and re-layouts  44.2 us (14%)
  blocking collectives  40.3 us (12%)
  starting transfers between devices  38.2 us (12%)
  other arithmetic  31.9 us (10%)
  matrix products  19.4 us (6%)
  between operations  17.3 us (5%)
    reduce_scatter x1, waiting for transfers between devices, on_device(): lax.psum_scatter(term_block, 'seq', scatter_dimension=0, tiled=True)  48.2 us
    psum x1, blocking collectives, on_device(): lax.psum((kernel_local, bias_local), ('seq', 'dp'))  40.3 us
    psum x1, waiting for transfers between devices, on_device(): lax.psum(partial_rows.astype(jnp.bfloat16), 'dp').astype(jnp.float32)  31.7 us
    psum x1, waiting for transfers between devices, on_device(): lax.psum((kernel_local, bias_local), ('seq', 'dp'))  20.2 us
    unnamed x119, local copies, waits for them, and re-layouts  15.6 us
    reduce_sum x2, other arithmetic, on_device(): jnp.sum(grad_conv * padded[tap:tap + frames_dev], axis=0)  10.5 us
    unnamed x2, other arithmetic  7.45 us
    all_to_all x1, waiting for transfers between devices, on_device(): lax.all_to_all(value_send, 'seq', split_axis=0, concat_axis=1, tiled=True)  7.34 us
  transfers between devices with their start and end apart: 13, of which 11 were waited for; matrix products, arithmetic and copies ran while one was open for 18% of the time, Pallas kernels for 0%

commit v1 on v0

--- a/solution.py
+++ b/solution.py
@@ -1,8 +1,11 @@
+import functools
 import math
 
 import jax
 import jax.numpy as jnp
 from jax import lax
+from jax.experimental import pallas as pl
+from jax.experimental.pallas import tpu as pltpu
 from jax.sharding import PartitionSpec as P
 
 D = 1536
@@ -83,7 +86,7 @@
     return results.reshape(row_total, width)
 
 
-def on_device(
+def general_device(
     block_input, query_proj, key_proj, value_proj, lengths, out_proj, kernel, conv_bias, grad_output
 ):
     frames_dev = block_input.shape[1]
@@ -178,7 +181,530 @@
     return (block_output[None], grad_input[None], grad_query[None], summed, grad_kernel, grad_bias)
 
 
+BF16 = jnp.bfloat16
+F32 = jnp.float32
+TAP_ROWS = 32
+WIDE = 32
+SIDE = 16
+CHUNK = 384
+LANES = 128
+MASKED_SCORE = -1e30
+VMEM_LIMIT = 56 * 1024 * 1024
+SCORE_SCALE = 1.0 / math.sqrt(HS)
+LOG2_SCALE = SCORE_SCALE * math.log2(math.e)
+
+
+def fits_fast(sizes):
+    seq_count, dp_count = sizes["seq"], sizes["dp"]
+    piece = D // (seq_count * dp_count)
+    return seq_count == H and dp_count * seq_count * piece == D and piece == 48
+
+
+def params():
+    return pltpu.CompilerParams(vmem_limit_bytes=VMEM_LIMIT)
+
+
+def whole(shape):
+    return pl.BlockSpec(shape, lambda *_: (0,) * len(shape))
+
+
+def pack_kernel(q_ref, k_ref, v_ref, out_ref):
+    for place, ref in enumerate((q_ref, k_ref, v_ref)):
+        frames = ref.shape[0]
+        out_ref[:, place * HS : (place + 1) * HS, :] = ref[...].T.reshape(H, HS, frames)
+
+
+def pack_heads(q, k, v):
+    frames = q.shape[0]
+    return pl.pallas_call(
+        pack_kernel,
+        out_shape=jax.ShapeDtypeStruct((H, 3 * HS, frames), BF16),
+        compiler_params=params(),
+        name="pack_heads",
+    )(q, k, v)
+
+
+def key_rows(k_ref, length, keys_sc):
+    blocks, _, frames = k_ref.shape
+    for block in range(blocks):
+        row = lax.broadcasted_iota(jnp.int32, (LANES - HS, frames), 0)
+        key = lax.broadcasted_iota(jnp.int32, (LANES - HS, frames), 1) + block * frames
+        extra = jnp.where((row == 0) & (key >= length), MASKED_SCORE, 0.0)
+        tall = jnp.concatenate([k_ref[block].astype(F32), extra], axis=0)
+        keys_sc[block * frames : (block + 1) * frames, :] = tall.T.astype(BF16)
+
+
+def query_columns(q_ref):
+    query = jnp.concatenate([q_ref[0], q_ref[1]], axis=1)
+    row = lax.broadcasted_iota(jnp.int32, (LANES - HS, query.shape[1]), 0)
+    return jnp.concatenate([query, jnp.where(row == 0, 1.0, 0.0).astype(BF16)], axis=0)
+
+
+def side_by_side(ref, wide_sc):
+    blocks, _, frames = ref.shape
+    for block in range(blocks):
+        wide_sc[:, block * frames : (block + 1) * frames] = ref[block]
+
+
+def forward_kernel(length_ref, q_ref, k_ref, v_ref, out_ref, lse_ref, keys_sc, values_sc):
+    step = pl.program_id(0)
+    blocks, _, frames = k_ref.shape
+
+    @pl.when(step == 0)
+    def _():
+        key_rows(k_ref, length_ref[0], keys_sc)
+        side_by_side(v_ref, values_sc)
+
+    scores = jnp.dot(keys_sc[...], query_columns(q_ref), preferred_element_type=F32) * LOG2_SCALE
+    top = jnp.max(scores, axis=0, keepdims=True)
+    raised = jnp.exp2(scores - top)
+    total = jnp.sum(raised, axis=0, keepdims=True)
+    weights = (raised * (1.0 / total)).astype(BF16)
+    lse_ref[...] = top + jnp.log2(total)
+    mixed = jnp.dot(values_sc[...], weights, preferred_element_type=F32).astype(BF16)
+    out_ref[2 * step, :HS, :] = mixed[:, :frames]
+    out_ref[2 * step + 1, :HS, :] = mixed[:, frames:]
+
+    @pl.when(step == pl.num_programs(0) - 1)
+    def _():
+        lane = lax.broadcasted_iota(jnp.int32, (HS, frames), 1)
+        nothing = jnp.zeros((HS, frames), F32)
+        for block in range(blocks):
+            left = nothing
+            right = nothing
+            if block > 0:
+                left = pltpu.roll(out_ref[block - 1, :HS, :].astype(F32), WIDE, 1)
+            if block < blocks - 1:
+                right = pltpu.roll(out_ref[block + 1, :HS, :].astype(F32), WIDE, 1)
+            both = jnp.where(lane < WIDE, left, right)
+            lower = pltpu.roll(both[HS // 2 :], 2 * WIDE, 1)
+            packed = jnp.where(lane[: HS // 2] < 2 * WIDE, both[: HS // 2], lower)
+            out_ref[block, HS:, :] = packed.astype(BF16)
+
+
+def forward_heads(length, received):
+    blocks, _, frames = received.shape
+    total = blocks * frames
+    block = (blocks, HS, frames)
+    return pl.pallas_call(
+        forward_kernel,
+        grid=(blocks // 2,),
+        in_specs=[
+            pl.BlockSpec(memory_space=pltpu.SMEM),
+            pl.BlockSpec((2, HS, frames), lambda i: (i, 0, 0)),
+            pl.BlockSpec(block, lambda i: (0, 1, 0)),
+            pl.BlockSpec(block, lambda i: (0, 2, 0)),
+        ],
+        out_specs=[
+            whole((blocks, HS + HS // 2, frames)),
+            pl.BlockSpec((1, 2 * frames), lambda i: (0, i)),
+        ],
+        out_shape=[
+            jax.ShapeDtypeStruct((blocks, HS + HS // 2, frames), BF16),
+            jax.ShapeDtypeStruct((1, total), F32),
+        ],
+        scratch_shapes=[pltpu.VMEM((total, LANES), BF16), pltpu.VMEM((HS, total), BF16)],
+        compiler_params=params(),
+        name="forward_heads",
+    )(length, received, received, received)
+
+
+def backward_kernel(
+    length_ref, q_ref, k_ref, v_ref, grad_ref, head_ref, lse_ref, out_ref, keys_sc, values_sc, wide_sc
+):
+    step = pl.program_id(0)
+    blocks, _, frames = k_ref.shape
+
+    @pl.when(step == 0)
+    def _():
+        key_rows(k_ref, length_ref[0], keys_sc)
+        side_by_side(k_ref, wide_sc)
+        for block in range(blocks):
+            rows = v_ref[block].astype(F32).T.astype(BF16)
+            values_sc[block * frames : (block + 1) * frames, :] = rows
+
+    scores = jnp.dot(keys_sc[...], query_columns(q_ref), preferred_element_type=F32) * LOG2_SCALE
+    probs = jnp.exp2(scores - lse_ref[...])
+    grad = jnp.concatenate([grad_ref[0], grad_ref[1]], axis=1)
+    head = jnp.concatenate([head_ref[0], head_ref[1]], axis=1)
+    delta = jnp.sum(grad.astype(F32) * head.astype(F32), axis=0, keepdims=True)
+    grad_prob = jnp.dot(values_sc[...], grad, preferred_element_type=F32)
+    grad_score = (probs * (grad_prob - delta)).astype(BF16)
+    result = jnp.dot(wide_sc[...], grad_score, preferred_element_type=F32) * SCORE_SCALE
+    out_ref[0] = result[:, :frames].astype(BF16)
+    out_ref[1] = result[:, frames:].astype(BF16)
+
+
+def backward_heads(length, received, grads, heads, lse):
+    blocks, _, frames = received.shape
+    total = blocks * frames
+    block = (blocks, HS, frames)
+    pair = pl.BlockSpec((2, HS, frames), lambda i: (i, 0, 0))
+    return pl.pallas_call(
+        backward_kernel,
+        grid=(blocks // 2,),
+        in_specs=[
+            pl.BlockSpec(memory_space=pltpu.SMEM),
+            pair,
+            pl.BlockSpec(block, lambda i: (0, 1, 0)),
+            pl.BlockSpec(block, lambda i: (0, 2, 0)),
+            pair,
+            pair,
+            pl.BlockSpec((1, 2 * frames), lambda i: (0, i)),
+        ],
+        out_specs=pair,
+        out_shape=jax.ShapeDtypeStruct((blocks, HS, frames), BF16),
+        scratch_shapes=[
+            pltpu.VMEM((total, LANES), BF16),
+            pltpu.VMEM((total, HS), BF16),
+            pltpu.VMEM((HS, total), BF16),
+        ],
+        compiler_params=params(),
+        name="backward_heads",
+    )(length, received, received, received, grads, heads, lse)
+
+
+def shifted_sum(ref, tile, rows, weight_of, start):
+    total = start
+    for low in range(8):
+        base = ref[tile, low : low + rows + 24, :]
+        for high in range(4):
+            offset = 8 * high + low
+            if 1 <= offset < TAP_ROWS:
+                total = total + weight_of(offset) * base[8 * high : 8 * high + rows]
+    return total
+
+
+def middle_kernel(
+    info_ref,
+    main_ref,
+    edge_ref,
+    input_ref,
+    cot_ref,
+    before_ref,
+    after_ref,
+    proj_ref,
+    tap_ref,
+    bias_ref,
+    block_out_ref,
+    grad_in_ref,
+    grad_heads_ref,
+    *rest,
+):
+    piece_refs = rest[:-6]
+    att_sc, grad_sc, masked_sc, gate_sc, taps_sc, piece_sc = rest[-6:]
+    dp_count = len(piece_refs)
+    step = pl.program_id(0)
+    frames = input_ref.shape[0]
+    tiles = CHUNK // LANES
+    rows = frames + 2 * WIDE
+    span = frames + 2 * SIDE
+    first, length, mine = info_ref[0], info_ref[1], info_ref[2]
+
+    @pl.when(step == 0)
+    def _():
+        main = main_ref[...].reshape(HD, frames)
+        att_sc[WIDE : WIDE + frames, :] = main.T
+        edge = edge_ref[...].astype(F32).reshape(H * (HS // 2), frames)
+        lower = pltpu.roll(edge, frames - 2 * WIDE, 1)
+        half = (H, HS // 2, frames)
+        tall = jnp.concatenate([edge.reshape(half), lower.reshape(half)], axis=1)
+        turned = tall.reshape(HD, frames).T.astype(BF16)
+        att_sc[:WIDE, :] = turned[:WIDE]
+        att_sc[WIDE + frames :, :] = turned[WIDE : 2 * WIDE]
+        grad_sc[...] = jnp.zeros_like(grad_sc)
+
+    projected = lax.dot_general(
+        att_sc[...], proj_ref[...], (((1,), (1,)), ((), ())), preferred_element_type=F32
+    )
+    wide_input = jnp.concatenate(
+        [before_ref[:WIDE, :], input_ref[...], after_ref[:WIDE, :]], axis=0
+    ).astype(F32)
+    mixed = (wide_input + projected).astype(BF16).astype(F32)
+    frame = first - WIDE + lax.broadcasted_iota(jnp.int32, (rows, CHUNK), 0)
+    valid = (frame >= 0) & (frame < length)
+    masked = jnp.where(valid, mixed, 0.0)
+    cot = jnp.concatenate(
+        [before_ref[WIDE:, :], cot_ref[...], after_ref[WIDE:, :]], axis=0
+    ).astype(F32)
+    inner = slice(WIDE - SIDE, WIDE + SIDE + frames)
+    cot = jnp.where(valid[inner], cot, 0.0)
+    for tile in range(tiles):
+        masked_sc[tile] = masked[:, tile * LANES : (tile + 1) * LANES]
+
+    own = slice(SIDE, SIDE + frames)
+    here = valid[WIDE : WIDE + frames, :LANES]
+    for tile in range(tiles):
+        lanes = slice(tile * LANES, (tile + 1) * LANES)
+        start = jnp.broadcast_to(bias_ref[:, lanes], (span, LANES))
+        conv = shifted_sum(
+            masked_sc, tile, span, lambda offset: tap_ref[offset - 1 : offset, lanes], start
+        )
+        gate = lax.logistic(conv)
+        center = masked_sc[tile, WIDE : WIDE + frames, :]
+        block_out_ref[:, lanes] = jnp.where(here, center + conv[own] * gate[own], 0.0).astype(BF16)
+        gated = cot[:, lanes] * gate * (1.0 + conv * (1.0 - gate))
+        gate_sc[tile] = gated
+        owned = gated[own]
+        for low in range(8):
+            base = masked_sc[tile, SIDE + low : SIDE + low + frames + 24, :]
+            for high in range(4):
+                offset = 8 * high + low
+                if 1 <= offset < TAP_ROWS:
+                    product = owned * base[8 * high : 8 * high + frames]
+                    taps_sc[offset - 1, :, lanes] = product.reshape(frames // 8, 8, LANES).sum(0)
+        taps_sc[TAP_ROWS - 1, :, lanes] = owned.reshape(frames // 8, 8, LANES).sum(0)
+        back = shifted_sum(
+            gate_sc,
+            tile,
+            frames,
+            lambda offset: tap_ref[KW - offset : KW - offset + 1, lanes],
+            jnp.zeros((frames, LANES), F32),
+        )
+        grad_in_ref[:, lanes] = (cot[own, lanes] + jnp.where(here, back, 0.0)).astype(BF16)
+
+    grad_in = grad_in_ref[...]
+    grad_sc[...] += jnp.dot(grad_in, proj_ref[...], preferred_element_type=F32)
+
+    piece = 48
+    half = piece // 2
+    slabs = CHUNK // (dp_count * piece)
+    turned = grad_in.T.reshape(slabs * dp_count, piece, frames)
+    taps = jnp.sum(taps_sc[...], axis=1)
+    high_part = taps.astype(BF16).astype(F32)
+    low_part = taps - high_part
+    four = jnp.concatenate([high_part, low_part, high_part, low_part], axis=0)
+    tall = four.T.reshape(slabs * dp_count, piece, LANES)
+    lane = lax.broadcasted_iota(jnp.int32, (half, LANES), 1)
+    slab_count = D // (dp_count * piece)
+    for owner in range(dp_count):
+        packed = []
+        for slab in range(slabs):
+            source = slab * dp_count + owner
+            where = pl.multiple_of((step * slabs + slab) * piece, piece)
+            piece_sc[owner, pl.ds(where, piece), :] = turned[source]
+            packed.append(
+                jnp.where(lane < LANES // 2, tall[source, :half], tall[source, half:])
+            )
+        where = pl.multiple_of(slab_count * piece + step * slabs * half, slabs * half)
+        piece_sc[owner, pl.ds(where, slabs * half), :] = jnp.concatenate(packed, axis=0).astype(BF16)
+
+    @pl.when(step == pl.num_programs(0) - 1)
+    def _():
+        grad_heads_ref[...] = grad_sc[...].T.astype(BF16).reshape(H, HS, frames)
+        for away, ref in enumerate(piece_refs):
+            ref[...] = piece_sc[lax.rem(mine + away, dp_count)]
+
+
+def middle(info, returned, block_input, grad_output, before, after, out_proj, kernel, bias, dp_count):
+    frames = block_input.shape[0]
+    halo = WIDE + SIDE
+    piece_rows = D // dp_count + D // dp_count // 2
+    column = lambda count: pl.BlockSpec((count, CHUNK), lambda i: (0, i))
+    return pl.pallas_call(
+        middle_kernel,
+        grid=(D // CHUNK,),
+        in_specs=[
+            pl.BlockSpec(memory_space=pltpu.SMEM),
+            pl.BlockSpec((H, HS, frames), lambda i: (0, 0, 0)),
+            pl.BlockSpec((H, HS // 2, frames), lambda i: (0, 2, 0)),
+            column(frames),
+            column(frames),
+            column(halo),
+            column(halo),
+            pl.BlockSpec((CHUNK, HD), lambda i: (i, 0)),
+            column(KW),
+            column(1),
+        ],
+        out_specs=[
+            column(frames),
+            column(frames),
+            whole((H, HS, frames)),
+        ]
+        + [whole((piece_rows, frames))] * dp_count,
+        out_shape=[
+            jax.ShapeDtypeStruct((frames, D), BF16),
+            jax.ShapeDtypeStruct((frames, D), BF16),
+            jax.ShapeDtypeStruct((H, HS, frames), BF16),
+        ]
+        + [jax.ShapeDtypeStruct((piece_rows, frames), BF16)] * dp_count,
+        scratch_shapes=[
+            pltpu.VMEM((frames + 2 * WIDE, HD), BF16),
+            pltpu.VMEM((frames, HD), F32),
+            pltpu.VMEM((CHUNK // LANES, frames + 2 * WIDE, LANES), F32),
+            pltpu.VMEM((CHUNK // LANES, frames + 2 * SIDE, LANES), F32),
+            pltpu.VMEM((TAP_ROWS, 8, CHUNK), F32),
+            pltpu.VMEM((dp_count, piece_rows, frames), BF16),
+        ],
+        compiler_params=params(),
+        name="middle",
+    )(info, returned, returned, block_input, grad_output, before, after, out_proj, kernel, bias)
+
+
+def split_parts(lane, value):
+    high_part = value.astype(BF16).astype(F32)
+    low_part = pltpu.roll(value - high_part, TAP_ROWS, 1)
+    return jnp.where(lane % (2 * TAP_ROWS) < TAP_ROWS, high_part, low_part)
+
+
+def join_parts(value):
+    return value + pltpu.roll(value, LANES - TAP_ROWS, 1)
+
+
+def product_kernel(*refs):
+    out_ref = refs[-1]
+    count = (len(refs) - 1) // 2
+    pieces, heads = refs[:count], refs[count : 2 * count]
+    slabs, piece, _ = out_ref.shape
+    frames = pieces[0].shape[1]
+    height = slabs * piece
+    total = jnp.zeros((height, HD), F32)
+    taps = jnp.zeros((height // 2, frames), F32)
+    for piece_ref, head_ref in zip(pieces, heads):
+        total += lax.dot_general(
+            piece_ref[:height, :],
+            head_ref[...].reshape(HD, frames),
+            (((1,), (1,)), ((), ())),
+            preferred_element_type=F32,
+        )
+        taps += piece_ref[height:, :].astype(F32)
+    out_ref[:, :, :HD] = total.astype(BF16).reshape(slabs, piece, HD)
+    lane = lax.broadcasted_iota(jnp.int32, taps.shape, 1)
+    parts = split_parts(lane, join_parts(taps)).reshape(slabs, piece // 2, LANES)
+    padded = jnp.concatenate([parts, jnp.zeros_like(parts)], axis=1)
+    out_ref[:, :, HD:] = padded.astype(BF16)
+
+
+def product(pieces, heads, returned, seq_count):
+    frames = returned.shape[2]
+    piece_rows = pieces[0].shape[0]
+    height = piece_rows * 2 // 3
+    head_spec = whole((H, HS, frames))
+    return pl.pallas_call(
+        product_kernel,
+        grid=(1,),
+        in_specs=[whole((piece_rows, frames))] * len(pieces) + [head_spec] * len(pieces),
+        out_specs=whole((seq_count, height // seq_count, HD + LANES)),
+        out_shape=jax.ShapeDtypeStruct((seq_count, height // seq_count, HD + LANES), BF16),
+        compiler_params=params(),
+        name="product",
+    )(*pieces, returned, *heads)
+
+
+def sum_kernel(in_ref, out_ref):
+    total = jnp.sum(in_ref[...].astype(F32), axis=0)
+    out_ref[:, :HD] = total[:, :HD].astype(BF16)
+    taps = total[:, HD:]
+    lane = lax.broadcasted_iota(jnp.int32, taps.shape, 1)
+    out_ref[:, HD:] = split_parts(lane, join_parts(taps)).astype(BF16)
+
+
+def sum_shares(shares):
+    _, piece, width = shares.shape
+    return pl.pallas_call(
+        sum_kernel,
+        out_shape=jax.ShapeDtypeStruct((piece, width), BF16),
+        compiler_params=params(),
+        name="sum_shares",
+    )(shares)
+
+
+def finish_kernel(in_ref, proj_ref, tap_ref, bias_ref):
+    owners, piece, _ = in_ref.shape
+    half = piece // 2
+    columns = []
+    for owner in range(owners):
+        proj_ref[owner * piece : (owner + 1) * piece, :] = in_ref[owner, :, :HD].astype(F32)
+        taps = join_parts(in_ref[owner, :half, HD:].astype(F32))
+        columns += [taps, pltpu.roll(taps, LANES // 2, 1)]
+    turned = jnp.concatenate(columns, axis=0).T
+    tap_ref[...] = turned[:KW]
+    bias_ref[...] = turned[KW : KW + 1]
+
+
+def finish(gathered):
+    owners, piece, _ = gathered.shape
+    width = owners * piece
+    return pl.pallas_call(
+        finish_kernel,
+        out_shape=[
+            jax.ShapeDtypeStruct((width, HD), F32),
+            jax.ShapeDtypeStruct((KW, width), F32),
+            jax.ShapeDtypeStruct((1, width), F32),
+        ],
+        compiler_params=params(),
+        name="finish",
+    )(gathered)
+
+
+def unpack_kernel(in_ref, out_ref):
+    out_ref[...] = in_ref[...].reshape(HD, in_ref.shape[2]).T
+
+
+def unpack_heads(heads):
+    frames = heads.shape[2]
+    return pl.pallas_call(
+        unpack_kernel,
+        out_shape=jax.ShapeDtypeStruct((frames, HD), BF16),
+        compiler_params=params(),
+        name="unpack_heads",
+    )(heads)
+
+
+def exchange(blocks, axis):
+    return lax.all_to_all(blocks, axis, split_axis=0, concat_axis=0, tiled=True)
+
+
+def fast_device(
+    block_input, query_proj, key_proj, value_proj, lengths, out_proj, kernel, conv_bias, grad_output
+):
+    frames = block_input.shape[1]
+    seq_count = lax.axis_size("seq")
+    dp_count = lax.axis_size("dp")
+    first_frame = lax.axis_index("seq") * frames
+    info = jnp.stack([first_frame, lengths[0], lax.axis_index("dp")]).astype(jnp.int32)
+
+    received = exchange(pack_heads(query_proj[0], key_proj[0], value_proj[0]), "seq")
+
+    last = jnp.concatenate([block_input[0, frames - WIDE :], grad_output[0, frames - SIDE :]])
+    leading = jnp.concatenate([block_input[0, :WIDE], grad_output[0, :SIDE]])
+    up = [(i, i + 1) for i in range(seq_count - 1)]
+    down = [(j, i) for i, j in up]
+    before = lax.ppermute(last, "seq", up)
+    after = lax.ppermute(leading, "seq", down)
+
+    sent, lse = forward_heads(lengths, received)
+    returned = exchange(sent, "seq")
+    mine = returned[:, :HS]
+    shifts = [[(i, (i + away) % dp_count) for i in range(dp_count)] for away in range(1, dp_count)]
+    heads = [lax.ppermute(mine, "dp", shift) for shift in shifts]
+
+    block_output, grad_input, grad_heads, *pieces = middle(
+        info,
+        returned,
+        block_input[0],
+        grad_output[0],
+        before,
+        after,
+        out_proj,
+        kernel,
+        conv_bias[None],
+        dp_count,
+    )
+    grads = exchange(grad_heads, "seq")
+    moved = [pieces[0]] + [
+        lax.ppermute(piece, "dp", shift) for piece, shift in zip(pieces[1:], shifts)
+    ]
+    grad_query = unpack_heads(exchange(backward_heads(lengths, received, grads, sent, lse), "seq"))
+
+    shares = exchange(product(moved, heads, returned, seq_count), "seq")
+    gathered = lax.all_gather(sum_shares(shares), "dp")
+    grad_proj, grad_kernel, grad_bias = finish(gathered)
+    return (block_output[None], grad_input[None], grad_query[None], grad_proj, grad_kernel, grad_bias[0])
+
+
 def solution(mesh):
+    device_fn = fast_device if fits_fast(mesh.shape) else general_device
     placed = (
         P("dp", "seq", None),
         P("dp", "seq", None),
@@ -191,7 +717,7 @@
         P("dp", "seq", None),
     )
     return jax.shard_map(
-        on_device,
+        device_fn,
         mesh=mesh,
         in_specs=placed,
         out_specs=(

time: 324 us -> 143 us (0.44)
  waiting for transfers between devices: 130 us -> 49.5 us
  local copies, waits for them, and re-layouts: 44.2 us -> 4.76 us
  Pallas kernels: 0 us -> 33.8 us
  other arithmetic: 31.9 us -> 0.69 us
  matrix products: 19.4 us -> 0 us
  blocking collectives: 40.3 us -> 22.1 us
  between operations: 17.3 us -> 1.49 us
  starting transfers between devices: 38.2 us -> 29.3 us
    psum x2 -> x0, waiting for transfers between devices: 51.9 us -> none  [the longest x1 31.7 us: on_device(): lax.psum(partial_rows.astype(jnp.bfloat16), 'dp').astype(jnp.float32)]
    reduce_scatter x1 -> x0, waiting for transfers between devices: 48.2 us -> none  [on_device(): lax.psum_scatter(term_block, 'seq', scatter_dimension=0, tiled=True)]
    psum x1 -> x0, blocking collectives: 40.3 us -> none  [on_device(): lax.psum((kernel_local, bias_local), ('seq', 'dp'))]
    pallas_call x0 -> x8, Pallas kernels: none -> 33.8 us  [the longest x1 12.1 us: middle(): pl.pallas_call(middle_kernel, grid=(D // CHUNK,), in_specs=[pl.BlockSpec(...]
    dot_general x11 -> x0, matrix products: 19.4 us -> none  [the longest x2 6.48 us: backward_one_block(): jnp.dot(grad_score, key_one, preferred_element_type=jnp.float32)]
    all_to_all x0 -> x1, blocking collectives: none -> 14.5 us  [exchange(): return lax.all_to_all(blocks, axis, split_axis=0, concat_axis=0, tiled=True)]
    ppermute x4 -> x8, waiting for transfers between devices: 5.05 us -> 17.8 us  [the longest x3 13 us: fast_device(): lax.ppermute(piece, 'dp', shift)]
    reduce_sum x5 -> x0, other arithmetic: 12.6 us -> none  [the longest x2 10.5 us: on_device(): jnp.sum(grad_conv * padded[tap:tap + frames_dev], axis=0)]
  transfers between devices with their start and end apart: 13 -> 12, of which waited for: 11 -> 7; matrix products, arithmetic and copies ran while one was open for 18% -> 2% of each run, Pallas kernels for 0% -> 3%
where the time goes in v1:
time: 143 us; the launch traced here: 142 us
  waiting for transfers between devices  49.5 us (35%)
  Pallas kernels  33.8 us (24%)
  starting transfers between devices  29.3 us (20%)
  blocking collectives  22.1 us (15%)
  local copies, waits for them, and re-layouts  4.76 us (3%)
  between operations  1.49 us (1%)
    all_to_all x4, waiting for transfers between devices, exchange(): return lax.all_to_all(blocks, axis, split_axis=0, concat_axis=0, tiled=True)  31.7 us
    all_to_all x4, starting transfers between devices, exchange(): return lax.all_to_all(blocks, axis, split_axis=0, concat_axis=0, tiled=True)  20.3 us
    all_to_all x1, blocking collectives, exchange(): return lax.all_to_all(blocks, axis, split_axis=0, concat_axis=0, tiled=True)  14.5 us
    ppermute x3, waiting for transfers between devices, fast_device(): lax.ppermute(piece, 'dp', shift)  13 us
    pallas_call x1, Pallas kernels, middle(): pl.pallas_call(middle_kernel, grid=(D // CHUNK,), in_specs=[pl.BlockSpec(...  12.1 us
    all_gather x1, blocking collectives, fast_device(): gathered = lax.all_gather(sum_shares(shares), 'dp')  7.59 us
    pallas_call x1, Pallas kernels, forward_heads(): pl.pallas_call(forward_kernel, grid=(blocks // 2,), in_specs=[pl.BlockSpe...  5.78 us
    pallas_call x1, Pallas kernels, backward_heads(): pl.pallas_call(backward_kernel, grid=(blocks // 2,), in_specs=[pl.BlockSp...  5.1 us
  transfers between devices with their start and end apart: 12, of which 7 were waited for; matrix products, arithmetic and copies ran while one was open for 2% of the time, Pallas kernels for 3%

profile of v1, /device:TPU:0, one launch (start us, length us, event | category | flops | bytes accessed | tf_op | source)
XLA Modules:
  0.0 141.7 jit_solution(13923246044615914682)
XLA Ops:
  0.6 0.0 copy-start.4
  0.6 2.2 %pack_heads.1 = bf16[8,288,128]{2,1,0:T(8,128)(2,1)} custom-call(bf16[128,768]{1,0:T(8,128)(2,1)} %bitcast.23, bf16[128,768]{1,0:T(8,128)(2,1)} %bitcast.24, bf16[128,768]{1,0:T(8,128)(2,1)} %bitcast.25), custom_call_target="tpu_custom_call" | custom-call | tf_op jit(solution)/shard_map/pack_heads/pallas_call | solution.py:219
  2.8 7.4 %all-to-all-start = ((bf16[8,288,128]{2,1,0:T(8,128)(2,1)}), bf16[8,288,128]{2,1,0:T(8,128)(2,1)S(1)}, u32[]{:S(2)}, u32[]{:S(2)}) async-start(bf16[8,288,128]{2,1,0:T(8,128)(2,1)} %pack_heads.1), calls=%async_computation | async-start | bytes 1179648 | tf_op jit(solution)/shard_map/all_to_all | solution.py:655
  10.9 0.8 slice_bitcast_fusion.2
  11.8 14.4 %all-to-all-done.q_ref.k_ref.v_ref = bf16[8,288,128]{2,1,0:T(8,128)(2,1)S(1)} async-done(((bf16[8,288,128]{2,1,0:T(8,128)(2,1)}), bf16[8,288,128]{2,1,0:T(8,128)(2,1)S(1)}, u32[]{:S(2)}, u32[]{:S(2)}) %all-to-all-start) | async-done | bytes 589856 | tf_op jit(solution)/shard_map/all_to_all | solution.py:655
  26.1 0.8 copy-done
  27.0 5.8 %forward_heads.1 = (bf16[8,144,128]{2,1,0:T(8,128)(2,1)}, f32[1,1024]{1,0:T(1,128)}) custom-call(s32[1]{0:T(128)S(6)} %copy.15.length_ref, bf16[8,288,128]{2,1,0:T(8,128)(2,1)} %copy-done, bf16[8,288,128]{2,1,0:T(8,128)(2,1)} %copy-done, bf16[8,288,128]{2,1,0:T(8,128)(2,1)} %copy-done), custom_call_target="tpu_custom_call" | custom-call | tf_op jit(solution)/shard_map/forward_heads/pallas_call | solution.py:289
  32.7 3.6 %all-to-all-start.1 = ((bf16[8,144,128]{2,1,0:T(8,128)(2,1)}), bf16[8,144,128]{2,1,0:T(8,128)(2,1)S(1)}, u32[]{:S(2)}, u32[]{:S(2)}) async-start(bf16[8,144,128]{2,1,0:T(8,128)(2,1)} %get-tuple-element.18.head_ref), calls=%async_computation.1 | async-start | bytes 589824 | tf_op jit(solution)/shard_map/all_to_all | solution.py:655
  36.4 3.9 %collective-permute-start = (bf16[48,1536]{1,0:T(8,128)(2,1)S(1)}, bf16[48,1536]{1,0:T(8,128)(2,1)S(1)}, u32[]{:S(2)}, u32[]{:S(2)}) collective-permute-start(bf16[48,1536]{1,0:T(8,128)(2,1)S(1)} %pad_maximum_fusion), channel_id=1, source_target_pairs={{0,4},{4,8},{8,12},{12,16},{16,20},{20,24},{24,28},{1,5},{5,9},{9,... | collective-permute-start | bytes 442376 | tf_op jit(solution)/shard_map/ppermute | solution.py:673
  40.3 1.3 collective-permute-start.1
  41.6 0.6 broadcast_in_dim.12.bias_ref
  42.2 0.7 pad_add_fusion.info_ref
  42.9 1.3 collective-permute-done.before_ref
  44.2 3.5 %collective-permute-done.1.after_ref = bf16[48,1536]{1,0:T(8,128)(2,1)S(1)} collective-permute-done((bf16[48,1536]{1,0:T(8,128)(2,1)S(1)}, bf16[48,1536]{1,0:T(8,128)(2,1)S(1)}, u32[]{:S(2)}, u32[]{:S(2)}) %collective-permute-start.1) | collective-permute-done | bytes 147488 | tf_op jit(solution)/shard_map/ppermute | solution.py:674
  47.7 0.0 all-to-all-done.1.main_ref.edge_ref.refs_4_
  47.7 0.0 copy-done.9
  47.7 0.7 copy-done.11
  48.4 0.1 copy-done.1
  48.5 12.1 %middle.1 = (bf16[128,1536]{1,0:T(8,128)(2,1)}, bf16[128,1536]{1,0:T(8,128)(2,1)}, bf16[8,96,128]{2,1,0:T(8,128)(2,1)}, bf16[576,128]{1,0:T(8,128)(2,1)}, bf16[5...) custom-call(s32[3]{0:T(128)} %pad_add_fusion.info_ref, bf16[8,144,128]{2,1,0:T(8,128)(2,1)} %copy-done.1, ...), custom_call_target="tpu_custom_call" | custom-call | tf_op jit(solution)/shard_map/middle/pallas_call | solution.py:504
  60.7 14.5 %all_to_all.25.grad_ref = bf16[8,96,128]{2,1,0:T(8,128)(2,1)} all-to-all(bf16[8,96,128]{2,1,0:T(8,128)(2,1)} %get-tuple-element.21), channel_id=1, replica_groups=mesh['seq'=8,'dp'=4] {'seq'}, dimensions={0} | all-to-all | bytes 393216 | tf_op jit(solution)/shard_map/all_to_all | solution.py:655
  75.2 5.1 %backward_heads.1 = bf16[8,96,128]{2,1,0:T(8,128)(2,1)} custom-call(s32[1]{0:T(128)S(6)} %copy.15.length_ref, bf16[8,288,128]{2,1,0:T(8,128)(2,1)} %copy-done, bf16[8,288,128]{2,1,0:T(8,128)(2,1)} %copy-done, bf16[8,288,128]{2,1,0:T(8,128)(2,1)} %copy-done, bf16[8,96,128]{2,1,0:T(8,128)(2,1)} %all_to_all.25.grad_ref, ...), custom_call_target="tpu_custom_call" | custom-call | tf_op jit(solution)/shard_map/backward_heads/pallas_call | solution.py:343
  80.3 3.4 %all-to-all-start.3 = ((bf16[8,96,128]{2,1,0:T(8,128)(2,1)}), bf16[8,96,128]{2,1,0:T(8,128)(2,1)S(1)}, u32[]{:S(2)}, u32[]{:S(2)}) async-start(bf16[8,96,128]{2,1,0:T(8,128)(2,1)} %backward_heads.1), calls=%async_computation.3 | async-start | bytes 393216 | tf_op jit(solution)/shard_map/all_to_all | solution.py:655
  83.7 0.1 collective-permute-start.2
  83.8 1.6 %collective-permute-start.5 = (bf16[8,96,128]{2,1,0:T(8,128)(2,1)S(1)}, bf16[8,96,128]{2,1,0:T(8,128)(2,1)S(1)}, u32[]{:S(2)}, u32[]{:S(2)}) collective-permute-start(bf16[8,96,128]{2,1,0:T(8,128)(2,1)S(1)} %slice.20), channel_id=1, source_target_pairs={{0,1},{1,2},{2,3},{3,0},{4,5},{5,6},{6,7},{7,4},{8,9},{9,10},{10,1... | collective-permute-start | bytes 589832 | tf_op jit(solution)/shard_map/ppermute | solution.py:680
  85.5 0.5 collective-permute-start.6
  86.0 0.9 collective-permute-start.7
  86.9 0.6 collective-permute-start.3
  87.5 0.9 collective-permute-done.2.refs_1_
  88.4 0.0 collective-permute-start.4
  88.4 11.6 %collective-permute-done.3.refs_2_ = bf16[576,128]{1,0:T(8,128)(2,1)S(1)} collective-permute-done((bf16[576,128]{1,0:T(8,128)(2,1)S(1)}, bf16[576,128]{1,0:T(8,128)(2,1)S(1)}, u32[]{:S(2)}, u32[]{:S(2)}) %collective-permute-start.3) | collective-permute-done | bytes 147488 | tf_op jit(solution)/shard_map/ppermute | solution.py:696
  100.0 0.6 collective-permute-done.4.refs_3_
  100.5 0.0 collective-permute-done.5.refs_5_
  100.5 0.0 collective-permute-done.6.refs_6_
  100.6 0.0 collective-permute-done.7.refs_7_
  100.6 0.0 copy-done.12
  100.6 0.6 copy-done.13
  101.2 0.1 copy-done.6
  101.3 0.1 copy-done.7
  101.3 0.1 copy-done.8
  101.4 3.0 %product.1 = bf16[8,48,896]{2,1,0:T(8,128)(2,1)} custom-call(bf16[576,128]{1,0:T(8,128)(2,1)} %get-tuple-element.23.refs_0_, bf16[576,128]{1,0:T(8,128)(2,1)} %copy-done.10, bf16[576,128]{1,0:T(8,128)(2,1)} %copy-done.12, bf16[576,128]{1,0:T(8,128)(2,1)} %copy-done.13, bf16[8,144,128]{2,1,0:T(8,128)(2,1)} %copy-done.1, bf16[8,96,128]{2,1,0:T(8,128)(2,1)} %copy-done.6, ...), custom_call_target="tpu_custom_call" | custom-call | tf_op jit(solution)/shard_map/product/pallas_call | solution.py:583
  104.4 0.0 all-to-all-done.3.in_ref
  104.4 5.9 %all-to-all-start.4 = ((bf16[8,48,896]{2,1,0:T(8,128)(2,1)}), bf16[8,48,896]{2,1,0:T(8,128)(2,1)S(1)}, u32[]{:S(2)}, u32[]{:S(2)}) async-start(bf16[8,48,896]{2,1,0:T(8,128)(2,1)} %product.1), calls=%async_computation.4 | async-start | bytes 1376256 | tf_op jit(solution)/shard_map/all_to_all | solution.py:655
  110.3 1.7 %unpack_heads.1 = bf16[128,768]{1,0:T(8,128)(2,1)} custom-call(bf16[8,96,128]{2,1,0:T(8,128)(2,1)} %copy-done.5), custom_call_target="tpu_custom_call" | custom-call | tf_op jit(solution)/shard_map/unpack_heads/pallas_call | solution.py:646
  112.0 17.3 %all-to-all-done.4.in_ref = bf16[8,48,896]{2,1,0:T(8,128)(2,1)S(1)} async-done(((bf16[8,48,896]{2,1,0:T(8,128)(2,1)}), bf16[8,48,896]{2,1,0:T(8,128)(2,1)S(1)}, u32[]{:S(2)}, u32[]{:S(2)}) %all-to-all-start.4) | async-done | bytes 688160 | tf_op jit(solution)/shard_map/all_to_all | solution.py:655
  129.4 0.9 copy-done.3
  130.2 1.9 %sum_shares.1 = bf16[48,896]{1,0:T(8,128)(2,1)} custom-call(bf16[8,48,896]{2,1,0:T(8,128)(2,1)} %copy-done.3), custom_call_target="tpu_custom_call" | custom-call | tf_op jit(solution)/shard_map/sum_shares/pallas_call | solution.py:604
  132.1 7.6 %all-gather = bf16[192,896]{1,0:T(8,128)(2,1)} all-gather(bf16[48,896]{1,0:T(8,128)(2,1)} %sum_shares.1), channel_id=2, replica_groups=mesh['seq'=8,'dp'=4] {'dp'}, dimensions={0}, use_global_device_ids=true | all-gather | bytes 430080 | tf_op jit(solution)/shard_map/all_gather | solution.py:701
  139.7 2.0 %finish.1 = (f32[192,768]{1,0:T(8,128)}, f32[31,192]{1,0:T(8,128)}, f32[1,192]{1,0:T(1,128)}) custom-call(bf16[4,48,896]{2,1,0:T(8,128)(2,1)} %bitcast.20), custom_call_target="tpu_custom_call" | custom-call | tf_op jit(solution)/shard_map/finish/pallas_call | solution.py:628
  (29 shorter events, 0.1 us)
Async XLA Ops:
  0.6 11.1 %copy-start.4 = (bf16[1,128,1536]{2,1,0:T(8,128)(2,1)S(1)}, bf16[1,128,1536]{2,1,0:T(8,128)(2,1)}, u32[]{:S(2)}) copy-start(bf16[1,128,1536]{2,1,0:T(8,128)(2,1)} %param.9) | copy-start | bytes 1179652
  2.8 38.8 %copy-start.14 = (f32[1536]{0:T(1024)S(1)}, f32[1536]{0:T(1024)}, u32[]{:S(2)}) copy-start(f32[1536]{0:T(1024)} %param.16) | copy-start | bytes 18436
  2.8 23.3 %all-to-all-start = ((bf16[8,288,128]{2,1,0:T(8,128)(2,1)}), bf16[8,288,128]{2,1,0:T(8,128)(2,1)S(1)}, u32[]{:S(2)}, u32[]{:S(2)}) async-start(bf16[8,288,128]{2,1,0:T(8,128)(2,1)} %pack_heads.1), calls=%async_computation | async-start | bytes 1179648 | tf_op jit(solution)/shard_map/all_to_all | solution.py:655
  26.1 0.8 copy-start
  32.7 15.0 %all-to-all-start.1 = ((bf16[8,144,128]{2,1,0:T(8,128)(2,1)}), bf16[8,144,128]{2,1,0:T(8,128)(2,1)S(1)}, u32[]{:S(2)}, u32[]{:S(2)}) async-start(bf16[8,144,128]{2,1,0:T(8,128)(2,1)} %get-tuple-element.18.head_ref), calls=%async_computation.1 | async-start | bytes 589824 | tf_op jit(solution)/shard_map/all_to_all | solution.py:655
  36.4 7.8 %collective-permute-start = (bf16[48,1536]{1,0:T(8,128)(2,1)S(1)}, bf16[48,1536]{1,0:T(8,128)(2,1)S(1)}, u32[]{:S(2)}, u32[]{:S(2)}) collective-permute-start(bf16[48,1536]{1,0:T(8,128)(2,1)S(1)} %pad_maximum_fusion), channel_id=1, source_target_pairs={{0,4},{4,8},{8,12},{12,16},{16,20},{20,24},{24,28},{1,5},{5,9},{9,... | collective-permute-start | bytes 442376 | tf_op jit(solution)/shard_map/ppermute | solution.py:673
  40.3 7.4 %collective-permute-start.1 = (bf16[48,1536]{1,0:T(8,128)(2,1)S(1)}, bf16[48,1536]{1,0:T(8,128)(2,1)S(1)}, u32[]{:S(2)}, u32[]{:S(2)}) collective-permute-start(bf16[48,1536]{1,0:T(8,128)(2,1)S(1)} %pad_maximum_fusion.1), channel_id=1, source_target_pairs={{4,0},{8,4},{12,8},{16,12},{20,16},{24,20},{28,24},{5,1},{9,5},{13... | collective-permute-start | bytes 442376 | tf_op jit(solution)/shard_map/ppermute | solution.py:674
  44.2 3.6 %copy-start.9 = (bf16[48,1536]{1,0:T(8,128)(2,1)}, bf16[48,1536]{1,0:T(8,128)(2,1)S(1)}, u32[]{:S(2)}) copy-start(bf16[48,1536]{1,0:T(8,128)(2,1)S(1)} %collective-permute-done.before_ref) | copy-start | bytes 442372
  47.7 0.7 copy-start.11
  47.7 0.8 copy-start.1
  60.6 23.1 %copy-start.17 = (bf16[576,128]{1,0:T(8,128)(2,1)S(1)}, bf16[576,128]{1,0:T(8,128)(2,1)}, u32[]{:S(2)}) copy-start(bf16[576,128]{1,0:T(8,128)(2,1)} %get-tuple-element.24) | copy-start | bytes 442372
  60.7 23.2 %copy-start.2 = (bf16[8,144,128]{2,1,0:T(8,128)(2,1)S(1)}, bf16[8,144,128]{2,1,0:T(8,128)(2,1)}, u32[]{:S(2)}) copy-start(bf16[8,144,128]{2,1,0:T(8,128)(2,1)} %copy-done.1) | copy-start | bytes 884740
  60.7 26.2 %copy-start.16 = (bf16[576,128]{1,0:T(8,128)(2,1)S(1)}, bf16[576,128]{1,0:T(8,128)(2,1)}, u32[]{:S(2)}) copy-start(bf16[576,128]{1,0:T(8,128)(2,1)} %get-tuple-element.25) | copy-start | bytes 442372
  60.7 27.7 %copy-start.15 = (bf16[576,128]{1,0:T(8,128)(2,1)S(1)}, bf16[576,128]{1,0:T(8,128)(2,1)}, u32[]{:S(2)}) copy-start(bf16[576,128]{1,0:T(8,128)(2,1)} %get-tuple-element.26) | copy-start | bytes 442372
  80.3 24.1 %all-to-all-start.3 = ((bf16[8,96,128]{2,1,0:T(8,128)(2,1)}), bf16[8,96,128]{2,1,0:T(8,128)(2,1)S(1)}, u32[]{:S(2)}, u32[]{:S(2)}) async-start(bf16[8,96,128]{2,1,0:T(8,128)(2,1)} %backward_heads.1), calls=%async_computation.3 | async-start | bytes 393216 | tf_op jit(solution)/shard_map/all_to_all | solution.py:655
  83.7 4.6 %collective-permute-start.2 = (bf16[576,128]{1,0:T(8,128)(2,1)S(1)}, bf16[576,128]{1,0:T(8,128)(2,1)S(1)}, u32[]{:S(2)}, u32[]{:S(2)}) collective-permute-start(bf16[576,128]{1,0:T(8,128)(2,1)S(1)} %copy-done.17), channel_id=1, source_target_pairs={{0,1},{1,2},{2,3},{3,0},{4,5},{5,6},{6,7},{7,4},{8,9},{9,10},{10,1... | collective-permute-start | bytes 442376 | tf_op jit(solution)/shard_map/ppermute | solution.py:696
  83.8 16.7 %collective-permute-start.5 = (bf16[8,96,128]{2,1,0:T(8,128)(2,1)S(1)}, bf16[8,96,128]{2,1,0:T(8,128)(2,1)S(1)}, u32[]{:S(2)}, u32[]{:S(2)}) collective-permute-start(bf16[8,96,128]{2,1,0:T(8,128)(2,1)S(1)} %slice.20), channel_id=1, source_target_pairs={{0,1},{1,2},{2,3},{3,0},{4,5},{5,6},{6,7},{7,4},{8,9},{9,10},{10,1... | collective-permute-start | bytes 589832 | tf_op jit(solution)/shard_map/ppermute | solution.py:680
  85.5 15.1 %collective-permute-start.6 = (bf16[8,96,128]{2,1,0:T(8,128)(2,1)S(1)}, bf16[8,96,128]{2,1,0:T(8,128)(2,1)S(1)}, u32[]{:S(2)}, u32[]{:S(2)}) collective-permute-start(bf16[8,96,128]{2,1,0:T(8,128)(2,1)S(1)} %slice.20), channel_id=1, source_target_pairs={{0,2},{1,3},{2,0},{3,1},{4,6},{5,7},{6,4},{7,5},{8,10},{9,11},{10,... | collective-permute-start | bytes 589832 | tf_op jit(solution)/shard_map/ppermute | solution.py:680
  86.0 14.6 %collective-permute-start.7 = (bf16[8,96,128]{2,1,0:T(8,128)(2,1)S(1)}, bf16[8,96,128]{2,1,0:T(8,128)(2,1)S(1)}, u32[]{:S(2)}, u32[]{:S(2)}) collective-permute-start(bf16[8,96,128]{2,1,0:T(8,128)(2,1)S(1)} %slice.20), channel_id=1, source_target_pairs={{0,3},{1,0},{2,1},{3,2},{4,7},{5,4},{6,5},{7,6},{8,11},{9,8},{10,9... | collective-permute-start | bytes 589832 | tf_op jit(solution)/shard_map/ppermute | solution.py:680
  86.9 13.0 %collective-permute-start.3 = (bf16[576,128]{1,0:T(8,128)(2,1)S(1)}, bf16[576,128]{1,0:T(8,128)(2,1)S(1)}, u32[]{:S(2)}, u32[]{:S(2)}) collective-permute-start(bf16[576,128]{1,0:T(8,128)(2,1)S(1)} %copy-done.16), channel_id=1, source_target_pairs={{0,2},{1,3},{2,0},{3,1},{4,6},{5,7},{6,4},{7,5},{8,10},{9,11},{10,... | collective-permute-start | bytes 442376 | tf_op jit(solution)/shard_map/ppermute | solution.py:696
  88.4 12.2 %copy-start.10 = (bf16[576,128]{1,0:T(8,128)(2,1)}, bf16[576,128]{1,0:T(8,128)(2,1)S(1)}, u32[]{:S(2)}) copy-start(bf16[576,128]{1,0:T(8,128)(2,1)S(1)} %collective-permute-done.2.refs_1_) | copy-start | bytes 442372
  88.4 12.2 %collective-permute-start.4 = (bf16[576,128]{1,0:T(8,128)(2,1)S(1)}, bf16[576,128]{1,0:T(8,128)(2,1)S(1)}, u32[]{:S(2)}, u32[]{:S(2)}) collective-permute-start(bf16[576,128]{1,0:T(8,128)(2,1)S(1)} %copy-done.15), channel_id=1, source_target_pairs={{0,3},{1,0},{2,1},{3,2},{4,7},{5,4},{6,5},{7,6},{8,11},{9,8},{10,9... | collective-permute-start | bytes 442376 | tf_op jit(solution)/shard_map/ppermute | solution.py:696
  99.9 0.7 copy-start.12
  100.5 0.7 copy-start.13
  100.5 0.7 copy-start.6
  100.6 0.8 copy-start.7
  100.6 0.8 copy-start.8
  104.4 5.9 %copy-start.5 = (bf16[8,96,128]{2,1,0:T(8,128)(2,1)}, bf16[8,96,128]{2,1,0:T(8,128)(2,1)S(1)}, u32[]{:S(2)}) copy-start(bf16[8,96,128]{2,1,0:T(8,128)(2,1)S(1)} %all-to-all-done.3.in_ref) | copy-start | bytes 589828
  104.4 24.9 %all-to-all-start.4 = ((bf16[8,48,896]{2,1,0:T(8,128)(2,1)}), bf16[8,48,896]{2,1,0:T(8,128)(2,1)S(1)}, u32[]{:S(2)}, u32[]{:S(2)}) async-start(bf16[8,48,896]{2,1,0:T(8,128)(2,1)} %product.1), calls=%async_computation.4 | async-start | bytes 1376256 | tf_op jit(solution)/shard_map/all_to_all | solution.py:655
  129.3 0.9 copy-start.3

commit v2 on v1

--- a/solution.py
+++ b/solution.py
@@ -189,7 +189,8 @@
 CHUNK = 384
 LANES = 128
 MASKED_SCORE = -1e30
-VMEM_LIMIT = 56 * 1024 * 1024
+QUERIES, KEYS, VALUES = (slice(place * HS, (place + 1) * HS) for place in range(3))
+VMEM_LIMIT = 40 * 1024 * 1024
 SCORE_SCALE = 1.0 / math.sqrt(HS)
 LOG2_SCALE = SCORE_SCALE * math.log2(math.e)
 
@@ -206,6 +207,22 @@
 
 def whole(shape):
     return pl.BlockSpec(shape, lambda *_: (0,) * len(shape))
+
+
+def near(array):
+    return pltpu.with_memory_space_constraint(array, pltpu.VMEM)
+
+
+def far(array):
+    return pltpu.with_memory_space_constraint(array, pltpu.HBM)
+
+
+def here(count=None):
+    spec = pl.BlockSpec(memory_space=pltpu.VMEM)
+    return spec if count is None else [spec] * count
+
+
+SCALARS = pl.BlockSpec(memory_space=pltpu.SMEM)
 
 
 def pack_kernel(q_ref, k_ref, v_ref, out_ref):
@@ -221,84 +238,73 @@
         out_shape=jax.ShapeDtypeStruct((H, 3 * HS, frames), BF16),
         compiler_params=params(),
         name="pack_heads",
-    )(q, k, v)
-
-
-def key_rows(k_ref, length, keys_sc):
-    blocks, _, frames = k_ref.shape
+    )(far(q), far(k), far(v))
+
+
+def key_rows(x_ref, length, keys_sc):
+    blocks, _, frames = x_ref.shape
     for block in range(blocks):
         row = lax.broadcasted_iota(jnp.int32, (LANES - HS, frames), 0)
         key = lax.broadcasted_iota(jnp.int32, (LANES - HS, frames), 1) + block * frames
         extra = jnp.where((row == 0) & (key >= length), MASKED_SCORE, 0.0)
-        tall = jnp.concatenate([k_ref[block].astype(F32), extra], axis=0)
+        tall = jnp.concatenate([x_ref[block, KEYS].astype(F32), extra], axis=0)
         keys_sc[block * frames : (block + 1) * frames, :] = tall.T.astype(BF16)
 
 
-def query_columns(q_ref):
-    query = jnp.concatenate([q_ref[0], q_ref[1]], axis=1)
+def pair_of(ref, first, rows):
+    return jnp.concatenate([ref[first, rows], ref[first + 1, rows]], axis=1)
+
+
+def query_columns(x_ref, first):
+    query = pair_of(x_ref, first, QUERIES)
     row = lax.broadcasted_iota(jnp.int32, (LANES - HS, query.shape[1]), 0)
     return jnp.concatenate([query, jnp.where(row == 0, 1.0, 0.0).astype(BF16)], axis=0)
 
 
-def side_by_side(ref, wide_sc):
-    blocks, _, frames = ref.shape
+def side_by_side(x_ref, rows, wide_sc):
+    blocks, _, frames = x_ref.shape
     for block in range(blocks):
-        wide_sc[:, block * frames : (block + 1) * frames] = ref[block]
-
-
-def forward_kernel(length_ref, q_ref, k_ref, v_ref, out_ref, lse_ref, keys_sc, values_sc):
-    step = pl.program_id(0)
-    blocks, _, frames = k_ref.shape
-
-    @pl.when(step == 0)
-    def _():
-        key_rows(k_ref, length_ref[0], keys_sc)
-        side_by_side(v_ref, values_sc)
-
-    scores = jnp.dot(keys_sc[...], query_columns(q_ref), preferred_element_type=F32) * LOG2_SCALE
-    top = jnp.max(scores, axis=0, keepdims=True)
-    raised = jnp.exp2(scores - top)
-    total = jnp.sum(raised, axis=0, keepdims=True)
-    weights = (raised * (1.0 / total)).astype(BF16)
-    lse_ref[...] = top + jnp.log2(total)
-    mixed = jnp.dot(values_sc[...], weights, preferred_element_type=F32).astype(BF16)
-    out_ref[2 * step, :HS, :] = mixed[:, :frames]
-    out_ref[2 * step + 1, :HS, :] = mixed[:, frames:]
-
-    @pl.when(step == pl.num_programs(0) - 1)
-    def _():
-        lane = lax.broadcasted_iota(jnp.int32, (HS, frames), 1)
-        nothing = jnp.zeros((HS, frames), F32)
-        for block in range(blocks):
-            left = nothing
-            right = nothing
-            if block > 0:
-                left = pltpu.roll(out_ref[block - 1, :HS, :].astype(F32), WIDE, 1)
-            if block < blocks - 1:
-                right = pltpu.roll(out_ref[block + 1, :HS, :].astype(F32), WIDE, 1)
-            both = jnp.where(lane < WIDE, left, right)
-            lower = pltpu.roll(both[HS // 2 :], 2 * WIDE, 1)
-            packed = jnp.where(lane[: HS // 2] < 2 * WIDE, both[: HS // 2], lower)
-            out_ref[block, HS:, :] = packed.astype(BF16)
-
-
-def forward_heads(length, received):
+        wide_sc[:, block * frames : (block + 1) * frames] = x_ref[block, rows]
+
+
+def forward_kernel(info_ref, x_ref, out_ref, lse_ref, keys_sc, values_sc):
+    blocks, _, frames = x_ref.shape
+    key_rows(x_ref, info_ref[1], keys_sc)
+    side_by_side(x_ref, VALUES, values_sc)
+    for first in range(0, blocks, 2):
+        scores = jnp.dot(keys_sc[...], query_columns(x_ref, first), preferred_element_type=F32)
+        scores = scores * LOG2_SCALE
+        top = jnp.max(scores, axis=0, keepdims=True)
+        raised = jnp.exp2(scores - top)
+        total = jnp.sum(raised, axis=0, keepdims=True)
+        weights = (raised * (1.0 / total)).astype(BF16)
+        lse_ref[:, first * frames : (first + 2) * frames] = top + jnp.log2(total)
+        mixed = jnp.dot(values_sc[...], weights, preferred_element_type=F32).astype(BF16)
+        out_ref[first, :HS, :] = mixed[:, :frames]
+        out_ref[first + 1, :HS, :] = mixed[:, frames:]
+
+    lane = lax.broadcasted_iota(jnp.int32, (HS, frames), 1)
+    nothing = jnp.zeros((HS, frames), F32)
+    for block in range(blocks):
+        left = nothing
+        right = nothing
+        if block > 0:
+            left = pltpu.roll(out_ref[block - 1, :HS, :].astype(F32), WIDE, 1)
+        if block < blocks - 1:
+            right = pltpu.roll(out_ref[block + 1, :HS, :].astype(F32), WIDE, 1)
+        both = jnp.where(lane < WIDE, left, right)
+        lower = pltpu.roll(both[HS // 2 :], 2 * WIDE, 1)
+        packed = jnp.where(lane[: HS // 2] < 2 * WIDE, both[: HS // 2], lower)
+        out_ref[block, HS:, :] = packed.astype(BF16)
+
+
+def forward_heads(info, received):
     blocks, _, frames = received.shape
     total = blocks * frames
-    block = (blocks, HS, frames)
     return pl.pallas_call(
         forward_kernel,
-        grid=(blocks // 2,),
-        in_specs=[
-            pl.BlockSpec(memory_space=pltpu.SMEM),
-            pl.BlockSpec((2, HS, frames), lambda i: (i, 0, 0)),
-            pl.BlockSpec(block, lambda i: (0, 1, 0)),
-            pl.BlockSpec(block, lambda i: (0, 2, 0)),
-        ],
-        out_specs=[
-            whole((blocks, HS + HS // 2, frames)),
-            pl.BlockSpec((1, 2 * frames), lambda i: (0, i)),
-        ],
+        in_specs=[SCALARS, here()],
+        out_specs=here(2),
         out_shape=[
             jax.ShapeDtypeStruct((blocks, HS + HS // 2, frames), BF16),
             jax.ShapeDtypeStruct((1, total), F32),
@@ -306,62 +312,50 @@
         scratch_shapes=[pltpu.VMEM((total, LANES), BF16), pltpu.VMEM((HS, total), BF16)],
         compiler_params=params(),
         name="forward_heads",
-    )(length, received, received, received)
-
-
-def backward_kernel(
-    length_ref, q_ref, k_ref, v_ref, grad_ref, head_ref, lse_ref, out_ref, keys_sc, values_sc, wide_sc
-):
-    step = pl.program_id(0)
-    blocks, _, frames = k_ref.shape
-
-    @pl.when(step == 0)
-    def _():
-        key_rows(k_ref, length_ref[0], keys_sc)
-        side_by_side(k_ref, wide_sc)
-        for block in range(blocks):
-            rows = v_ref[block].astype(F32).T.astype(BF16)
-            values_sc[block * frames : (block + 1) * frames, :] = rows
-
-    scores = jnp.dot(keys_sc[...], query_columns(q_ref), preferred_element_type=F32) * LOG2_SCALE
-    probs = jnp.exp2(scores - lse_ref[...])
-    grad = jnp.concatenate([grad_ref[0], grad_ref[1]], axis=1)
-    head = jnp.concatenate([head_ref[0], head_ref[1]], axis=1)
-    delta = jnp.sum(grad.astype(F32) * head.astype(F32), axis=0, keepdims=True)
-    grad_prob = jnp.dot(values_sc[...], grad, preferred_element_type=F32)
-    grad_score = (probs * (grad_prob - delta)).astype(BF16)
-    result = jnp.dot(wide_sc[...], grad_score, preferred_element_type=F32) * SCORE_SCALE
-    out_ref[0] = result[:, :frames].astype(BF16)
-    out_ref[1] = result[:, frames:].astype(BF16)
-
-
-def backward_heads(length, received, grads, heads, lse):
+    )(info, near(received))
+
+
+def backward_kernel(info_ref, x_ref, grad_ref, head_ref, lse_ref, *rest):
+    outs, (keys_sc, values_sc, wide_sc, result_sc) = rest[:-4], rest[-4:]
+    blocks, _, frames = x_ref.shape
+    key_rows(x_ref, info_ref[1], keys_sc)
+    side_by_side(x_ref, KEYS, wide_sc)
+    for block in range(blocks):
+        rows = x_ref[block, VALUES].astype(F32).T.astype(BF16)
+        values_sc[block * frames : (block + 1) * frames, :] = rows
+
+    for first in range(0, blocks, 2):
+        scores = jnp.dot(keys_sc[...], query_columns(x_ref, first), preferred_element_type=F32)
+        probs = jnp.exp2(scores * LOG2_SCALE - lse_ref[:, first * frames : (first + 2) * frames])
+        grad = pair_of(grad_ref, first, slice(0, HS))
+        head = pair_of(head_ref, first, slice(0, HS))
+        delta = jnp.sum(grad.astype(F32) * head.astype(F32), axis=0, keepdims=True)
+        grad_prob = jnp.dot(values_sc[...], grad, preferred_element_type=F32)
+        grad_score = (probs * (grad_prob - delta)).astype(BF16)
+        result = jnp.dot(wide_sc[...], grad_score, preferred_element_type=F32) * SCORE_SCALE
+        result_sc[first] = result[:, :frames].astype(BF16)
+        result_sc[first + 1] = result[:, frames:].astype(BF16)
+    for away, out_ref in enumerate(outs):
+        out_ref[...] = result_sc[lax.rem(info_ref[3] + away, blocks)]
+
+
+def backward_heads(info, received, grads, heads, lse):
     blocks, _, frames = received.shape
     total = blocks * frames
-    block = (blocks, HS, frames)
-    pair = pl.BlockSpec((2, HS, frames), lambda i: (i, 0, 0))
     return pl.pallas_call(
         backward_kernel,
-        grid=(blocks // 2,),
-        in_specs=[
-            pl.BlockSpec(memory_space=pltpu.SMEM),
-            pair,
-            pl.BlockSpec(block, lambda i: (0, 1, 0)),
-            pl.BlockSpec(block, lambda i: (0, 2, 0)),
-            pair,
-            pair,
-            pl.BlockSpec((1, 2 * frames), lambda i: (0, i)),
-        ],
-        out_specs=pair,
-        out_shape=jax.ShapeDtypeStruct((blocks, HS, frames), BF16),
+        in_specs=[SCALARS] + here(4),
+        out_specs=here(blocks),
+        out_shape=[jax.ShapeDtypeStruct((HS, frames), BF16)] * blocks,
         scratch_shapes=[
             pltpu.VMEM((total, LANES), BF16),
             pltpu.VMEM((total, HS), BF16),
             pltpu.VMEM((HS, total), BF16),
+            pltpu.VMEM((blocks, HS, frames), BF16),
         ],
         compiler_params=params(),
         name="backward_heads",
-    )(length, received, received, received, grads, heads, lse)
+    )(info, near(received), near(grads), heads, lse)
 
 
 def shifted_sum(ref, tile, rows, weight_of, start):
@@ -377,8 +371,7 @@
 
 def middle_kernel(
     info_ref,
-    main_ref,
-    edge_ref,
+    att_ref,
     input_ref,
     cot_ref,
     before_ref,
@@ -403,9 +396,9 @@
 
     @pl.when(step == 0)
     def _():
-        main = main_ref[...].reshape(HD, frames)
+        main = att_ref[:, :HS, :].reshape(HD, frames)
         att_sc[WIDE : WIDE + frames, :] = main.T
-        edge = edge_ref[...].astype(F32).reshape(H * (HS // 2), frames)
+        edge = att_ref[:, HS:, :].astype(F32).reshape(H * (HS // 2), frames)
         lower = pltpu.roll(edge, frames - 2 * WIDE, 1)
         half = (H, HS // 2, frames)
         tall = jnp.concatenate([edge.reshape(half), lower.reshape(half)], axis=1)
@@ -417,15 +410,16 @@
     projected = lax.dot_general(
         att_sc[...], proj_ref[...], (((1,), (1,)), ((), ())), preferred_element_type=F32
     )
+    chunk = pl.ds(pl.multiple_of(step * CHUNK, CHUNK), CHUNK)
     wide_input = jnp.concatenate(
-        [before_ref[:WIDE, :], input_ref[...], after_ref[:WIDE, :]], axis=0
+        [before_ref[:WIDE, chunk], input_ref[...], after_ref[:WIDE, chunk]], axis=0
     ).astype(F32)
     mixed = (wide_input + projected).astype(BF16).astype(F32)
     frame = first - WIDE + lax.broadcasted_iota(jnp.int32, (rows, CHUNK), 0)
     valid = (frame >= 0) & (frame < length)
     masked = jnp.where(valid, mixed, 0.0)
     cot = jnp.concatenate(
-        [before_ref[WIDE:, :], cot_ref[...], after_ref[WIDE:, :]], axis=0
+        [before_ref[WIDE:, chunk], cot_ref[...], after_ref[WIDE:, chunk]], axis=0
     ).astype(F32)
     inner = slice(WIDE - SIDE, WIDE + SIDE + frames)
     cot = jnp.where(valid[inner], cot, 0.0)
@@ -433,7 +427,7 @@
         masked_sc[tile] = masked[:, tile * LANES : (tile + 1) * LANES]
 
     own = slice(SIDE, SIDE + frames)
-    here = valid[WIDE : WIDE + frames, :LANES]
+    inside = valid[WIDE : WIDE + frames, :LANES]
     for tile in range(tiles):
         lanes = slice(tile * LANES, (tile + 1) * LANES)
         start = jnp.broadcast_to(bias_ref[:, lanes], (span, LANES))
@@ -442,7 +436,7 @@
         )
         gate = lax.logistic(conv)
         center = masked_sc[tile, WIDE : WIDE + frames, :]
-        block_out_ref[:, lanes] = jnp.where(here, center + conv[own] * gate[own], 0.0).astype(BF16)
+        block_out_ref[:, lanes] = jnp.where(inside, center + conv[own] * gate[own], 0.0).astype(BF16)
         gated = cot[:, lanes] * gate * (1.0 + conv * (1.0 - gate))
         gate_sc[tile] = gated
         owned = gated[own]
@@ -461,7 +455,7 @@
             lambda offset: tap_ref[KW - offset : KW - offset + 1, lanes],
             jnp.zeros((frames, LANES), F32),
         )
-        grad_in_ref[:, lanes] = (cot[own, lanes] + jnp.where(here, back, 0.0)).astype(BF16)
+        grad_in_ref[:, lanes] = (cot[own, lanes] + jnp.where(inside, back, 0.0)).astype(BF16)
 
     grad_in = grad_in_ref[...]
     grad_sc[...] += jnp.dot(grad_in, proj_ref[...], preferred_element_type=F32)
@@ -498,20 +492,18 @@
 
 def middle(info, returned, block_input, grad_output, before, after, out_proj, kernel, bias, dp_count):
     frames = block_input.shape[0]
-    halo = WIDE + SIDE
     piece_rows = D // dp_count + D // dp_count // 2
     column = lambda count: pl.BlockSpec((count, CHUNK), lambda i: (0, i))
     return pl.pallas_call(
         middle_kernel,
         grid=(D // CHUNK,),
         in_specs=[
-            pl.BlockSpec(memory_space=pltpu.SMEM),
-            pl.BlockSpec((H, HS, frames), lambda i: (0, 0, 0)),
-            pl.BlockSpec((H, HS // 2, frames), lambda i: (0, 2, 0)),
+            SCALARS,
+            here(),
             column(frames),
             column(frames),
-            column(halo),
-            column(halo),
+            here(),
+            here(),
             pl.BlockSpec((CHUNK, HD), lambda i: (i, 0)),
             column(KW),
             column(1),
@@ -538,7 +530,17 @@
         ],
         compiler_params=params(),
         name="middle",
-    )(info, returned, returned, block_input, grad_output, before, after, out_proj, kernel, bias)
+    )(
+        info,
+        near(returned),
+        far(block_input),
+        far(grad_output),
+        near(before),
+        near(after),
+        far(out_proj),
+        far(kernel),
+        bias,
+    )
 
 
 def split_parts(lane, value):
@@ -551,71 +553,83 @@
     return value + pltpu.roll(value, LANES - TAP_ROWS, 1)
 
 
+def store_share(out_ref, share, taps):
+    piece = share.shape[-2]
+    for tile in range(HD // LANES):
+        rows = slice(tile * piece, (tile + 1) * piece)
+        out_ref[..., rows, :] = share[..., tile * LANES : (tile + 1) * LANES].astype(BF16)
+    out_ref[..., HD // LANES * piece :, :] = taps.astype(BF16)
+
+
 def product_kernel(*refs):
     out_ref = refs[-1]
     count = (len(refs) - 1) // 2
     pieces, heads = refs[:count], refs[count : 2 * count]
-    slabs, piece, _ = out_ref.shape
+    slabs = out_ref.shape[0]
     frames = pieces[0].shape[1]
-    height = slabs * piece
+    height = pieces[0].shape[0] * 2 // 3
+    piece = height // slabs
     total = jnp.zeros((height, HD), F32)
     taps = jnp.zeros((height // 2, frames), F32)
     for piece_ref, head_ref in zip(pieces, heads):
         total += lax.dot_general(
             piece_ref[:height, :],
-            head_ref[...].reshape(HD, frames),
+            head_ref[:, :HS, :].reshape(HD, frames),
             (((1,), (1,)), ((), ())),
             preferred_element_type=F32,
         )
         taps += piece_ref[height:, :].astype(F32)
-    out_ref[:, :, :HD] = total.astype(BF16).reshape(slabs, piece, HD)
     lane = lax.broadcasted_iota(jnp.int32, taps.shape, 1)
     parts = split_parts(lane, join_parts(taps)).reshape(slabs, piece // 2, LANES)
-    padded = jnp.concatenate([parts, jnp.zeros_like(parts)], axis=1)
-    out_ref[:, :, HD:] = padded.astype(BF16)
+    store_share(out_ref, total.reshape(slabs, piece, HD), parts)
 
 
 def product(pieces, heads, returned, seq_count):
-    frames = returned.shape[2]
-    piece_rows = pieces[0].shape[0]
-    height = piece_rows * 2 // 3
-    head_spec = whole((H, HS, frames))
+    height = pieces[0].shape[0] * 2 // 3
+    piece = height // seq_count
+    share_rows = piece * HD // LANES + piece // 2
+    near_heads = [near(array) for array in [returned, *heads]]
+    near_pieces = [pieces[0]] + [near(array) for array in pieces[1:]]
     return pl.pallas_call(
         product_kernel,
-        grid=(1,),
-        in_specs=[whole((piece_rows, frames))] * len(pieces) + [head_spec] * len(pieces),
-        out_specs=whole((seq_count, height // seq_count, HD + LANES)),
-        out_shape=jax.ShapeDtypeStruct((seq_count, height // seq_count, HD + LANES), BF16),
+        in_specs=here(2 * len(pieces)),
+        out_specs=here(),
+        out_shape=jax.ShapeDtypeStruct((seq_count, share_rows, LANES), BF16),
         compiler_params=params(),
         name="product",
-    )(*pieces, returned, *heads)
+    )(*near_pieces, *near_heads)
 
 
 def sum_kernel(in_ref, out_ref):
     total = jnp.sum(in_ref[...].astype(F32), axis=0)
-    out_ref[:, :HD] = total[:, :HD].astype(BF16)
-    taps = total[:, HD:]
+    rows = total.shape[0] * 12 // 13
+    out_ref[:rows, :] = total[:rows].astype(BF16)
+    taps = total[rows:]
     lane = lax.broadcasted_iota(jnp.int32, taps.shape, 1)
-    out_ref[:, HD:] = split_parts(lane, join_parts(taps)).astype(BF16)
+    out_ref[rows:, :] = split_parts(lane, join_parts(taps)).astype(BF16)
 
 
 def sum_shares(shares):
-    _, piece, width = shares.shape
     return pl.pallas_call(
         sum_kernel,
-        out_shape=jax.ShapeDtypeStruct((piece, width), BF16),
+        in_specs=[here()],
+        out_specs=here(),
+        out_shape=jax.ShapeDtypeStruct(shares.shape[1:], BF16),
         compiler_params=params(),
         name="sum_shares",
-    )(shares)
+    )(near(shares))
 
 
 def finish_kernel(in_ref, proj_ref, tap_ref, bias_ref):
-    owners, piece, _ = in_ref.shape
-    half = piece // 2
+    owners, share_rows, _ = in_ref.shape
+    rows = share_rows * 12 // 13
+    piece = rows * LANES // HD
     columns = []
     for owner in range(owners):
-        proj_ref[owner * piece : (owner + 1) * piece, :] = in_ref[owner, :, :HD].astype(F32)
-        taps = join_parts(in_ref[owner, :half, HD:].astype(F32))
+        for tile in range(HD // LANES):
+            part = in_ref[owner, tile * piece : (tile + 1) * piece, :].astype(F32)
+            proj_ref[owner * piece : (owner + 1) * piece, tile * LANES : (tile + 1) * LANES] = part
+        taps = join_parts(in_ref[owner, rows:, :].astype(F32))
         columns += [taps, pltpu.roll(taps, LANES // 2, 1)]
     turned = jnp.concatenate(columns, axis=0).T
     tap_ref[...] = turned[:KW]
@@ -623,10 +637,12 @@
 
 
 def finish(gathered):
-    owners, piece, _ = gathered.shape
-    width = owners * piece
+    owners, share_rows, _ = gathered.shape
+    width = owners * share_rows * 12 // 13 * LANES // HD
     return pl.pallas_call(
         finish_kernel,
+        in_specs=[here()],
+        out_specs=here(3),
         out_shape=[
             jax.ShapeDtypeStruct((width, HD), F32),
             jax.ShapeDtypeStruct((KW, width), F32),
@@ -634,21 +650,38 @@
         ],
         compiler_params=params(),
         name="finish",
-    )(gathered)
-
-
-def unpack_kernel(in_ref, out_ref):
-    out_ref[...] = in_ref[...].reshape(HD, in_ref.shape[2]).T
-
-
-def unpack_heads(heads):
-    frames = heads.shape[2]
+    )(near(gathered))
+
+
+def unpack_kernel(info_ref, *refs):
+    heads, out_ref, heads_sc = refs[:-2], refs[-2], refs[-1]
+    for away, head_ref in enumerate(heads):
+        heads_sc[lax.rem(info_ref[3] - away + H, H)] = head_ref[...]
+    out_ref[...] = heads_sc[...].reshape(HD, heads_sc.shape[2]).T
+
+
+def unpack_heads(info, heads):
+    frames = heads[0].shape[1]
     return pl.pallas_call(
         unpack_kernel,
+        in_specs=[SCALARS] + here(H),
+        out_specs=here(),
         out_shape=jax.ShapeDtypeStruct((frames, HD), BF16),
+        scratch_shapes=[pltpu.VMEM((H, HS, frames), BF16)],
         compiler_params=params(),
         name="unpack_heads",
-    )(heads)
+    )(info, heads[0], *[near(head) for head in heads[1:]])
+
+
+def ring(count, away):
+    return [(i, (i + away) % count) for i in range(count)]
+
+
+def send_round(blocks, axis):
+    count = len(blocks)
+    return [blocks[0]] + [
+        lax.ppermute(blocks[away], axis, ring(count, away)) for away in range(1, count)
+    ]
 
 
 def exchange(blocks, axis):
@@ -661,8 +694,9 @@
     frames = block_input.shape[1]
     seq_count = lax.axis_size("seq")
     dp_count = lax.axis_size("dp")
-    first_frame = lax.axis_index("seq") * frames
-    info = jnp.stack([first_frame, lengths[0], lax.axis_index("dp")]).astype(jnp.int32)
+    place = lax.axis_index("seq")
+    info = jnp.stack([place * frames, lengths[0], lax.axis_index("dp"), place]).astype(jnp.int32)
+    bias_row = conv_bias[None]
 
     received = exchange(pack_heads(query_proj[0], key_proj[0], value_proj[0]), "seq")
 
@@ -672,13 +706,14 @@
     down = [(j, i) for i, j in up]
     before = lax.ppermute(last, "seq", up)
     after = lax.ppermute(leading, "seq", down)
-
-    sent, lse = forward_heads(lengths, received)
+    received, before, after, info, bias_row = lax.optimization_barrier(
+        (received, before, after, info, bias_row)
+    )
+
+    sent, lse = forward_heads(info, received)
     returned = exchange(sent, "seq")
     mine = returned[:, :HS]
-    shifts = [[(i, (i + away) % dp_count) for i in range(dp_count)] for away in range(1, dp_count)]
-    heads = [lax.ppermute(mine, "dp", shift) for shift in shifts]
-
+    heads = send_round([mine] * dp_count, "dp")[1:]
     block_output, grad_input, grad_heads, *pieces = middle(
         info,
         returned,
@@ -688,16 +723,20 @@
         after,
         out_proj,
         kernel,
-        conv_bias[None],
+        bias_row,
         dp_count,
     )
+    grad_heads, heads, pieces = lax.optimization_barrier((grad_heads, heads, pieces))
+
     grads = exchange(grad_heads, "seq")
-    moved = [pieces[0]] + [
-        lax.ppermute(piece, "dp", shift) for piece, shift in zip(pieces[1:], shifts)
-    ]
-    grad_query = unpack_heads(exchange(backward_heads(lengths, received, grads, sent, lse), "seq"))
-
-    shares = exchange(product(moved, heads, returned, seq_count), "seq")
+    moved = send_round(pieces, "dp")
+    grads, moved = lax.optimization_barrier((grads, moved))
+    shares = product(moved, heads, returned, seq_count)
+    shares, grads = lax.optimization_barrier((shares, grads))
+    shares = exchange(shares, "seq")
+    query_parts = send_round(backward_heads(info, received, grads, sent, lse), "seq")
+    shares, query_parts = lax.optimization_barrier((shares, query_parts))
+    grad_query = unpack_heads(info, query_parts)
     gathered = lax.all_gather(sum_shares(shares), "dp")
     grad_proj, grad_kernel, grad_bias = finish(gathered)
     return (block_output[None], grad_input[None], grad_query[None], grad_proj, grad_kernel, grad_bias[0])

time: 143 us -> 110 us (0.77)
  waiting for transfers between devices: 49.5 us -> 27.2 us
  Pallas kernels: 33.8 us -> 24.5 us
  starting transfers between devices: 29.3 us -> 34.1 us
  local copies, waits for them, and re-layouts: 4.76 us -> 0.88 us
    all_to_all x4 -> x3, waiting for transfers between devices: 31.7 us -> 6 us  [exchange(): return lax.all_to_all(blocks, axis, split_axis=0, concat_axis=0, tiled=True)]
    ppermute x6 -> x13, starting transfers between devices: 3.72 us -> 13.6 us  [send_round(): lax.ppermute(blocks[away], axis, ring(count, away))]
    pallas_call x7, Pallas kernels: 31.6 us -> 22.4 us  [the longest x1 11.6 us: middle(): pl.pallas_call(middle_kernel, grid=(D // CHUNK,), in_specs=[SCALARS, here...]
    all_to_all x4 -> x3, starting transfers between devices: 20.3 us -> 15.3 us  [exchange(): return lax.all_to_all(blocks, axis, split_axis=0, concat_axis=0, tiled=True)]
    ppermute x1, waiting for transfers between devices: 1.27 us -> 4.92 us  [fast_device(): before = lax.ppermute(last, 'seq', up)]
    unnamed x36 -> x4, local copies, waits for them, and re-layouts: 3.3 us -> 0.01 us
    ppermute x1, waiting for transfers between devices: 3.54 us -> 0.93 us  [fast_device(): after = lax.ppermute(leading, 'seq', down)]
    ppermute x6 -> x13, waiting for transfers between devices: 13 us -> 15.4 us  [send_round(): lax.ppermute(blocks[away], axis, ring(count, away))]
  transfers between devices with their start and end apart: 12 -> 18, of which waited for: 7 -> 10; matrix products, arithmetic and copies ran while one was open for 2% -> 1% of each run, Pallas kernels for 3% -> 13%
where the time goes in v2:
time: 110 us; the launch traced here: 109 us
  starting transfers between devices  34.1 us (31%)
  waiting for transfers between devices  27.2 us (25%)
  Pallas kernels  24.5 us (22%)
  blocking collectives  20.7 us (19%)
  between operations  1.45 us (1%)
    ppermute x13, waiting for transfers between devices, send_round(): lax.ppermute(blocks[away], axis, ring(count, away))  15.4 us
    all_to_all x3, starting transfers between devices, exchange(): return lax.all_to_all(blocks, axis, split_axis=0, concat_axis=0, tiled=True)  15.3 us
    all_to_all x1, blocking collectives, exchange(): return lax.all_to_all(blocks, axis, split_axis=0, concat_axis=0, tiled=True)  14.8 us
    ppermute x13, starting transfers between devices, send_round(): lax.ppermute(blocks[away], axis, ring(count, away))  13.6 us
    pallas_call x1, Pallas kernels, middle(): pl.pallas_call(middle_kernel, grid=(D // CHUNK,), in_specs=[SCALARS, here...  11.6 us
    all_to_all x3, waiting for transfers between devices, exchange(): return lax.all_to_all(blocks, axis, split_axis=0, concat_axis=0, tiled=True)  6 us
    all_gather x1, blocking collectives, fast_device(): gathered = lax.all_gather(sum_shares(shares), 'dp')  5.95 us
    ppermute x1, waiting for transfers between devices, fast_device(): before = lax.ppermute(last, 'seq', up)  4.92 us
  transfers between devices with their start and end apart: 18, of which 10 were waited for; matrix products, arithmetic and copies ran while one was open for 1% of the time, Pallas kernels for 13%

profile of v2, /device:TPU:0, one launch (start us, length us, event | category | flops | bytes accessed | tf_op | source)
XLA Modules:
  0.0 109.0 jit_solution(9498560840412120668)
XLA Ops:
  0.6 0.0 copy-start
  0.7 2.2 %pack_heads.1 = bf16[8,288,128]{2,1,0:T(8,128)(2,1)} custom-call(bf16[128,768]{1,0:T(8,128)(2,1)} %bitcast.24, bf16[128,768]{1,0:T(8,128)(2,1)} %bitcast.25, bf16[128,768]{1,0:T(8,128)(2,1)} %bitcast.26), custom_call_target="tpu_custom_call" | custom-call | tf_op jit(solution)/shard_map/pack_heads/pallas_call | solution.py:236
  2.8 7.3 %all-to-all-start = ((bf16[8,288,128]{2,1,0:T(8,128)(2,1)}), bf16[8,288,128]{2,1,0:T(8,128)(2,1)S(1)}, u32[]{:S(2)}, u32[]{:S(2)}) async-start(bf16[8,288,128]{2,1,0:T(8,128)(2,1)} %pack_heads.1), calls=%async_computation | async-start | bytes 1179648 | tf_op jit(solution)/shard_map/all_to_all | solution.py:688
  10.1 0.8 slice_bitcast_fusion.2
  11.0 3.9 %collective-permute-start = (bf16[48,1536]{1,0:T(8,128)(2,1)S(1)}, bf16[48,1536]{1,0:T(8,128)(2,1)S(1)}, u32[]{:S(2)}, u32[]{:S(2)}) collective-permute-start(bf16[48,1536]{1,0:T(8,128)(2,1)S(1)} %pad_maximum_fusion), channel_id=1, source_target_pairs={{0,4},{4,8},{8,12},{12,16},{16,20},{20,24},{24,28},{1,5},{5,9},{9,... | collective-permute-start | bytes 442376 | tf_op jit(solution)/shard_map/ppermute | solution.py:707
  14.9 1.3 %collective-permute-start.1 = (bf16[48,1536]{1,0:T(8,128)(2,1)S(1)}, bf16[48,1536]{1,0:T(8,128)(2,1)S(1)}, u32[]{:S(2)}, u32[]{:S(2)}) collective-permute-start(bf16[48,1536]{1,0:T(8,128)(2,1)S(1)} %pad_maximum_fusion.1), channel_id=1, source_target_pairs={{4,0},{8,4},{12,8},{16,12},{20,16},{24,20},{28,24},{5,1},{9,5},{13... | collective-permute-start | bytes 442376 | tf_op jit(solution)/shard_map/ppermute | solution.py:708
  16.9 0.1 pad_add_fusion.info_ref
  17.0 4.9 %collective-permute-done.before_ref = bf16[48,1536]{1,0:T(8,128)(2,1)S(1)} collective-permute-done((bf16[48,1536]{1,0:T(8,128)(2,1)S(1)}, bf16[48,1536]{1,0:T(8,128)(2,1)S(1)}, u32[]{:S(2)}, u32[]{:S(2)}) %collective-permute-start) | collective-permute-done | bytes 147488 | tf_op jit(solution)/shard_map/ppermute | solution.py:707
  21.9 0.9 collective-permute-done.1.after_ref
  22.9 4.6 %all-to-all-done.x_ref = bf16[8,288,128]{2,1,0:T(8,128)(2,1)S(1)} async-done(((bf16[8,288,128]{2,1,0:T(8,128)(2,1)}), bf16[8,288,128]{2,1,0:T(8,128)(2,1)S(1)}, u32[]{:S(2)}, u32[]{:S(2)}) %all-to-all-start) | async-done | bytes 589856 | tf_op jit(solution)/shard_map/all_to_all | solution.py:688
  27.5 4.0 %forward_heads.1 = (bf16[8,144,128]{2,1,0:T(8,128)(2,1)S(1)}, f32[1,1024]{1,0:T(1,128)S(1)}) custom-call(s32[4]{0:T(128)S(1)} %pad_add_fusion.info_ref, bf16[8,288,128]{2,1,0:T(8,128)(2,1)S(1)} %all-to-all-done.x_ref), custom_call_target="tpu_custom_call" | custom-call | tf_op jit(solution)/shard_map/forward_heads/pallas_call | solution.py:304
  31.5 14.8 %all_to_all.20.att_ref.refs_4_ = bf16[8,144,128]{2,1,0:T(8,128)(2,1)S(1)} all-to-all(bf16[8,144,128]{2,1,0:T(8,128)(2,1)S(1)} %get-tuple-element.57.head_ref), channel_id=1, replica_groups=mesh['seq'=8,'dp'=4] {'seq'}, dimensions={0} | all-to-all | bytes 589824 | tf_op jit(solution)/shard_map/all_to_all | solution.py:688
  46.3 0.1 collective-permute-start.4
  46.4 1.6 %collective-permute-start.3 = (bf16[8,96,128]{2,1,0:T(8,128)(2,1)S(1)}, bf16[8,96,128]{2,1,0:T(8,128)(2,1)S(1)}, u32[]{:S(2)}, u32[]{:S(2)}) collective-permute-start(bf16[8,96,128]{2,1,0:T(8,128)(2,1)S(1)} %slice.20), channel_id=1, source_target_pairs={{0,2},{1,3},{2,0},{3,1},{4,6},{5,7},{6,4},{7,5},{8,10},{9,11},{10,... | collective-permute-start | bytes 589832 | tf_op jit(solution)/shard_map/ppermute | solution.py:683
  47.9 0.2 collective-permute-start.2
  48.1 11.6 %middle.1 = (bf16[128,1536]{1,0:T(8,128)(2,1)}, bf16[128,1536]{1,0:T(8,128)(2,1)}, bf16[8,96,128]{2,1,0:T(8,128)(2,1)}, bf16[576,128]{1,0:T(8,128)(2,1)S(1)}, bf...) custom-call(s32[4]{0:T(128)S(1)} %pad_add_fusion.info_ref, ...), custom_call_target="tpu_custom_call" | custom-call | tf_op jit(solution)/shard_map/middle/pallas_call | solution.py:497
  59.7 0.0 collective-permute-done.3.refs_6_
  59.7 0.0 collective-permute-done.2.refs_5_
  59.8 3.4 %all-to-all-start.2 = ((bf16[8,96,128]{2,1,0:T(8,128)(2,1)}), bf16[8,96,128]{2,1,0:T(8,128)(2,1)S(1)}, u32[]{:S(2)}, u32[]{:S(2)}) async-start(bf16[8,96,128]{2,1,0:T(8,128)(2,1)} %get-tuple-element.68), calls=%async_computation.2 | async-start | bytes 393216 | tf_op jit(solution)/shard_map/all_to_all | solution.py:688
  63.2 0.5 collective-permute-start.5
  63.7 1.5 %collective-permute-start.6 = (bf16[576,128]{1,0:T(8,128)(2,1)S(1)}, bf16[576,128]{1,0:T(8,128)(2,1)S(1)}, u32[]{:S(2)}, u32[]{:S(2)}) collective-permute-start(bf16[576,128]{1,0:T(8,128)(2,1)S(1)} %get-tuple-element.71), channel_id=1, source_target_pairs={{0,2},{1,3},{2,0},{3,1},{4,6},{5,7},{6,4},{7,5},{8,10},{9,11},{10,... | collective-permute-start | bytes 442376 | tf_op jit(solution)/shard_map/ppermute | solution.py:683
  65.2 0.0 collective-permute-start.7
  65.2 3.1 %collective-permute-done.5.refs_1_ = bf16[576,128]{1,0:T(8,128)(2,1)S(1)} collective-permute-done((bf16[576,128]{1,0:T(8,128)(2,1)S(1)}, bf16[576,128]{1,0:T(8,128)(2,1)S(1)}, u32[]{:S(2)}, u32[]{:S(2)}) %collective-permute-start.5) | collective-permute-done | bytes 147488 | tf_op jit(solution)/shard_map/ppermute | solution.py:683
  68.3 2.1 %collective-permute-done.6.refs_2_ = bf16[576,128]{1,0:T(8,128)(2,1)S(1)} collective-permute-done((bf16[576,128]{1,0:T(8,128)(2,1)S(1)}, bf16[576,128]{1,0:T(8,128)(2,1)S(1)}, u32[]{:S(2)}, u32[]{:S(2)}) %collective-permute-start.6) | collective-permute-done | bytes 147488 | tf_op jit(solution)/shard_map/ppermute | solution.py:683
  70.4 0.2 collective-permute-done.7.refs_3_
  70.6 1.4 %all-to-all-done.2.grad_ref = bf16[8,96,128]{2,1,0:T(8,128)(2,1)S(1)} async-done(((bf16[8,96,128]{2,1,0:T(8,128)(2,1)}), bf16[8,96,128]{2,1,0:T(8,128)(2,1)S(1)}, u32[]{:S(2)}, u32[]{:S(2)}) %all-to-all-start.2) | async-done | bytes 196640 | tf_op jit(solution)/shard_map/all_to_all | solution.py:688
  72.0 1.6 %product.1 = bf16[8,312,128]{2,1,0:T(8,128)(2,1)} custom-call(bf16[576,128]{1,0:T(8,128)(2,1)S(1)} %get-tuple-element.73.refs_0_, bf16[576,128]{1,0:T(8,128)(2,1)S(1)} %collective-permute-done.5.refs_1_, bf16[576,128]{1,0:T(8,128)(2,1)S(1)} %collective-permute-done.6.refs_2_, bf16[576,128]{1,0:T(8,128)(2,1)S(1)} %collective-permute-done.7.refs_3_, ...), custom_call_target="tpu_custom_call" | custom-call | tf_op jit(solution)/shard_map/product/pallas_call | solution.py:593
  73.6 4.6 %all-to-all-start.3 = ((bf16[8,312,128]{2,1,0:T(8,128)(2,1)}), bf16[8,312,128]{2,1,0:T(8,128)(2,1)S(1)}, u32[]{:S(2)}, u32[]{:S(2)}) async-start(bf16[8,312,128]{2,1,0:T(8,128)(2,1)} %product.1), calls=%async_computation.3 | async-start | bytes 1277952 | tf_op jit(solution)/shard_map/all_to_all | solution.py:688
  78.2 2.6 %backward_heads.1 = (bf16[96,128]{1,0:T(8,128)(2,1)S(1)}, bf16[96,128]{1,0:T(8,128)(2,1)S(1)}, bf16[96,128]{1,0:T(8,128)(2,1)S(1)}, bf16[96,128]{1,0:T(8,128)(2,...) custom-call(s32[4]{0:T(128)S(1)} %pad_add_fusion.info_ref, ...), custom_call_target="tpu_custom_call" | custom-call | tf_op jit(solution)/shard_map/backward_heads/pallas_call | solution.py:345
  80.8 2.1 %collective-permute-start.8 = (bf16[96,128]{1,0:T(8,128)(2,1)S(1)}, bf16[96,128]{1,0:T(8,128)(2,1)S(1)}, u32[]{:S(2)}, u32[]{:S(2)}) collective-permute-start(bf16[96,128]{1,0:T(8,128)(2,1)S(1)} %get-tuple-element.85), channel_id=1, source_target_pairs={{0,4},{4,8},{8,12},{12,16},{16,20},{20,24},{24,28},{28,0},{1,5},{5... | collective-permute-start | bytes 73736 | tf_op jit(solution)/shard_map/ppermute | solution.py:683
  82.8 1.5 %collective-permute-start.9 = (bf16[96,128]{1,0:T(8,128)(2,1)S(1)}, bf16[96,128]{1,0:T(8,128)(2,1)S(1)}, u32[]{:S(2)}, u32[]{:S(2)}) collective-permute-start(bf16[96,128]{1,0:T(8,128)(2,1)S(1)} %get-tuple-element.86), channel_id=1, source_target_pairs={{0,8},{4,12},{8,16},{12,20},{16,24},{20,28},{24,0},{28,4},{1,9},{5... | collective-permute-start | bytes 73736 | tf_op jit(solution)/shard_map/ppermute | solution.py:683
  84.3 2.4 %collective-permute-start.10 = (bf16[96,128]{1,0:T(8,128)(2,1)S(1)}, bf16[96,128]{1,0:T(8,128)(2,1)S(1)}, u32[]{:S(2)}, u32[]{:S(2)}) collective-permute-start(bf16[96,128]{1,0:T(8,128)(2,1)S(1)} %get-tuple-element.87), channel_id=1, source_target_pairs={{0,12},{4,16},{8,20},{12,24},{16,28},{20,0},{24,4},{28,8},{1,13},{... | collective-permute-start | bytes 73736 | tf_op jit(solution)/shard_map/ppermute | solution.py:683
  86.7 1.5 %collective-permute-start.11 = (bf16[96,128]{1,0:T(8,128)(2,1)S(1)}, bf16[96,128]{1,0:T(8,128)(2,1)S(1)}, u32[]{:S(2)}, u32[]{:S(2)}) collective-permute-start(bf16[96,128]{1,0:T(8,128)(2,1)S(1)} %get-tuple-element.88), channel_id=1, source_target_pairs={{0,16},{4,20},{8,24},{12,28},{16,0},{20,4},{24,8},{28,12},{1,17},{... | collective-permute-start | bytes 73736 | tf_op jit(solution)/shard_map/ppermute | solution.py:683
  88.1 2.4 %collective-permute-start.12 = (bf16[96,128]{1,0:T(8,128)(2,1)S(1)}, bf16[96,128]{1,0:T(8,128)(2,1)S(1)}, u32[]{:S(2)}, u32[]{:S(2)}) collective-permute-start(bf16[96,128]{1,0:T(8,128)(2,1)S(1)} %get-tuple-element.89), channel_id=1, source_target_pairs={{0,20},{4,24},{8,28},{12,0},{16,4},{20,8},{24,12},{28,16},{1,21},{... | collective-permute-start | bytes 73736 | tf_op jit(solution)/shard_map/ppermute | solution.py:683
  90.5 4.8 %collective-permute-done.8.refs_1_ = bf16[96,128]{1,0:T(8,128)(2,1)S(1)} collective-permute-done((bf16[96,128]{1,0:T(8,128)(2,1)S(1)}, bf16[96,128]{1,0:T(8,128)(2,1)S(1)}, u32[]{:S(2)}, u32[]{:S(2)}) %collective-permute-start.8) | collective-permute-done | bytes 24608 | tf_op jit(solution)/shard_map/ppermute | solution.py:683
  95.3 0.0 collective-permute-start.13
  95.3 0.0 collective-permute-done.9.refs_2_
  95.3 0.0 collective-permute-start.14
  95.3 4.4 %collective-permute-done.10.refs_3_ = bf16[96,128]{1,0:T(8,128)(2,1)S(1)} collective-permute-done((bf16[96,128]{1,0:T(8,128)(2,1)S(1)}, bf16[96,128]{1,0:T(8,128)(2,1)S(1)}, u32[]{:S(2)}, u32[]{:S(2)}) %collective-permute-start.10) | collective-permute-done | bytes 24608 | tf_op jit(solution)/shard_map/ppermute | solution.py:683
  99.8 0.0 collective-permute-done.11.refs_4_
  99.8 0.0 collective-permute-done.12.refs_5_
  99.8 0.8 collective-permute-done.13.refs_6_
  100.5 0.0 collective-permute-done.14.refs_7_
  100.6 0.0 all-to-all-done.3.in_ref
  100.6 0.2 sum_shares.1
  100.7 5.9 %all-gather = bf16[1248,128]{1,0:T(8,128)(2,1)S(1)} all-gather(bf16[312,128]{1,0:T(8,128)(2,1)S(1)} %sum_shares.1), channel_id=2, replica_groups=mesh['seq'=8,'dp'=4] {'dp'}, dimensions={0}, use_global_device_ids=true | all-gather | bytes 399360 | tf_op jit(solution)/shard_map/all_gather | solution.py:740
  106.7 1.0 finish.1
  107.7 1.4 %unpack_heads.1 = bf16[128,768]{1,0:T(8,128)(2,1)} custom-call(s32[4]{0:T(128)S(1)} %pad_add_fusion.info_ref, bf16[96,128]{1,0:T(8,128)(2,1)S(1)} %get-tuple-element.92.refs_0_, bf16[96,128]{1,0:T(8,128)(2,1)S(1)} %collective-permute-done.8.refs_1_, bf16[96,128]{1,0:T(8,128)(2,1)S(1)} %collective-permute-done.9.refs_2_, ...), custom_call_target="tpu_custom_call" | custom-call | tf_op jit(solution)/shard_map/unpack_heads/pallas_call | solution.py:665
  (9 shorter events, 0.1 us)
Async XLA Ops:
  0.6 9.5 %copy-start = (bf16[1,128,1536]{2,1,0:T(8,128)(2,1)S(1)}, bf16[1,128,1536]{2,1,0:T(8,128)(2,1)}, u32[]{:S(2)}) copy-start(bf16[1,128,1536]{2,1,0:T(8,128)(2,1)} %param.9) | copy-start | bytes 1179652
  0.6 16.3 %copy-start.1 = (f32[1536]{0:T(1024)S(1)}, f32[1536]{0:T(1024)}, u32[]{:S(2)}) copy-start(f32[1536]{0:T(1024)} %param.16) | copy-start | bytes 18436
  2.8 24.6 %all-to-all-start = ((bf16[8,288,128]{2,1,0:T(8,128)(2,1)}), bf16[8,288,128]{2,1,0:T(8,128)(2,1)S(1)}, u32[]{:S(2)}, u32[]{:S(2)}) async-start(bf16[8,288,128]{2,1,0:T(8,128)(2,1)} %pack_heads.1), calls=%async_computation | async-start | bytes 1179648 | tf_op jit(solution)/shard_map/all_to_all | solution.py:688
  11.0 10.9 %collective-permute-start = (bf16[48,1536]{1,0:T(8,128)(2,1)S(1)}, bf16[48,1536]{1,0:T(8,128)(2,1)S(1)}, u32[]{:S(2)}, u32[]{:S(2)}) collective-permute-start(bf16[48,1536]{1,0:T(8,128)(2,1)S(1)} %pad_maximum_fusion), channel_id=1, source_target_pairs={{0,4},{4,8},{8,12},{12,16},{16,20},{20,24},{24,28},{1,5},{5,9},{9,... | collective-permute-start | bytes 442376 | tf_op jit(solution)/shard_map/ppermute | solution.py:707
  14.9 7.9 %collective-permute-start.1 = (bf16[48,1536]{1,0:T(8,128)(2,1)S(1)}, bf16[48,1536]{1,0:T(8,128)(2,1)S(1)}, u32[]{:S(2)}, u32[]{:S(2)}) collective-permute-start(bf16[48,1536]{1,0:T(8,128)(2,1)S(1)} %pad_maximum_fusion.1), channel_id=1, source_target_pairs={{4,0},{8,4},{12,8},{16,12},{20,16},{24,20},{28,24},{5,1},{9,5},{13... | collective-permute-start | bytes 442376 | tf_op jit(solution)/shard_map/ppermute | solution.py:708
  46.3 13.4 %collective-permute-start.4 = (bf16[8,96,128]{2,1,0:T(8,128)(2,1)S(1)}, bf16[8,96,128]{2,1,0:T(8,128)(2,1)S(1)}, u32[]{:S(2)}, u32[]{:S(2)}) collective-permute-start(bf16[8,96,128]{2,1,0:T(8,128)(2,1)S(1)} %slice.20), channel_id=1, source_target_pairs={{0,3},{1,0},{2,1},{3,2},{4,7},{5,4},{6,5},{7,6},{8,11},{9,8},{10,9... | collective-permute-start | bytes 589832 | tf_op jit(solution)/shard_map/ppermute | solution.py:683
  46.4 13.4 %collective-permute-start.3 = (bf16[8,96,128]{2,1,0:T(8,128)(2,1)S(1)}, bf16[8,96,128]{2,1,0:T(8,128)(2,1)S(1)}, u32[]{:S(2)}, u32[]{:S(2)}) collective-permute-start(bf16[8,96,128]{2,1,0:T(8,128)(2,1)S(1)} %slice.20), channel_id=1, source_target_pairs={{0,2},{1,3},{2,0},{3,1},{4,6},{5,7},{6,4},{7,5},{8,10},{9,11},{10,... | collective-permute-start | bytes 589832 | tf_op jit(solution)/shard_map/ppermute | solution.py:683
  47.9 11.8 %collective-permute-start.2 = (bf16[8,96,128]{2,1,0:T(8,128)(2,1)S(1)}, bf16[8,96,128]{2,1,0:T(8,128)(2,1)S(1)}, u32[]{:S(2)}, u32[]{:S(2)}) collective-permute-start(bf16[8,96,128]{2,1,0:T(8,128)(2,1)S(1)} %slice.20), channel_id=1, source_target_pairs={{0,1},{1,2},{2,3},{3,0},{4,5},{5,6},{6,7},{7,4},{8,9},{9,10},{10,1... | collective-permute-start | bytes 589832 | tf_op jit(solution)/shard_map/ppermute | solution.py:683
  59.8 12.2 %all-to-all-start.2 = ((bf16[8,96,128]{2,1,0:T(8,128)(2,1)}), bf16[8,96,128]{2,1,0:T(8,128)(2,1)S(1)}, u32[]{:S(2)}, u32[]{:S(2)}) async-start(bf16[8,96,128]{2,1,0:T(8,128)(2,1)} %get-tuple-element.68), calls=%async_computation.2 | async-start | bytes 393216 | tf_op jit(solution)/shard_map/all_to_all | solution.py:688
  63.2 5.1 %collective-permute-start.5 = (bf16[576,128]{1,0:T(8,128)(2,1)S(1)}, bf16[576,128]{1,0:T(8,128)(2,1)S(1)}, u32[]{:S(2)}, u32[]{:S(2)}) collective-permute-start(bf16[576,128]{1,0:T(8,128)(2,1)S(1)} %get-tuple-element.70), channel_id=1, source_target_pairs={{0,1},{1,2},{2,3},{3,0},{4,5},{5,6},{6,7},{7,4},{8,9},{9,10},{10,1... | collective-permute-start | bytes 442376 | tf_op jit(solution)/shard_map/ppermute | solution.py:683
  63.7 6.7 %collective-permute-start.6 = (bf16[576,128]{1,0:T(8,128)(2,1)S(1)}, bf16[576,128]{1,0:T(8,128)(2,1)S(1)}, u32[]{:S(2)}, u32[]{:S(2)}) collective-permute-start(bf16[576,128]{1,0:T(8,128)(2,1)S(1)} %get-tuple-element.71), channel_id=1, source_target_pairs={{0,2},{1,3},{2,0},{3,1},{4,6},{5,7},{6,4},{7,5},{8,10},{9,11},{10,... | collective-permute-start | bytes 442376 | tf_op jit(solution)/shard_map/ppermute | solution.py:683
  65.2 5.4 %collective-permute-start.7 = (bf16[576,128]{1,0:T(8,128)(2,1)S(1)}, bf16[576,128]{1,0:T(8,128)(2,1)S(1)}, u32[]{:S(2)}, u32[]{:S(2)}) collective-permute-start(bf16[576,128]{1,0:T(8,128)(2,1)S(1)} %get-tuple-element.72), channel_id=1, source_target_pairs={{0,3},{1,0},{2,1},{3,2},{4,7},{5,4},{6,5},{7,6},{8,11},{9,8},{10,9... | collective-permute-start | bytes 442376 | tf_op jit(solution)/shard_map/ppermute | solution.py:683
  73.6 26.9 %all-to-all-start.3 = ((bf16[8,312,128]{2,1,0:T(8,128)(2,1)}), bf16[8,312,128]{2,1,0:T(8,128)(2,1)S(1)}, u32[]{:S(2)}, u32[]{:S(2)}) async-start(bf16[8,312,128]{2,1,0:T(8,128)(2,1)} %product.1), calls=%async_computation.3 | async-start | bytes 1277952 | tf_op jit(solution)/shard_map/all_to_all | solution.py:688
  80.8 14.6 %collective-permute-start.8 = (bf16[96,128]{1,0:T(8,128)(2,1)S(1)}, bf16[96,128]{1,0:T(8,128)(2,1)S(1)}, u32[]{:S(2)}, u32[]{:S(2)}) collective-permute-start(bf16[96,128]{1,0:T(8,128)(2,1)S(1)} %get-tuple-element.85), channel_id=1, source_target_pairs={{0,4},{4,8},{8,12},{12,16},{16,20},{20,24},{24,28},{28,0},{1,5},{5... | collective-permute-start | bytes 73736 | tf_op jit(solution)/shard_map/ppermute | solution.py:683
  82.8 12.5 %collective-permute-start.9 = (bf16[96,128]{1,0:T(8,128)(2,1)S(1)}, bf16[96,128]{1,0:T(8,128)(2,1)S(1)}, u32[]{:S(2)}, u32[]{:S(2)}) collective-permute-start(bf16[96,128]{1,0:T(8,128)(2,1)S(1)} %get-tuple-element.86), channel_id=1, source_target_pairs={{0,8},{4,12},{8,16},{12,20},{16,24},{20,28},{24,0},{28,4},{1,9},{5... | collective-permute-start | bytes 73736 | tf_op jit(solution)/shard_map/ppermute | solution.py:683
  84.3 15.5 %collective-permute-start.10 = (bf16[96,128]{1,0:T(8,128)(2,1)S(1)}, bf16[96,128]{1,0:T(8,128)(2,1)S(1)}, u32[]{:S(2)}, u32[]{:S(2)}) collective-permute-start(bf16[96,128]{1,0:T(8,128)(2,1)S(1)} %get-tuple-element.87), channel_id=1, source_target_pairs={{0,12},{4,16},{8,20},{12,24},{16,28},{20,0},{24,4},{28,8},{1,13},{... | collective-permute-start | bytes 73736 | tf_op jit(solution)/shard_map/ppermute | solution.py:683
  86.7 13.1 %collective-permute-start.11 = (bf16[96,128]{1,0:T(8,128)(2,1)S(1)}, bf16[96,128]{1,0:T(8,128)(2,1)S(1)}, u32[]{:S(2)}, u32[]{:S(2)}) collective-permute-start(bf16[96,128]{1,0:T(8,128)(2,1)S(1)} %get-tuple-element.88), channel_id=1, source_target_pairs={{0,16},{4,20},{8,24},{12,28},{16,0},{20,4},{24,8},{28,12},{1,17},{... | collective-permute-start | bytes 73736 | tf_op jit(solution)/shard_map/ppermute | solution.py:683
  88.1 11.6 %collective-permute-start.12 = (bf16[96,128]{1,0:T(8,128)(2,1)S(1)}, bf16[96,128]{1,0:T(8,128)(2,1)S(1)}, u32[]{:S(2)}, u32[]{:S(2)}) collective-permute-start(bf16[96,128]{1,0:T(8,128)(2,1)S(1)} %get-tuple-element.89), channel_id=1, source_target_pairs={{0,20},{4,24},{8,28},{12,0},{16,4},{20,8},{24,12},{28,16},{1,21},{... | collective-permute-start | bytes 73736 | tf_op jit(solution)/shard_map/ppermute | solution.py:683
  95.3 5.2 %collective-permute-start.13 = (bf16[96,128]{1,0:T(8,128)(2,1)S(1)}, bf16[96,128]{1,0:T(8,128)(2,1)S(1)}, u32[]{:S(2)}, u32[]{:S(2)}) collective-permute-start(bf16[96,128]{1,0:T(8,128)(2,1)S(1)} %get-tuple-element.90), channel_id=1, source_target_pairs={{0,24},{4,28},{8,0},{12,4},{16,8},{20,12},{24,16},{28,20},{1,25},{... | collective-permute-start | bytes 73736 | tf_op jit(solution)/shard_map/ppermute | solution.py:683
  95.3 5.2 %collective-permute-start.14 = (bf16[96,128]{1,0:T(8,128)(2,1)S(1)}, bf16[96,128]{1,0:T(8,128)(2,1)S(1)}, u32[]{:S(2)}, u32[]{:S(2)}) collective-permute-start(bf16[96,128]{1,0:T(8,128)(2,1)S(1)} %get-tuple-element.91), channel_id=1, source_target_pairs={{0,28},{4,0},{8,4},{12,8},{16,12},{20,16},{24,20},{28,24},{1,29},{... | collective-permute-start | bytes 73736 | tf_op jit(solution)/shard_map/ppermute | solution.py:683

commit v3 on v2

--- a/solution.py
+++ b/solution.py
@@ -316,7 +316,7 @@
 
 
 def backward_kernel(info_ref, x_ref, grad_ref, head_ref, lse_ref, *rest):
-    outs, (keys_sc, values_sc, wide_sc, result_sc) = rest[:-4], rest[-4:]
+    keep_ref, give_ref, keys_sc, values_sc, wide_sc, result_sc = rest
     blocks, _, frames = x_ref.shape
     key_rows(x_ref, info_ref[1], keys_sc)
     side_by_side(x_ref, KEYS, wide_sc)
@@ -335,8 +335,10 @@
         result = jnp.dot(wide_sc[...], grad_score, preferred_element_type=F32) * SCORE_SCALE
         result_sc[first] = result[:, :frames].astype(BF16)
         result_sc[first + 1] = result[:, frames:].astype(BF16)
-    for away, out_ref in enumerate(outs):
-        out_ref[...] = result_sc[lax.rem(info_ref[3] + away, blocks)]
+    side = lax.rem(info_ref[3], 2)
+    for layer in range(blocks // 2):
+        keep_ref[layer] = result_sc[2 * layer + side]
+        give_ref[layer] = result_sc[2 * layer + 1 - side]
 
 
 def backward_heads(info, received, grads, heads, lse):
@@ -345,8 +347,8 @@
     return pl.pallas_call(
         backward_kernel,
         in_specs=[SCALARS] + here(4),
-        out_specs=here(blocks),
-        out_shape=[jax.ShapeDtypeStruct((HS, frames), BF16)] * blocks,
+        out_specs=here(2),
+        out_shape=[jax.ShapeDtypeStruct((blocks // 2, HS, frames), BF16)] * 2,
         scratch_shapes=[
             pltpu.VMEM((total, LANES), BF16),
             pltpu.VMEM((total, HS), BF16),
@@ -620,7 +622,29 @@
     )(near(shares))
 
 
-def finish_kernel(in_ref, proj_ref, tap_ref, bias_ref):
+def pair_kernel(info_ref, own_ref, other_ref, *outs):
+    count = len(outs)
+    layer = lax.div(info_ref[3], 2)
+    for away, out_ref in enumerate(outs):
+        target = lax.rem(layer + away, count)
+        out_ref[0] = own_ref[target]
+        out_ref[1] = other_ref[target]
+
+
+def pair_heads(info, own, other):
+    count, rows, frames = own.shape
+    return pl.pallas_call(
+        pair_kernel,
+        in_specs=[SCALARS] + here(2),
+        out_specs=here(count),
+        out_shape=[jax.ShapeDtypeStruct((2, rows, frames), BF16)] * count,
+        compiler_params=params(),
+        name="pair_heads",
+    )(info, own, near(other))
+
+
+def finish_kernel(info_ref, in_ref, *rest):
+    pairs, (proj_ref, tap_ref, bias_ref, query_ref, heads_sc) = rest[:-5], rest[-5:]
     owners, share_rows, _ = in_ref.shape
     rows = share_rows * 12 // 13
     piece = rows * LANES // HD
@@ -634,53 +658,44 @@
     turned = jnp.concatenate(columns, axis=0).T
     tap_ref[...] = turned[:KW]
     bias_ref[...] = turned[KW : KW + 1]
-
-
-def finish(gathered):
+    count = len(pairs)
+    layer, side = lax.div(info_ref[3], 2), lax.rem(info_ref[3], 2)
+    for away, pair_ref in enumerate(pairs):
+        source = 2 * lax.rem(layer - away + count, count)
+        heads_sc[source + side] = pair_ref[0]
+        heads_sc[source + 1 - side] = pair_ref[1]
+    query_ref[...] = heads_sc[...].reshape(HD, heads_sc.shape[2]).T
+
+
+def finish(info, gathered, pairs):
     owners, share_rows, _ = gathered.shape
     width = owners * share_rows * 12 // 13 * LANES // HD
+    frames = pairs[0].shape[2]
     return pl.pallas_call(
         finish_kernel,
-        in_specs=[here()],
-        out_specs=here(3),
+        in_specs=[SCALARS] + here(1 + len(pairs)),
+        out_specs=here(4),
         out_shape=[
             jax.ShapeDtypeStruct((width, HD), F32),
             jax.ShapeDtypeStruct((KW, width), F32),
             jax.ShapeDtypeStruct((1, width), F32),
+            jax.ShapeDtypeStruct((frames, HD), BF16),
         ],
+        scratch_shapes=[pltpu.VMEM((H, HS, frames), BF16)],
         compiler_params=params(),
         name="finish",
-    )(near(gathered))
-
-
-def unpack_kernel(info_ref, *refs):
-    heads, out_ref, heads_sc = refs[:-2], refs[-2], refs[-1]
-    for away, head_ref in enumerate(heads):
-        heads_sc[lax.rem(info_ref[3] - away + H, H)] = head_ref[...]
-    out_ref[...] = heads_sc[...].reshape(HD, heads_sc.shape[2]).T
-
-
-def unpack_heads(info, heads):
-    frames = heads[0].shape[1]
-    return pl.pallas_call(
-        unpack_kernel,
-        in_specs=[SCALARS] + here(H),
-        out_specs=here(),
-        out_shape=jax.ShapeDtypeStruct((frames, HD), BF16),
-        scratch_shapes=[pltpu.VMEM((H, HS, frames), BF16)],
-        compiler_params=params(),
-        name="unpack_heads",
-    )(info, heads[0], *[near(head) for head in heads[1:]])
+    )(info, near(gathered), pairs[0], *[near(pair) for pair in pairs[1:]])
 
 
 def ring(count, away):
     return [(i, (i + away) % count) for i in range(count)]
 
 
-def send_round(blocks, axis):
-    count = len(blocks)
+def send_round(blocks, axis, stride=1):
+    count = len(blocks) * stride
     return [blocks[0]] + [
-        lax.ppermute(blocks[away], axis, ring(count, away)) for away in range(1, count)
+        lax.ppermute(blocks[away], axis, ring(count, away * stride))
+        for away in range(1, len(blocks))
     ]
 
 
@@ -734,11 +749,11 @@
     shares = product(moved, heads, returned, seq_count)
     shares, grads = lax.optimization_barrier((shares, grads))
     shares = exchange(shares, "seq")
-    query_parts = send_round(backward_heads(info, received, grads, sent, lse), "seq")
-    shares, query_parts = lax.optimization_barrier((shares, query_parts))
-    grad_query = unpack_heads(info, query_parts)
+    keep, give = backward_heads(info, received, grads, sent, lse)
+    other = lax.ppermute(give, "seq", [(i, i ^ 1) for i in range(seq_count)])
+    pairs = send_round(pair_heads(info, keep, other), "seq", 2)
     gathered = lax.all_gather(sum_shares(shares), "dp")
-    grad_proj, grad_kernel, grad_bias = finish(gathered)
+    grad_proj, grad_kernel, grad_bias, grad_query = finish(info, gathered, pairs)
     return (block_output[None], grad_input[None], grad_query[None], grad_proj, grad_kernel, grad_bias[0])
 
 

time: 110 us -> 107 us (0.973)
  waiting for transfers between devices: 27.2 us -> 24 us
  blocking collectives: 20.7 us -> 22.9 us
  starting transfers between devices: 34.1 us -> 32.8 us
    ppermute x13 -> x10, waiting for transfers between devices: 15.4 us -> 11.9 us  [the longest x1 6.48 us: fast_device(): other = lax.ppermute(give, 'seq', [(i, i ^ 1) for i in range(seq_count)])]
    all_gather x1, blocking collectives: 5.95 us -> 8.16 us  [fast_device(): gathered = lax.all_gather(sum_shares(shares), 'dp')]
    ppermute x13 -> x10, starting transfers between devices: 13.6 us -> 12.3 us  [the longest x9 10.2 us: send_round(): lax.ppermute(blocks[away], axis, ring(count, away * stride))]
  transfers between devices with their start and end apart: 18 -> 15, of which waited for: 10 -> 9; matrix products, arithmetic and copies ran while one was open for 1% -> 1% of each run, Pallas kernels for 13% -> 14%
where the time goes in v3:
time: 107 us
  starting transfers between devices  32.8 us (31%)
  Pallas kernels  24.5 us (23%)
  waiting for transfers between devices  24 us (22%)
  blocking collectives  22.9 us (21%)
  between operations  1.45 us (1%)
    all_to_all x3, starting transfers between devices, exchange(): return lax.all_to_all(blocks, axis, split_axis=0, concat_axis=0, tiled=True)  15.3 us
    all_to_all x1, blocking collectives, exchange(): return lax.all_to_all(blocks, axis, split_axis=0, concat_axis=0, tiled=True)  14.8 us
    pallas_call x1, Pallas kernels, middle(): pl.pallas_call(middle_kernel, grid=(D // CHUNK,), in_specs=[SCALARS, here...  11.6 us
    ppermute x9, starting transfers between devices, send_round(): lax.ppermute(blocks[away], axis, ring(count, away * stride))  10.2 us
    all_gather x1, blocking collectives, fast_device(): gathered = lax.all_gather(sum_shares(shares), 'dp')  8.16 us
    ppermute x1, waiting for transfers between devices, fast_device(): other = lax.ppermute(give, 'seq', [(i, i ^ 1) for i in range(seq_count)])  6.48 us
    all_to_all x3, waiting for transfers between devices, exchange(): return lax.all_to_all(blocks, axis, split_axis=0, concat_axis=0, tiled=True)  6.24 us
    ppermute x9, waiting for transfers between devices, send_round(): lax.ppermute(blocks[away], axis, ring(count, away * stride))  5.37 us
  transfers between devices with their start and end apart: 15, of which 9 were waited for; matrix products, arithmetic and copies ran while one was open for 1% of the time, Pallas kernels for 14%

profile of v3, /device:TPU:0, one launch (start us, length us, event | category | flops | bytes accessed | tf_op | source)
XLA Modules:
  0.0 106.5 jit_solution(2826430232584715515)
XLA Ops:
  0.6 0.0 copy-start
  0.6 0.0 copy-start.1
  0.7 2.2 %pack_heads.1 = bf16[8,288,128]{2,1,0:T(8,128)(2,1)} custom-call(bf16[128,768]{1,0:T(8,128)(2,1)} %bitcast.24, bf16[128,768]{1,0:T(8,128)(2,1)} %bitcast.25, bf16[128,768]{1,0:T(8,128)(2,1)} %bitcast.26), custom_call_target="tpu_custom_call" | custom-call | tf_op jit(solution)/shard_map/pack_heads/pallas_call | solution.py:236
  2.8 7.3 %all-to-all-start = ((bf16[8,288,128]{2,1,0:T(8,128)(2,1)}), bf16[8,288,128]{2,1,0:T(8,128)(2,1)S(1)}, u32[]{:S(2)}, u32[]{:S(2)}) async-start(bf16[8,288,128]{2,1,0:T(8,128)(2,1)} %pack_heads.1), calls=%async_computation | async-start | bytes 1179648 | tf_op jit(solution)/shard_map/all_to_all | solution.py:703
  10.1 0.0 copy-done
  10.1 0.8 slice_bitcast_fusion.2
  11.0 3.9 %collective-permute-start = (bf16[48,1536]{1,0:T(8,128)(2,1)S(1)}, bf16[48,1536]{1,0:T(8,128)(2,1)S(1)}, u32[]{:S(2)}, u32[]{:S(2)}) collective-permute-start(bf16[48,1536]{1,0:T(8,128)(2,1)S(1)} %pad_maximum_fusion), channel_id=1, source_target_pairs={{0,4},{4,8},{8,12},{12,16},{16,20},{20,24},{24,28},{1,5},{5,9},{9,... | collective-permute-start | bytes 442376 | tf_op jit(solution)/shard_map/ppermute | solution.py:722
  14.9 1.3 %collective-permute-start.1 = (bf16[48,1536]{1,0:T(8,128)(2,1)S(1)}, bf16[48,1536]{1,0:T(8,128)(2,1)S(1)}, u32[]{:S(2)}, u32[]{:S(2)}) collective-permute-start(bf16[48,1536]{1,0:T(8,128)(2,1)S(1)} %pad_maximum_fusion.1), channel_id=1, source_target_pairs={{4,0},{8,4},{12,8},{16,12},{20,16},{24,20},{28,24},{5,1},{9,5},{13... | collective-permute-start | bytes 442376 | tf_op jit(solution)/shard_map/ppermute | solution.py:723
  16.9 0.0 copy-done.1
  16.9 0.1 pad_add_fusion.info_ref
  17.0 4.9 %collective-permute-done.before_ref = bf16[48,1536]{1,0:T(8,128)(2,1)S(1)} collective-permute-done((bf16[48,1536]{1,0:T(8,128)(2,1)S(1)}, bf16[48,1536]{1,0:T(8,128)(2,1)S(1)}, u32[]{:S(2)}, u32[]{:S(2)}) %collective-permute-start) | collective-permute-done | bytes 147488 | tf_op jit(solution)/shard_map/ppermute | solution.py:722
  21.9 0.9 collective-permute-done.1.after_ref
  22.9 4.6 %all-to-all-done.x_ref = bf16[8,288,128]{2,1,0:T(8,128)(2,1)S(1)} async-done(((bf16[8,288,128]{2,1,0:T(8,128)(2,1)}), bf16[8,288,128]{2,1,0:T(8,128)(2,1)S(1)}, u32[]{:S(2)}, u32[]{:S(2)}) %all-to-all-start) | async-done | bytes 589856 | tf_op jit(solution)/shard_map/all_to_all | solution.py:703
  27.5 4.0 %forward_heads.1 = (bf16[8,144,128]{2,1,0:T(8,128)(2,1)S(1)}, f32[1,1024]{1,0:T(1,128)S(1)}) custom-call(s32[4]{0:T(128)S(1)} %pad_add_fusion.info_ref, bf16[8,288,128]{2,1,0:T(8,128)(2,1)S(1)} %all-to-all-done.x_ref), custom_call_target="tpu_custom_call" | custom-call | tf_op jit(solution)/shard_map/forward_heads/pallas_call | solution.py:304
  31.5 14.8 %all_to_all.20.att_ref.refs_4_ = bf16[8,144,128]{2,1,0:T(8,128)(2,1)S(1)} all-to-all(bf16[8,144,128]{2,1,0:T(8,128)(2,1)S(1)} %get-tuple-element.47.head_ref), channel_id=1, replica_groups=mesh['seq'=8,'dp'=4] {'seq'}, dimensions={0} | all-to-all | bytes 589824 | tf_op jit(solution)/shard_map/all_to_all | solution.py:703
  46.3 0.1 collective-permute-start.4
  46.4 1.6 %collective-permute-start.3 = (bf16[8,96,128]{2,1,0:T(8,128)(2,1)S(1)}, bf16[8,96,128]{2,1,0:T(8,128)(2,1)S(1)}, u32[]{:S(2)}, u32[]{:S(2)}) collective-permute-start(bf16[8,96,128]{2,1,0:T(8,128)(2,1)S(1)} %slice.20), channel_id=1, source_target_pairs={{0,2},{1,3},{2,0},{3,1},{4,6},{5,7},{6,4},{7,5},{8,10},{9,11},{10,... | collective-permute-start | bytes 589832 | tf_op jit(solution)/shard_map/ppermute | solution.py:697
  47.9 0.2 collective-permute-start.2
  48.1 11.6 %middle.1 = (bf16[128,1536]{1,0:T(8,128)(2,1)}, bf16[128,1536]{1,0:T(8,128)(2,1)}, bf16[8,96,128]{2,1,0:T(8,128)(2,1)}, bf16[576,128]{1,0:T(8,128)(2,1)S(1)}, bf...) custom-call(s32[4]{0:T(128)S(1)} %pad_add_fusion.info_ref, ...), custom_call_target="tpu_custom_call" | custom-call | tf_op jit(solution)/shard_map/middle/pallas_call | solution.py:499
  59.7 0.0 collective-permute-done.4.refs_7_
  59.7 0.0 collective-permute-done.3.refs_6_
  59.7 0.0 collective-permute-done.2.refs_5_
  59.8 3.4 %all-to-all-start.2 = ((bf16[8,96,128]{2,1,0:T(8,128)(2,1)}), bf16[8,96,128]{2,1,0:T(8,128)(2,1)S(1)}, u32[]{:S(2)}, u32[]{:S(2)}) async-start(bf16[8,96,128]{2,1,0:T(8,128)(2,1)} %get-tuple-element.58), calls=%async_computation.2 | async-start | bytes 393216 | tf_op jit(solution)/shard_map/all_to_all | solution.py:703
  63.2 0.5 collective-permute-start.5
  63.7 1.5 %collective-permute-start.6 = (bf16[576,128]{1,0:T(8,128)(2,1)S(1)}, bf16[576,128]{1,0:T(8,128)(2,1)S(1)}, u32[]{:S(2)}, u32[]{:S(2)}) collective-permute-start(bf16[576,128]{1,0:T(8,128)(2,1)S(1)} %get-tuple-element.61), channel_id=1, source_target_pairs={{0,2},{1,3},{2,0},{3,1},{4,6},{5,7},{6,4},{7,5},{8,10},{9,11},{10,... | collective-permute-start | bytes 442376 | tf_op jit(solution)/shard_map/ppermute | solution.py:697
  65.2 0.0 collective-permute-start.7
  65.2 3.1 %collective-permute-done.5.refs_1_ = bf16[576,128]{1,0:T(8,128)(2,1)S(1)} collective-permute-done((bf16[576,128]{1,0:T(8,128)(2,1)S(1)}, bf16[576,128]{1,0:T(8,128)(2,1)S(1)}, u32[]{:S(2)}, u32[]{:S(2)}) %collective-permute-start.5) | collective-permute-done | bytes 147488 | tf_op jit(solution)/shard_map/ppermute | solution.py:697
  68.3 2.1 %collective-permute-done.6.refs_2_ = bf16[576,128]{1,0:T(8,128)(2,1)S(1)} collective-permute-done((bf16[576,128]{1,0:T(8,128)(2,1)S(1)}, bf16[576,128]{1,0:T(8,128)(2,1)S(1)}, u32[]{:S(2)}, u32[]{:S(2)}) %collective-permute-start.6) | collective-permute-done | bytes 147488 | tf_op jit(solution)/shard_map/ppermute | solution.py:697
  70.4 0.2 collective-permute-done.7.refs_3_
  70.6 1.4 %all-to-all-done.2.grad_ref = bf16[8,96,128]{2,1,0:T(8,128)(2,1)S(1)} async-done(((bf16[8,96,128]{2,1,0:T(8,128)(2,1)}), bf16[8,96,128]{2,1,0:T(8,128)(2,1)S(1)}, u32[]{:S(2)}, u32[]{:S(2)}) %all-to-all-start.2) | async-done | bytes 196640 | tf_op jit(solution)/shard_map/all_to_all | solution.py:703
  72.0 1.6 %product.1 = bf16[8,312,128]{2,1,0:T(8,128)(2,1)} custom-call(bf16[576,128]{1,0:T(8,128)(2,1)S(1)} %get-tuple-element.63.refs_0_, bf16[576,128]{1,0:T(8,128)(2,1)S(1)} %collective-permute-done.5.refs_1_, bf16[576,128]{1,0:T(8,128)(2,1)S(1)} %collective-permute-done.6.refs_2_, bf16[576,128]{1,0:T(8,128)(2,1)S(1)} %collective-permute-done.7.refs_3_, ...), custom_call_target="tpu_custom_call" | custom-call | tf_op jit(solution)/shard_map/product/pallas_call | solution.py:595
  73.6 4.6 %all-to-all-start.3 = ((bf16[8,312,128]{2,1,0:T(8,128)(2,1)}), bf16[8,312,128]{2,1,0:T(8,128)(2,1)S(1)}, u32[]{:S(2)}, u32[]{:S(2)}) async-start(bf16[8,312,128]{2,1,0:T(8,128)(2,1)} %product.1), calls=%async_computation.3 | async-start | bytes 1277952 | tf_op jit(solution)/shard_map/all_to_all | solution.py:703
  78.2 2.6 %backward_heads.1 = (bf16[4,96,128]{2,1,0:T(8,128)(2,1)S(1)}, bf16[4,96,128]{2,1,0:T(8,128)(2,1)S(1)}) custom-call(s32[4]{0:T(128)S(1)} %pad_add_fusion.info_ref, bf16[8,288,128]{2,1,0:T(8,128)(2,1)S(1)} %all-to-all-done.x_ref, bf16[8,96,128]{2,1,0:T(8,128)(2,1)S(1)} %all-to-all-done.2.grad_ref, bf16[8,144,128]{2,1,0:T(8,128)(2,1)S(1)} %get-tuple-element.47.head_ref, ...), custom_call_target="tpu_custom_call" | custom-call | tf_op jit(solution)/shard_map/backward_heads/pallas_call | solution.py:347
  80.8 2.1 %collective-permute-start.8 = (bf16[4,96,128]{2,1,0:T(8,128)(2,1)S(1)}, bf16[4,96,128]{2,1,0:T(8,128)(2,1)S(1)}, u32[]{:S(2)}, u32[]{:S(2)}) collective-permute-start(bf16[4,96,128]{2,1,0:T(8,128)(2,1)S(1)} %get-tuple-element.75), channel_id=1, source_target_pairs={{0,4},{4,0},{8,12},{12,8},{16,20},{20,16},{24,28},{28,24},{1,5},{5... | collective-permute-start | bytes 294920 | tf_op jit(solution)/shard_map/ppermute | solution.py:753
  82.9 6.5 %collective-permute-done.8.other_ref = bf16[4,96,128]{2,1,0:T(8,128)(2,1)S(1)} collective-permute-done((bf16[4,96,128]{2,1,0:T(8,128)(2,1)S(1)}, bf16[4,96,128]{2,1,0:T(8,128)(2,1)S(1)}, u32[]{:S(2)}, u32[]{:S(2)}) %collective-permute-start.8) | collective-permute-done | bytes 98336 | tf_op jit(solution)/shard_map/ppermute | solution.py:753
  89.4 0.6 pair_heads.1
  89.9 0.1 collective-permute-start.9
  90.0 6.2 %collective-permute-start.10 = (bf16[2,96,128]{2,1,0:T(8,128)(2,1)S(1)}, bf16[2,96,128]{2,1,0:T(8,128)(2,1)S(1)}, u32[]{:S(2)}, u32[]{:S(2)}) collective-permute-start(bf16[2,96,128]{2,1,0:T(8,128)(2,1)S(1)} %get-tuple-element.78), channel_id=1, source_target_pairs={{0,16},{4,20},{8,24},{12,28},{16,0},{20,4},{24,8},{28,12},{1,17},{... | collective-permute-start | bytes 147464 | tf_op jit(solution)/shard_map/ppermute | solution.py:697
  96.2 0.0 collective-permute-start.11
  96.2 0.2 all-to-all-done.3.in_ref
  96.5 0.2 sum_shares.1
  96.7 8.2 %all-gather = bf16[1248,128]{1,0:T(8,128)(2,1)S(1)} all-gather(bf16[312,128]{1,0:T(8,128)(2,1)S(1)} %sum_shares.1), channel_id=2, replica_groups=mesh['seq'=8,'dp'=4] {'dp'}, dimensions={0}, use_global_device_ids=true | all-gather | bytes 399360 | tf_op jit(solution)/shard_map/all_gather | solution.py:755
  104.8 0.0 collective-permute-done.9.rest_1_
  104.8 0.0 collective-permute-done.10.rest_2_
  104.8 0.0 collective-permute-done.11.rest_3_
  104.8 1.7 %finish.1 = (f32[192,768]{1,0:T(8,128)}, f32[31,192]{1,0:T(8,128)}, f32[1,192]{1,0:T(1,128)}, bf16[128,768]{1,0:T(8,128)(2,1)}) custom-call(s32[4]{0:T(128)S(1)} %pad_add_fusion.info_ref, bf16[4,312,128]{2,1,0:T(8,128)(2,1)S(1)} %bitcast.21, bf16[2,96,128]{2,1,0:T(8,128)(2,1)S(1)} %get-tuple-element.76.rest_0_, ...), custom_call_target="tpu_custom_call" | custom-call | tf_op jit(solution)/shard_map/finish/pallas_call | solution.py:674
  (5 shorter events, 0.1 us)
Async XLA Ops:
  0.6 9.5 %copy-start = (bf16[1,128,1536]{2,1,0:T(8,128)(2,1)S(1)}, bf16[1,128,1536]{2,1,0:T(8,128)(2,1)}, u32[]{:S(2)}) copy-start(bf16[1,128,1536]{2,1,0:T(8,128)(2,1)} %param.9) | copy-start | bytes 1179652
  0.6 16.3 %copy-start.1 = (f32[1536]{0:T(1024)S(1)}, f32[1536]{0:T(1024)}, u32[]{:S(2)}) copy-start(f32[1536]{0:T(1024)} %param.16) | copy-start | bytes 18436
  2.8 24.6 %all-to-all-start = ((bf16[8,288,128]{2,1,0:T(8,128)(2,1)}), bf16[8,288,128]{2,1,0:T(8,128)(2,1)S(1)}, u32[]{:S(2)}, u32[]{:S(2)}) async-start(bf16[8,288,128]{2,1,0:T(8,128)(2,1)} %pack_heads.1), calls=%async_computation | async-start | bytes 1179648 | tf_op jit(solution)/shard_map/all_to_all | solution.py:703
  11.0 10.9 %collective-permute-start = (bf16[48,1536]{1,0:T(8,128)(2,1)S(1)}, bf16[48,1536]{1,0:T(8,128)(2,1)S(1)}, u32[]{:S(2)}, u32[]{:S(2)}) collective-permute-start(bf16[48,1536]{1,0:T(8,128)(2,1)S(1)} %pad_maximum_fusion), channel_id=1, source_target_pairs={{0,4},{4,8},{8,12},{12,16},{16,20},{20,24},{24,28},{1,5},{5,9},{9,... | collective-permute-start | bytes 442376 | tf_op jit(solution)/shard_map/ppermute | solution.py:722
  14.9 7.9 %collective-permute-start.1 = (bf16[48,1536]{1,0:T(8,128)(2,1)S(1)}, bf16[48,1536]{1,0:T(8,128)(2,1)S(1)}, u32[]{:S(2)}, u32[]{:S(2)}) collective-permute-start(bf16[48,1536]{1,0:T(8,128)(2,1)S(1)} %pad_maximum_fusion.1), channel_id=1, source_target_pairs={{4,0},{8,4},{12,8},{16,12},{20,16},{24,20},{28,24},{5,1},{9,5},{13... | collective-permute-start | bytes 442376 | tf_op jit(solution)/shard_map/ppermute | solution.py:723
  46.3 13.4 %collective-permute-start.4 = (bf16[8,96,128]{2,1,0:T(8,128)(2,1)S(1)}, bf16[8,96,128]{2,1,0:T(8,128)(2,1)S(1)}, u32[]{:S(2)}, u32[]{:S(2)}) collective-permute-start(bf16[8,96,128]{2,1,0:T(8,128)(2,1)S(1)} %slice.20), channel_id=1, source_target_pairs={{0,3},{1,0},{2,1},{3,2},{4,7},{5,4},{6,5},{7,6},{8,11},{9,8},{10,9... | collective-permute-start | bytes 589832 | tf_op jit(solution)/shard_map/ppermute | solution.py:697
  46.4 13.4 %collective-permute-start.3 = (bf16[8,96,128]{2,1,0:T(8,128)(2,1)S(1)}, bf16[8,96,128]{2,1,0:T(8,128)(2,1)S(1)}, u32[]{:S(2)}, u32[]{:S(2)}) collective-permute-start(bf16[8,96,128]{2,1,0:T(8,128)(2,1)S(1)} %slice.20), channel_id=1, source_target_pairs={{0,2},{1,3},{2,0},{3,1},{4,6},{5,7},{6,4},{7,5},{8,10},{9,11},{10,... | collective-permute-start | bytes 589832 | tf_op jit(solution)/shard_map/ppermute | solution.py:697
  47.9 11.8 %collective-permute-start.2 = (bf16[8,96,128]{2,1,0:T(8,128)(2,1)S(1)}, bf16[8,96,128]{2,1,0:T(8,128)(2,1)S(1)}, u32[]{:S(2)}, u32[]{:S(2)}) collective-permute-start(bf16[8,96,128]{2,1,0:T(8,128)(2,1)S(1)} %slice.20), channel_id=1, source_target_pairs={{0,1},{1,2},{2,3},{3,0},{4,5},{5,6},{6,7},{7,4},{8,9},{9,10},{10,1... | collective-permute-start | bytes 589832 | tf_op jit(solution)/shard_map/ppermute | solution.py:697
  59.8 12.2 %all-to-all-start.2 = ((bf16[8,96,128]{2,1,0:T(8,128)(2,1)}), bf16[8,96,128]{2,1,0:T(8,128)(2,1)S(1)}, u32[]{:S(2)}, u32[]{:S(2)}) async-start(bf16[8,96,128]{2,1,0:T(8,128)(2,1)} %get-tuple-element.58), calls=%async_computation.2 | async-start | bytes 393216 | tf_op jit(solution)/shard_map/all_to_all | solution.py:703
  63.2 5.1 %collective-permute-start.5 = (bf16[576,128]{1,0:T(8,128)(2,1)S(1)}, bf16[576,128]{1,0:T(8,128)(2,1)S(1)}, u32[]{:S(2)}, u32[]{:S(2)}) collective-permute-start(bf16[576,128]{1,0:T(8,128)(2,1)S(1)} %get-tuple-element.60), channel_id=1, source_target_pairs={{0,1},{1,2},{2,3},{3,0},{4,5},{5,6},{6,7},{7,4},{8,9},{9,10},{10,1... | collective-permute-start | bytes 442376 | tf_op jit(solution)/shard_map/ppermute | solution.py:697
  63.7 6.7 %collective-permute-start.6 = (bf16[576,128]{1,0:T(8,128)(2,1)S(1)}, bf16[576,128]{1,0:T(8,128)(2,1)S(1)}, u32[]{:S(2)}, u32[]{:S(2)}) collective-permute-start(bf16[576,128]{1,0:T(8,128)(2,1)S(1)} %get-tuple-element.61), channel_id=1, source_target_pairs={{0,2},{1,3},{2,0},{3,1},{4,6},{5,7},{6,4},{7,5},{8,10},{9,11},{10,... | collective-permute-start | bytes 442376 | tf_op jit(solution)/shard_map/ppermute | solution.py:697
  65.2 5.4 %collective-permute-start.7 = (bf16[576,128]{1,0:T(8,128)(2,1)S(1)}, bf16[576,128]{1,0:T(8,128)(2,1)S(1)}, u32[]{:S(2)}, u32[]{:S(2)}) collective-permute-start(bf16[576,128]{1,0:T(8,128)(2,1)S(1)} %get-tuple-element.62), channel_id=1, source_target_pairs={{0,3},{1,0},{2,1},{3,2},{4,7},{5,4},{6,5},{7,6},{8,11},{9,8},{10,9... | collective-permute-start | bytes 442376 | tf_op jit(solution)/shard_map/ppermute | solution.py:697
  73.6 22.9 %all-to-all-start.3 = ((bf16[8,312,128]{2,1,0:T(8,128)(2,1)}), bf16[8,312,128]{2,1,0:T(8,128)(2,1)S(1)}, u32[]{:S(2)}, u32[]{:S(2)}) async-start(bf16[8,312,128]{2,1,0:T(8,128)(2,1)} %product.1), calls=%async_computation.3 | async-start | bytes 1277952 | tf_op jit(solution)/shard_map/all_to_all | solution.py:703
  80.8 8.6 %collective-permute-start.8 = (bf16[4,96,128]{2,1,0:T(8,128)(2,1)S(1)}, bf16[4,96,128]{2,1,0:T(8,128)(2,1)S(1)}, u32[]{:S(2)}, u32[]{:S(2)}) collective-permute-start(bf16[4,96,128]{2,1,0:T(8,128)(2,1)S(1)} %get-tuple-element.75), channel_id=1, source_target_pairs={{0,4},{4,0},{8,12},{12,8},{16,20},{20,16},{24,28},{28,24},{1,5},{5... | collective-permute-start | bytes 294920 | tf_op jit(solution)/shard_map/ppermute | solution.py:753
  89.9 14.9 %collective-permute-start.9 = (bf16[2,96,128]{2,1,0:T(8,128)(2,1)S(1)}, bf16[2,96,128]{2,1,0:T(8,128)(2,1)S(1)}, u32[]{:S(2)}, u32[]{:S(2)}) collective-permute-start(bf16[2,96,128]{2,1,0:T(8,128)(2,1)S(1)} %get-tuple-element.77), channel_id=1, source_target_pairs={{0,8},{4,12},{8,16},{12,20},{16,24},{20,28},{24,0},{28,4},{1,9},{5... | collective-permute-start | bytes 147464 | tf_op jit(solution)/shard_map/ppermute | solution.py:697
  90.0 14.8 %collective-permute-start.10 = (bf16[2,96,128]{2,1,0:T(8,128)(2,1)S(1)}, bf16[2,96,128]{2,1,0:T(8,128)(2,1)S(1)}, u32[]{:S(2)}, u32[]{:S(2)}) collective-permute-start(bf16[2,96,128]{2,1,0:T(8,128)(2,1)S(1)} %get-tuple-element.78), channel_id=1, source_target_pairs={{0,16},{4,20},{8,24},{12,28},{16,0},{20,4},{24,8},{28,12},{1,17},{... | collective-permute-start | bytes 147464 | tf_op jit(solution)/shard_map/ppermute | solution.py:697
  96.2 8.6 %collective-permute-start.11 = (bf16[2,96,128]{2,1,0:T(8,128)(2,1)S(1)}, bf16[2,96,128]{2,1,0:T(8,128)(2,1)S(1)}, u32[]{:S(2)}, u32[]{:S(2)}) collective-permute-start(bf16[2,96,128]{2,1,0:T(8,128)(2,1)S(1)} %get-tuple-element.79), channel_id=1, source_target_pairs={{0,24},{4,28},{8,0},{12,4},{16,8},{20,12},{24,16},{28,20},{1,25},{... | collective-permute-start | bytes 147464 | tf_op jit(solution)/shard_map/ppermute | solution.py:697

commit v4 on v3

--- a/solution.py
+++ b/solution.py
@@ -186,7 +186,7 @@
 TAP_ROWS = 32
 WIDE = 32
 SIDE = 16
-CHUNK = 384
+CHUNK = 768
 LANES = 128
 MASKED_SCORE = -1e30
 QUERIES, KEYS, VALUES = (slice(place * HS, (place + 1) * HS) for place in range(3))
@@ -267,19 +267,35 @@
         wide_sc[:, block * frames : (block + 1) * frames] = x_ref[block, rows]
 
 
-def forward_kernel(info_ref, x_ref, out_ref, lse_ref, keys_sc, values_sc):
+def forward_kernel(
+    info_ref, x_ref, out_ref, lse_ref, keys_sc, values_sc, scores_sc, weights_sc
+):
     blocks, _, frames = x_ref.shape
     key_rows(x_ref, info_ref[1], keys_sc)
     side_by_side(x_ref, VALUES, values_sc)
     for first in range(0, blocks, 2):
-        scores = jnp.dot(keys_sc[...], query_columns(x_ref, first), preferred_element_type=F32)
-        scores = scores * LOG2_SCALE
-        top = jnp.max(scores, axis=0, keepdims=True)
-        raised = jnp.exp2(scores - top)
-        total = jnp.sum(raised, axis=0, keepdims=True)
-        weights = (raised * (1.0 / total)).astype(BF16)
+        turn = first // 2 % 2
+        query = query_columns(x_ref, first)
+        wide = query.shape[1]
+        chunks = [slice(row, row + frames) for row in range(0, blocks * frames, frames)]
+        peak = None
+        for chunk in chunks:
+            part = jnp.dot(keys_sc[chunk, :], query, preferred_element_type=F32)
+            scores_sc[turn, chunk, :] = part
+            part = part.reshape(frames // 8, 8, wide).max(0)
+            peak = part if peak is None else jnp.maximum(peak, part)
+        top = jnp.max(peak, axis=0, keepdims=True) * LOG2_SCALE
+        total = jnp.zeros((8, wide), F32)
+        for chunk in chunks:
+            raised = jnp.exp2(scores_sc[turn, chunk, :] * LOG2_SCALE - top)
+            scores_sc[turn, chunk, :] = raised
+            total += raised.reshape(frames // 8, 8, wide).sum(0)
+        total = jnp.sum(total, axis=0, keepdims=True)
+        shrink = 1.0 / total
         lse_ref[:, first * frames : (first + 2) * frames] = top + jnp.log2(total)
-        mixed = jnp.dot(values_sc[...], weights, preferred_element_type=F32).astype(BF16)
+        for chunk in chunks:
+            weights_sc[turn, chunk, :] = (scores_sc[turn, chunk, :] * shrink).astype(BF16)
+        mixed = jnp.dot(values_sc[...], weights_sc[turn], preferred_element_type=F32).astype(BF16)
         out_ref[first, :HS, :] = mixed[:, :frames]
         out_ref[first + 1, :HS, :] = mixed[:, frames:]
 
@@ -309,7 +325,12 @@
             jax.ShapeDtypeStruct((blocks, HS + HS // 2, frames), BF16),
             jax.ShapeDtypeStruct((1, total), F32),
         ],
-        scratch_shapes=[pltpu.VMEM((total, LANES), BF16), pltpu.VMEM((HS, total), BF16)],
+        scratch_shapes=[
+            pltpu.VMEM((total, LANES), BF16),
+            pltpu.VMEM((HS, total), BF16),
+            pltpu.VMEM((2, total, 2 * frames), F32),
+            pltpu.VMEM((2, total, 2 * frames), BF16),
+        ],
         compiler_params=params(),
         name="forward_heads",
     )(info, near(received))
@@ -409,29 +430,26 @@
         att_sc[WIDE + frames :, :] = turned[WIDE : 2 * WIDE]
         grad_sc[...] = jnp.zeros_like(grad_sc)
 
-    projected = lax.dot_general(
-        att_sc[...], proj_ref[...], (((1,), (1,)), ((), ())), preferred_element_type=F32
-    )
-    chunk = pl.ds(pl.multiple_of(step * CHUNK, CHUNK), CHUNK)
-    wide_input = jnp.concatenate(
-        [before_ref[:WIDE, chunk], input_ref[...], after_ref[:WIDE, chunk]], axis=0
-    ).astype(F32)
-    mixed = (wide_input + projected).astype(BF16).astype(F32)
-    frame = first - WIDE + lax.broadcasted_iota(jnp.int32, (rows, CHUNK), 0)
+    frame = first - WIDE + lax.broadcasted_iota(jnp.int32, (rows, LANES), 0)
     valid = (frame >= 0) & (frame < length)
-    masked = jnp.where(valid, mixed, 0.0)
-    cot = jnp.concatenate(
-        [before_ref[WIDE:, chunk], cot_ref[...], after_ref[WIDE:, chunk]], axis=0
-    ).astype(F32)
     inner = slice(WIDE - SIDE, WIDE + SIDE + frames)
-    cot = jnp.where(valid[inner], cot, 0.0)
-    for tile in range(tiles):
-        masked_sc[tile] = masked[:, tile * LANES : (tile + 1) * LANES]
-
     own = slice(SIDE, SIDE + frames)
-    inside = valid[WIDE : WIDE + frames, :LANES]
+    inside = valid[WIDE : WIDE + frames]
     for tile in range(tiles):
         lanes = slice(tile * LANES, (tile + 1) * LANES)
+        place = pl.ds(pl.multiple_of(step * CHUNK + tile * LANES, LANES), LANES)
+        wide_input = jnp.concatenate(
+            [before_ref[:WIDE, place], input_ref[:, lanes], after_ref[:WIDE, place]], axis=0
+        ).astype(F32)
+        projected = lax.dot_general(
+            att_sc[...], proj_ref[lanes, :], (((1,), (1,)), ((), ())), preferred_element_type=F32
+        )
+        mixed = (wide_input + projected).astype(BF16).astype(F32)
+        masked_sc[tile] = jnp.where(valid, mixed, 0.0)
+        cot = jnp.concatenate(
+            [before_ref[WIDE:, place], cot_ref[:, lanes], after_ref[WIDE:, place]], axis=0
+        ).astype(F32)
+        cot = jnp.where(valid[inner], cot, 0.0)
         start = jnp.broadcast_to(bias_ref[:, lanes], (span, LANES))
         conv = shifted_sum(
             masked_sc, tile, span, lambda offset: tap_ref[offset - 1 : offset, lanes], start
@@ -439,7 +457,7 @@
         gate = lax.logistic(conv)
         center = masked_sc[tile, WIDE : WIDE + frames, :]
         block_out_ref[:, lanes] = jnp.where(inside, center + conv[own] * gate[own], 0.0).astype(BF16)
-        gated = cot[:, lanes] * gate * (1.0 + conv * (1.0 - gate))
+        gated = cot * gate * (1.0 + conv * (1.0 - gate))
         gate_sc[tile] = gated
         owned = gated[own]
         for low in range(8):
@@ -457,7 +475,7 @@
             lambda offset: tap_ref[KW - offset : KW - offset + 1, lanes],
             jnp.zeros((frames, LANES), F32),
         )
-        grad_in_ref[:, lanes] = (cot[own, lanes] + jnp.where(inside, back, 0.0)).astype(BF16)
+        grad_in_ref[:, lanes] = (cot[own] + jnp.where(inside, back, 0.0)).astype(BF16)
 
     grad_in = grad_in_ref[...]
     grad_sc[...] += jnp.dot(grad_in, proj_ref[...], preferred_element_type=F32)

time: 107 us -> 106 us (level)
  Pallas kernels: 24.5 us -> 23.2 us
where the time goes in v4:
time: 106 us; the launch traced here: 105 us
  starting transfers between devices  32.8 us (31%)
  waiting for transfers between devices  23.9 us (23%)
  Pallas kernels  23.2 us (22%)
  blocking collectives  22.9 us (22%)
  between operations  1.45 us (1%)
    all_to_all x3, starting transfers between devices, exchange(): return lax.all_to_all(blocks, axis, split_axis=0, concat_axis=0, tiled=True)  15.3 us
    all_to_all x1, blocking collectives, exchange(): return lax.all_to_all(blocks, axis, split_axis=0, concat_axis=0, tiled=True)  14.8 us
    pallas_call x1, Pallas kernels, middle(): pl.pallas_call(middle_kernel, grid=(D // CHUNK,), in_specs=[SCALARS, here...  11.1 us
    ppermute x9, starting transfers between devices, send_round(): lax.ppermute(blocks[away], axis, ring(count, away * stride))  10.2 us
    all_gather x1, blocking collectives, fast_device(): gathered = lax.all_gather(sum_shares(shares), 'dp')  8.16 us
    ppermute x1, waiting for transfers between devices, fast_device(): other = lax.ppermute(give, 'seq', [(i, i ^ 1) for i in range(seq_count)])  6.47 us
    all_to_all x3, waiting for transfers between devices, exchange(): return lax.all_to_all(blocks, axis, split_axis=0, concat_axis=0, tiled=True)  6.24 us
    ppermute x9, waiting for transfers between devices, send_round(): lax.ppermute(blocks[away], axis, ring(count, away * stride))  5.37 us
  transfers between devices with their start and end apart: 15, of which 9 were waited for; matrix products, arithmetic and copies ran while one was open for 1% of the time, Pallas kernels for 14%

profile of v4, /device:TPU:0, one launch (start us, length us, event | category | flops | bytes accessed | tf_op | source)
XLA Modules:
  0.0 105.2 jit_solution(2709724709328003893)
XLA Ops:
  0.6 0.0 copy-start
  0.6 0.0 copy-start.1
  0.7 2.2 %pack_heads.1 = bf16[8,288,128]{2,1,0:T(8,128)(2,1)} custom-call(bf16[128,768]{1,0:T(8,128)(2,1)} %bitcast.24, bf16[128,768]{1,0:T(8,128)(2,1)} %bitcast.25, bf16[128,768]{1,0:T(8,128)(2,1)} %bitcast.26), custom_call_target="tpu_custom_call" | custom-call | tf_op jit(solution)/shard_map/pack_heads/pallas_call | solution.py:236
  2.8 7.3 %all-to-all-start = ((bf16[8,288,128]{2,1,0:T(8,128)(2,1)}), bf16[8,288,128]{2,1,0:T(8,128)(2,1)S(1)}, u32[]{:S(2)}, u32[]{:S(2)}) async-start(bf16[8,288,128]{2,1,0:T(8,128)(2,1)} %pack_heads.1), calls=%async_computation | async-start | bytes 1179648 | tf_op jit(solution)/shard_map/all_to_all | solution.py:721
  10.1 0.0 copy-done
  10.1 0.8 slice_bitcast_fusion.2
  11.0 3.9 %collective-permute-start = (bf16[48,1536]{1,0:T(8,128)(2,1)S(1)}, bf16[48,1536]{1,0:T(8,128)(2,1)S(1)}, u32[]{:S(2)}, u32[]{:S(2)}) collective-permute-start(bf16[48,1536]{1,0:T(8,128)(2,1)S(1)} %pad_maximum_fusion), channel_id=1, source_target_pairs={{0,4},{4,8},{8,12},{12,16},{16,20},{20,24},{24,28},{1,5},{5,9},{9,... | collective-permute-start | bytes 442376 | tf_op jit(solution)/shard_map/ppermute | solution.py:740
  14.9 1.3 %collective-permute-start.1 = (bf16[48,1536]{1,0:T(8,128)(2,1)S(1)}, bf16[48,1536]{1,0:T(8,128)(2,1)S(1)}, u32[]{:S(2)}, u32[]{:S(2)}) collective-permute-start(bf16[48,1536]{1,0:T(8,128)(2,1)S(1)} %pad_maximum_fusion.1), channel_id=1, source_target_pairs={{4,0},{8,4},{12,8},{16,12},{20,16},{24,20},{28,24},{5,1},{9,5},{13... | collective-permute-start | bytes 442376 | tf_op jit(solution)/shard_map/ppermute | solution.py:741
  16.9 0.0 copy-done.1
  16.9 0.1 pad_add_fusion.info_ref
  17.0 4.9 %collective-permute-done.before_ref = bf16[48,1536]{1,0:T(8,128)(2,1)S(1)} collective-permute-done((bf16[48,1536]{1,0:T(8,128)(2,1)S(1)}, bf16[48,1536]{1,0:T(8,128)(2,1)S(1)}, u32[]{:S(2)}, u32[]{:S(2)}) %collective-permute-start) | collective-permute-done | bytes 147488 | tf_op jit(solution)/shard_map/ppermute | solution.py:740
  21.9 0.9 collective-permute-done.1.after_ref
  22.9 4.6 %all-to-all-done.x_ref = bf16[8,288,128]{2,1,0:T(8,128)(2,1)S(1)} async-done(((bf16[8,288,128]{2,1,0:T(8,128)(2,1)}), bf16[8,288,128]{2,1,0:T(8,128)(2,1)S(1)}, u32[]{:S(2)}, u32[]{:S(2)}) %all-to-all-start) | async-done | bytes 589856 | tf_op jit(solution)/shard_map/all_to_all | solution.py:721
  27.5 3.3 %forward_heads.1 = (bf16[8,144,128]{2,1,0:T(8,128)(2,1)S(1)}, f32[1,1024]{1,0:T(1,128)S(1)}) custom-call(s32[4]{0:T(128)S(1)} %pad_add_fusion.info_ref, bf16[8,288,128]{2,1,0:T(8,128)(2,1)S(1)} %all-to-all-done.x_ref), custom_call_target="tpu_custom_call" | custom-call | tf_op jit(solution)/shard_map/forward_heads/pallas_call | solution.py:320
  30.8 14.8 %all_to_all.20.att_ref.refs_4_ = bf16[8,144,128]{2,1,0:T(8,128)(2,1)S(1)} all-to-all(bf16[8,144,128]{2,1,0:T(8,128)(2,1)S(1)} %get-tuple-element.47.head_ref), channel_id=1, replica_groups=mesh['seq'=8,'dp'=4] {'seq'}, dimensions={0} | all-to-all | bytes 589824 | tf_op jit(solution)/shard_map/all_to_all | solution.py:721
  45.5 0.1 collective-permute-start.4
  45.6 1.6 %collective-permute-start.3 = (bf16[8,96,128]{2,1,0:T(8,128)(2,1)S(1)}, bf16[8,96,128]{2,1,0:T(8,128)(2,1)S(1)}, u32[]{:S(2)}, u32[]{:S(2)}) collective-permute-start(bf16[8,96,128]{2,1,0:T(8,128)(2,1)S(1)} %slice.20), channel_id=1, source_target_pairs={{0,2},{1,3},{2,0},{3,1},{4,6},{5,7},{6,4},{7,5},{8,10},{9,11},{10,... | collective-permute-start | bytes 589832 | tf_op jit(solution)/shard_map/ppermute | solution.py:715
  47.2 0.2 collective-permute-start.2
  47.3 11.1 %middle.1 = (bf16[128,1536]{1,0:T(8,128)(2,1)}, bf16[128,1536]{1,0:T(8,128)(2,1)}, bf16[8,96,128]{2,1,0:T(8,128)(2,1)}, bf16[576,128]{1,0:T(8,128)(2,1)S(1)}, bf...) custom-call(s32[4]{0:T(128)S(1)} %pad_add_fusion.info_ref, ...), custom_call_target="tpu_custom_call" | custom-call | tf_op jit(solution)/shard_map/middle/pallas_call | solution.py:517
  58.4 0.0 collective-permute-done.4.refs_7_
  58.4 0.0 collective-permute-done.3.refs_6_
  58.5 0.0 collective-permute-done.2.refs_5_
  58.5 3.4 %all-to-all-start.2 = ((bf16[8,96,128]{2,1,0:T(8,128)(2,1)}), bf16[8,96,128]{2,1,0:T(8,128)(2,1)S(1)}, u32[]{:S(2)}, u32[]{:S(2)}) async-start(bf16[8,96,128]{2,1,0:T(8,128)(2,1)} %get-tuple-element.58), calls=%async_computation.2 | async-start | bytes 393216 | tf_op jit(solution)/shard_map/all_to_all | solution.py:721
  61.9 0.5 collective-permute-start.5
  62.4 1.5 %collective-permute-start.6 = (bf16[576,128]{1,0:T(8,128)(2,1)S(1)}, bf16[576,128]{1,0:T(8,128)(2,1)S(1)}, u32[]{:S(2)}, u32[]{:S(2)}) collective-permute-start(bf16[576,128]{1,0:T(8,128)(2,1)S(1)} %get-tuple-element.61), channel_id=1, source_target_pairs={{0,2},{1,3},{2,0},{3,1},{4,6},{5,7},{6,4},{7,5},{8,10},{9,11},{10,... | collective-permute-start | bytes 442376 | tf_op jit(solution)/shard_map/ppermute | solution.py:715
  63.9 0.0 collective-permute-start.7
  64.0 3.1 %collective-permute-done.5.refs_1_ = bf16[576,128]{1,0:T(8,128)(2,1)S(1)} collective-permute-done((bf16[576,128]{1,0:T(8,128)(2,1)S(1)}, bf16[576,128]{1,0:T(8,128)(2,1)S(1)}, u32[]{:S(2)}, u32[]{:S(2)}) %collective-permute-start.5) | collective-permute-done | bytes 147488 | tf_op jit(solution)/shard_map/ppermute | solution.py:715
  67.0 2.1 %collective-permute-done.6.refs_2_ = bf16[576,128]{1,0:T(8,128)(2,1)S(1)} collective-permute-done((bf16[576,128]{1,0:T(8,128)(2,1)S(1)}, bf16[576,128]{1,0:T(8,128)(2,1)S(1)}, u32[]{:S(2)}, u32[]{:S(2)}) %collective-permute-start.6) | collective-permute-done | bytes 147488 | tf_op jit(solution)/shard_map/ppermute | solution.py:715
  69.1 0.2 collective-permute-done.7.refs_3_
  69.3 1.4 %all-to-all-done.2.grad_ref = bf16[8,96,128]{2,1,0:T(8,128)(2,1)S(1)} async-done(((bf16[8,96,128]{2,1,0:T(8,128)(2,1)}), bf16[8,96,128]{2,1,0:T(8,128)(2,1)S(1)}, u32[]{:S(2)}, u32[]{:S(2)}) %all-to-all-start.2) | async-done | bytes 196640 | tf_op jit(solution)/shard_map/all_to_all | solution.py:721
  70.7 1.6 %product.1 = bf16[8,312,128]{2,1,0:T(8,128)(2,1)} custom-call(bf16[576,128]{1,0:T(8,128)(2,1)S(1)} %get-tuple-element.63.refs_0_, bf16[576,128]{1,0:T(8,128)(2,1)S(1)} %collective-permute-done.5.refs_1_, bf16[576,128]{1,0:T(8,128)(2,1)S(1)} %collective-permute-done.6.refs_2_, bf16[576,128]{1,0:T(8,128)(2,1)S(1)} %collective-permute-done.7.refs_3_, ...), custom_call_target="tpu_custom_call" | custom-call | tf_op jit(solution)/shard_map/product/pallas_call | solution.py:613
  72.3 4.6 %all-to-all-start.3 = ((bf16[8,312,128]{2,1,0:T(8,128)(2,1)}), bf16[8,312,128]{2,1,0:T(8,128)(2,1)S(1)}, u32[]{:S(2)}, u32[]{:S(2)}) async-start(bf16[8,312,128]{2,1,0:T(8,128)(2,1)} %product.1), calls=%async_computation.3 | async-start | bytes 1277952 | tf_op jit(solution)/shard_map/all_to_all | solution.py:721
  76.9 2.6 %backward_heads.1 = (bf16[4,96,128]{2,1,0:T(8,128)(2,1)S(1)}, bf16[4,96,128]{2,1,0:T(8,128)(2,1)S(1)}) custom-call(s32[4]{0:T(128)S(1)} %pad_add_fusion.info_ref, bf16[8,288,128]{2,1,0:T(8,128)(2,1)S(1)} %all-to-all-done.x_ref, bf16[8,96,128]{2,1,0:T(8,128)(2,1)S(1)} %all-to-all-done.2.grad_ref, bf16[8,144,128]{2,1,0:T(8,128)(2,1)S(1)} %get-tuple-element.47.head_ref, ...), custom_call_target="tpu_custom_call" | custom-call | tf_op jit(solution)/shard_map/backward_heads/pallas_call | solution.py:368
  79.5 2.1 %collective-permute-start.8 = (bf16[4,96,128]{2,1,0:T(8,128)(2,1)S(1)}, bf16[4,96,128]{2,1,0:T(8,128)(2,1)S(1)}, u32[]{:S(2)}, u32[]{:S(2)}) collective-permute-start(bf16[4,96,128]{2,1,0:T(8,128)(2,1)S(1)} %get-tuple-element.75), channel_id=1, source_target_pairs={{0,4},{4,0},{8,12},{12,8},{16,20},{20,16},{24,28},{28,24},{1,5},{5... | collective-permute-start | bytes 294920 | tf_op jit(solution)/shard_map/ppermute | solution.py:771
  81.6 6.5 %collective-permute-done.8.other_ref = bf16[4,96,128]{2,1,0:T(8,128)(2,1)S(1)} collective-permute-done((bf16[4,96,128]{2,1,0:T(8,128)(2,1)S(1)}, bf16[4,96,128]{2,1,0:T(8,128)(2,1)S(1)}, u32[]{:S(2)}, u32[]{:S(2)}) %collective-permute-start.8) | collective-permute-done | bytes 98336 | tf_op jit(solution)/shard_map/ppermute | solution.py:771
  88.1 0.6 pair_heads.1
  88.7 0.1 collective-permute-start.9
  88.7 6.2 %collective-permute-start.10 = (bf16[2,96,128]{2,1,0:T(8,128)(2,1)S(1)}, bf16[2,96,128]{2,1,0:T(8,128)(2,1)S(1)}, u32[]{:S(2)}, u32[]{:S(2)}) collective-permute-start(bf16[2,96,128]{2,1,0:T(8,128)(2,1)S(1)} %get-tuple-element.78), channel_id=1, source_target_pairs={{0,16},{4,20},{8,24},{12,28},{16,0},{20,4},{24,8},{28,12},{1,17},{... | collective-permute-start | bytes 147464 | tf_op jit(solution)/shard_map/ppermute | solution.py:715
  95.0 0.0 collective-permute-start.11
  95.0 0.2 all-to-all-done.3.in_ref
  95.2 0.2 sum_shares.1
  95.4 8.2 %all-gather = bf16[1248,128]{1,0:T(8,128)(2,1)S(1)} all-gather(bf16[312,128]{1,0:T(8,128)(2,1)S(1)} %sum_shares.1), channel_id=2, replica_groups=mesh['seq'=8,'dp'=4] {'dp'}, dimensions={0}, use_global_device_ids=true | all-gather | bytes 399360 | tf_op jit(solution)/shard_map/all_gather | solution.py:773
  103.5 0.0 collective-permute-done.9.rest_1_
  103.5 0.0 collective-permute-done.10.rest_2_
  103.5 0.0 collective-permute-done.11.rest_3_
  103.6 1.7 %finish.1 = (f32[192,768]{1,0:T(8,128)}, f32[31,192]{1,0:T(8,128)}, f32[1,192]{1,0:T(1,128)}, bf16[128,768]{1,0:T(8,128)(2,1)}) custom-call(s32[4]{0:T(128)S(1)} %pad_add_fusion.info_ref, bf16[4,312,128]{2,1,0:T(8,128)(2,1)S(1)} %bitcast.21, bf16[2,96,128]{2,1,0:T(8,128)(2,1)S(1)} %get-tuple-element.76.rest_0_, ...), custom_call_target="tpu_custom_call" | custom-call | tf_op jit(solution)/shard_map/finish/pallas_call | solution.py:692
  (5 shorter events, 0.1 us)
Async XLA Ops:
  0.6 9.5 %copy-start = (bf16[1,128,1536]{2,1,0:T(8,128)(2,1)S(1)}, bf16[1,128,1536]{2,1,0:T(8,128)(2,1)}, u32[]{:S(2)}) copy-start(bf16[1,128,1536]{2,1,0:T(8,128)(2,1)} %param.9) | copy-start | bytes 1179652
  0.6 16.3 %copy-start.1 = (f32[1536]{0:T(1024)S(1)}, f32[1536]{0:T(1024)}, u32[]{:S(2)}) copy-start(f32[1536]{0:T(1024)} %param.16) | copy-start | bytes 18436
  2.8 24.6 %all-to-all-start = ((bf16[8,288,128]{2,1,0:T(8,128)(2,1)}), bf16[8,288,128]{2,1,0:T(8,128)(2,1)S(1)}, u32[]{:S(2)}, u32[]{:S(2)}) async-start(bf16[8,288,128]{2,1,0:T(8,128)(2,1)} %pack_heads.1), calls=%async_computation | async-start | bytes 1179648 | tf_op jit(solution)/shard_map/all_to_all | solution.py:721
  11.0 10.9 %collective-permute-start = (bf16[48,1536]{1,0:T(8,128)(2,1)S(1)}, bf16[48,1536]{1,0:T(8,128)(2,1)S(1)}, u32[]{:S(2)}, u32[]{:S(2)}) collective-permute-start(bf16[48,1536]{1,0:T(8,128)(2,1)S(1)} %pad_maximum_fusion), channel_id=1, source_target_pairs={{0,4},{4,8},{8,12},{12,16},{16,20},{20,24},{24,28},{1,5},{5,9},{9,... | collective-permute-start | bytes 442376 | tf_op jit(solution)/shard_map/ppermute | solution.py:740
  14.9 7.9 %collective-permute-start.1 = (bf16[48,1536]{1,0:T(8,128)(2,1)S(1)}, bf16[48,1536]{1,0:T(8,128)(2,1)S(1)}, u32[]{:S(2)}, u32[]{:S(2)}) collective-permute-start(bf16[48,1536]{1,0:T(8,128)(2,1)S(1)} %pad_maximum_fusion.1), channel_id=1, source_target_pairs={{4,0},{8,4},{12,8},{16,12},{20,16},{24,20},{28,24},{5,1},{9,5},{13... | collective-permute-start | bytes 442376 | tf_op jit(solution)/shard_map/ppermute | solution.py:741
  45.5 12.9 %collective-permute-start.4 = (bf16[8,96,128]{2,1,0:T(8,128)(2,1)S(1)}, bf16[8,96,128]{2,1,0:T(8,128)(2,1)S(1)}, u32[]{:S(2)}, u32[]{:S(2)}) collective-permute-start(bf16[8,96,128]{2,1,0:T(8,128)(2,1)S(1)} %slice.20), channel_id=1, source_target_pairs={{0,3},{1,0},{2,1},{3,2},{4,7},{5,4},{6,5},{7,6},{8,11},{9,8},{10,9... | collective-permute-start | bytes 589832 | tf_op jit(solution)/shard_map/ppermute | solution.py:715
  45.6 12.8 %collective-permute-start.3 = (bf16[8,96,128]{2,1,0:T(8,128)(2,1)S(1)}, bf16[8,96,128]{2,1,0:T(8,128)(2,1)S(1)}, u32[]{:S(2)}, u32[]{:S(2)}) collective-permute-start(bf16[8,96,128]{2,1,0:T(8,128)(2,1)S(1)} %slice.20), channel_id=1, source_target_pairs={{0,2},{1,3},{2,0},{3,1},{4,6},{5,7},{6,4},{7,5},{8,10},{9,11},{10,... | collective-permute-start | bytes 589832 | tf_op jit(solution)/shard_map/ppermute | solution.py:715
  47.2 11.3 %collective-permute-start.2 = (bf16[8,96,128]{2,1,0:T(8,128)(2,1)S(1)}, bf16[8,96,128]{2,1,0:T(8,128)(2,1)S(1)}, u32[]{:S(2)}, u32[]{:S(2)}) collective-permute-start(bf16[8,96,128]{2,1,0:T(8,128)(2,1)S(1)} %slice.20), channel_id=1, source_target_pairs={{0,1},{1,2},{2,3},{3,0},{4,5},{5,6},{6,7},{7,4},{8,9},{9,10},{10,1... | collective-permute-start | bytes 589832 | tf_op jit(solution)/shard_map/ppermute | solution.py:715
  58.5 12.2 %all-to-all-start.2 = ((bf16[8,96,128]{2,1,0:T(8,128)(2,1)}), bf16[8,96,128]{2,1,0:T(8,128)(2,1)S(1)}, u32[]{:S(2)}, u32[]{:S(2)}) async-start(bf16[8,96,128]{2,1,0:T(8,128)(2,1)} %get-tuple-element.58), calls=%async_computation.2 | async-start | bytes 393216 | tf_op jit(solution)/shard_map/all_to_all | solution.py:721
  61.9 5.1 %collective-permute-start.5 = (bf16[576,128]{1,0:T(8,128)(2,1)S(1)}, bf16[576,128]{1,0:T(8,128)(2,1)S(1)}, u32[]{:S(2)}, u32[]{:S(2)}) collective-permute-start(bf16[576,128]{1,0:T(8,128)(2,1)S(1)} %get-tuple-element.60), channel_id=1, source_target_pairs={{0,1},{1,2},{2,3},{3,0},{4,5},{5,6},{6,7},{7,4},{8,9},{9,10},{10,1... | collective-permute-start | bytes 442376 | tf_op jit(solution)/shard_map/ppermute | solution.py:715
  62.4 6.7 %collective-permute-start.6 = (bf16[576,128]{1,0:T(8,128)(2,1)S(1)}, bf16[576,128]{1,0:T(8,128)(2,1)S(1)}, u32[]{:S(2)}, u32[]{:S(2)}) collective-permute-start(bf16[576,128]{1,0:T(8,128)(2,1)S(1)} %get-tuple-element.61), channel_id=1, source_target_pairs={{0,2},{1,3},{2,0},{3,1},{4,6},{5,7},{6,4},{7,5},{8,10},{9,11},{10,... | collective-permute-start | bytes 442376 | tf_op jit(solution)/shard_map/ppermute | solution.py:715
  63.9 5.4 %collective-permute-start.7 = (bf16[576,128]{1,0:T(8,128)(2,1)S(1)}, bf16[576,128]{1,0:T(8,128)(2,1)S(1)}, u32[]{:S(2)}, u32[]{:S(2)}) collective-permute-start(bf16[576,128]{1,0:T(8,128)(2,1)S(1)} %get-tuple-element.62), channel_id=1, source_target_pairs={{0,3},{1,0},{2,1},{3,2},{4,7},{5,4},{6,5},{7,6},{8,11},{9,8},{10,9... | collective-permute-start | bytes 442376 | tf_op jit(solution)/shard_map/ppermute | solution.py:715
  72.3 22.9 %all-to-all-start.3 = ((bf16[8,312,128]{2,1,0:T(8,128)(2,1)}), bf16[8,312,128]{2,1,0:T(8,128)(2,1)S(1)}, u32[]{:S(2)}, u32[]{:S(2)}) async-start(bf16[8,312,128]{2,1,0:T(8,128)(2,1)} %product.1), calls=%async_computation.3 | async-start | bytes 1277952 | tf_op jit(solution)/shard_map/all_to_all | solution.py:721
  79.5 8.6 %collective-permute-start.8 = (bf16[4,96,128]{2,1,0:T(8,128)(2,1)S(1)}, bf16[4,96,128]{2,1,0:T(8,128)(2,1)S(1)}, u32[]{:S(2)}, u32[]{:S(2)}) collective-permute-start(bf16[4,96,128]{2,1,0:T(8,128)(2,1)S(1)} %get-tuple-element.75), channel_id=1, source_target_pairs={{0,4},{4,0},{8,12},{12,8},{16,20},{20,16},{24,28},{28,24},{1,5},{5... | collective-permute-start | bytes 294920 | tf_op jit(solution)/shard_map/ppermute | solution.py:771
  88.7 14.9 %collective-permute-start.9 = (bf16[2,96,128]{2,1,0:T(8,128)(2,1)S(1)}, bf16[2,96,128]{2,1,0:T(8,128)(2,1)S(1)}, u32[]{:S(2)}, u32[]{:S(2)}) collective-permute-start(bf16[2,96,128]{2,1,0:T(8,128)(2,1)S(1)} %get-tuple-element.77), channel_id=1, source_target_pairs={{0,8},{4,12},{8,16},{12,20},{16,24},{20,28},{24,0},{28,4},{1,9},{5... | collective-permute-start | bytes 147464 | tf_op jit(solution)/shard_map/ppermute | solution.py:715
  88.7 14.8 %collective-permute-start.10 = (bf16[2,96,128]{2,1,0:T(8,128)(2,1)S(1)}, bf16[2,96,128]{2,1,0:T(8,128)(2,1)S(1)}, u32[]{:S(2)}, u32[]{:S(2)}) collective-permute-start(bf16[2,96,128]{2,1,0:T(8,128)(2,1)S(1)} %get-tuple-element.78), channel_id=1, source_target_pairs={{0,16},{4,20},{8,24},{12,28},{16,0},{20,4},{24,8},{28,12},{1,17},{... | collective-permute-start | bytes 147464 | tf_op jit(solution)/shard_map/ppermute | solution.py:715
  95.0 8.6 %collective-permute-start.11 = (bf16[2,96,128]{2,1,0:T(8,128)(2,1)S(1)}, bf16[2,96,128]{2,1,0:T(8,128)(2,1)S(1)}, u32[]{:S(2)}, u32[]{:S(2)}) collective-permute-start(bf16[2,96,128]{2,1,0:T(8,128)(2,1)S(1)} %get-tuple-element.79), channel_id=1, source_target_pairs={{0,24},{4,28},{8,0},{12,4},{16,8},{20,12},{24,16},{28,20},{1,25},{... | collective-permute-start | bytes 147464 | tf_op jit(solution)/shard_map/ppermute | solution.py:715

commit v5 on v4

--- a/solution.py
+++ b/solution.py
@@ -226,15 +226,18 @@
 
 
 def pack_kernel(q_ref, k_ref, v_ref, out_ref):
+    heads, _, frames = out_ref.shape
     for place, ref in enumerate((q_ref, k_ref, v_ref)):
-        frames = ref.shape[0]
-        out_ref[:, place * HS : (place + 1) * HS, :] = ref[...].T.reshape(H, HS, frames)
+        out_ref[:, place * HS : (place + 1) * HS, :] = ref[...].T.reshape(heads, HS, frames)
 
 
 def pack_heads(q, k, v):
     frames = q.shape[0]
     return pl.pallas_call(
         pack_kernel,
+        grid=(2,),
+        in_specs=[pl.BlockSpec((frames, HD // 2), lambda i: (0, i))] * 3,
+        out_specs=pl.BlockSpec((H // 2, 3 * HS, frames), lambda i: (i, 0, 0)),
         out_shape=jax.ShapeDtypeStruct((H, 3 * HS, frames), BF16),
         compiler_params=params(),
         name="pack_heads",

time: 106 us -> 106 us (level)
  no operation moved by 1% of the time
where the time goes in v5:
time: 106 us; the launch traced here: 105 us
  starting transfers between devices  32.8 us (31%)
  waiting for transfers between devices  23.9 us (23%)
  Pallas kernels  23.1 us (22%)
  blocking collectives  22.9 us (22%)
  between operations  1.45 us (1%)
    all_to_all x3, starting transfers between devices, exchange(): return lax.all_to_all(blocks, axis, split_axis=0, concat_axis=0, tiled=True)  15.3 us
    all_to_all x1, blocking collectives, exchange(): return lax.all_to_all(blocks, axis, split_axis=0, concat_axis=0, tiled=True)  14.8 us
    pallas_call x1, Pallas kernels, middle(): pl.pallas_call(middle_kernel, grid=(D // CHUNK,), in_specs=[SCALARS, here...  11.1 us
    ppermute x9, starting transfers between devices, send_round(): lax.ppermute(blocks[away], axis, ring(count, away * stride))  10.2 us
    all_gather x1, blocking collectives, fast_device(): gathered = lax.all_gather(sum_shares(shares), 'dp')  8.17 us
    ppermute x1, waiting for transfers between devices, fast_device(): other = lax.ppermute(give, 'seq', [(i, i ^ 1) for i in range(seq_count)])  6.47 us
    all_to_all x3, waiting for transfers between devices, exchange(): return lax.all_to_all(blocks, axis, split_axis=0, concat_axis=0, tiled=True)  6.24 us
    ppermute x9, waiting for transfers between devices, send_round(): lax.ppermute(blocks[away], axis, ring(count, away * stride))  5.37 us
  transfers between devices with their start and end apart: 15, of which 9 were waited for; matrix products, arithmetic and copies ran while one was open for 1% of the time, Pallas kernels for 14%

profile of v5, /device:TPU:0, one launch (start us, length us, event | category | flops | bytes accessed | tf_op | source)
XLA Modules:
  0.0 105.1 jit_solution(5957934006755242977)
XLA Ops:
  0.6 0.0 copy-start
  0.6 0.0 copy-start.1
  0.7 2.1 %pack_heads.1 = bf16[8,288,128]{2,1,0:T(8,128)(2,1)} custom-call(bf16[128,768]{1,0:T(8,128)(2,1)} %bitcast.24, bf16[128,768]{1,0:T(8,128)(2,1)} %bitcast.25, bf16[128,768]{1,0:T(8,128)(2,1)} %bitcast.26), custom_call_target="tpu_custom_call" | custom-call | tf_op jit(solution)/shard_map/pack_heads/pallas_call | solution.py:236
  2.7 7.3 %all-to-all-start = ((bf16[8,288,128]{2,1,0:T(8,128)(2,1)}), bf16[8,288,128]{2,1,0:T(8,128)(2,1)S(1)}, u32[]{:S(2)}, u32[]{:S(2)}) async-start(bf16[8,288,128]{2,1,0:T(8,128)(2,1)} %pack_heads.1), calls=%async_computation | async-start | bytes 1179648 | tf_op jit(solution)/shard_map/all_to_all | solution.py:724
  10.0 0.0 copy-done
  10.0 0.8 slice_bitcast_fusion.2
  10.9 3.9 %collective-permute-start = (bf16[48,1536]{1,0:T(8,128)(2,1)S(1)}, bf16[48,1536]{1,0:T(8,128)(2,1)S(1)}, u32[]{:S(2)}, u32[]{:S(2)}) collective-permute-start(bf16[48,1536]{1,0:T(8,128)(2,1)S(1)} %pad_maximum_fusion), channel_id=1, source_target_pairs={{0,4},{4,8},{8,12},{12,16},{16,20},{20,24},{24,28},{1,5},{5,9},{9,... | collective-permute-start | bytes 442376 | tf_op jit(solution)/shard_map/ppermute | solution.py:743
  14.8 1.3 %collective-permute-start.1 = (bf16[48,1536]{1,0:T(8,128)(2,1)S(1)}, bf16[48,1536]{1,0:T(8,128)(2,1)S(1)}, u32[]{:S(2)}, u32[]{:S(2)}) collective-permute-start(bf16[48,1536]{1,0:T(8,128)(2,1)S(1)} %pad_maximum_fusion.1), channel_id=1, source_target_pairs={{4,0},{8,4},{12,8},{16,12},{20,16},{24,20},{28,24},{5,1},{9,5},{13... | collective-permute-start | bytes 442376 | tf_op jit(solution)/shard_map/ppermute | solution.py:744
  16.8 0.0 copy-done.1
  16.8 0.1 pad_add_fusion.info_ref
  16.9 4.9 %collective-permute-done.before_ref = bf16[48,1536]{1,0:T(8,128)(2,1)S(1)} collective-permute-done((bf16[48,1536]{1,0:T(8,128)(2,1)S(1)}, bf16[48,1536]{1,0:T(8,128)(2,1)S(1)}, u32[]{:S(2)}, u32[]{:S(2)}) %collective-permute-start) | collective-permute-done | bytes 147488 | tf_op jit(solution)/shard_map/ppermute | solution.py:743
  21.8 0.9 collective-permute-done.1.after_ref
  22.7 4.6 %all-to-all-done.x_ref = bf16[8,288,128]{2,1,0:T(8,128)(2,1)S(1)} async-done(((bf16[8,288,128]{2,1,0:T(8,128)(2,1)}), bf16[8,288,128]{2,1,0:T(8,128)(2,1)S(1)}, u32[]{:S(2)}, u32[]{:S(2)}) %all-to-all-start) | async-done | bytes 589856 | tf_op jit(solution)/shard_map/all_to_all | solution.py:724
  27.4 3.3 %forward_heads.1 = (bf16[8,144,128]{2,1,0:T(8,128)(2,1)S(1)}, f32[1,1024]{1,0:T(1,128)S(1)}) custom-call(s32[4]{0:T(128)S(1)} %pad_add_fusion.info_ref, bf16[8,288,128]{2,1,0:T(8,128)(2,1)S(1)} %all-to-all-done.x_ref), custom_call_target="tpu_custom_call" | custom-call | tf_op jit(solution)/shard_map/forward_heads/pallas_call | solution.py:323
  30.6 14.8 %all_to_all.20.att_ref.refs_4_ = bf16[8,144,128]{2,1,0:T(8,128)(2,1)S(1)} all-to-all(bf16[8,144,128]{2,1,0:T(8,128)(2,1)S(1)} %get-tuple-element.47.head_ref), channel_id=1, replica_groups=mesh['seq'=8,'dp'=4] {'seq'}, dimensions={0} | all-to-all | bytes 589824 | tf_op jit(solution)/shard_map/all_to_all | solution.py:724
  45.4 0.1 collective-permute-start.4
  45.5 1.6 %collective-permute-start.3 = (bf16[8,96,128]{2,1,0:T(8,128)(2,1)S(1)}, bf16[8,96,128]{2,1,0:T(8,128)(2,1)S(1)}, u32[]{:S(2)}, u32[]{:S(2)}) collective-permute-start(bf16[8,96,128]{2,1,0:T(8,128)(2,1)S(1)} %slice.20), channel_id=1, source_target_pairs={{0,2},{1,3},{2,0},{3,1},{4,6},{5,7},{6,4},{7,5},{8,10},{9,11},{10,... | collective-permute-start | bytes 589832 | tf_op jit(solution)/shard_map/ppermute | solution.py:718
  47.0 0.2 collective-permute-start.2
  47.2 11.1 %middle.1 = (bf16[128,1536]{1,0:T(8,128)(2,1)}, bf16[128,1536]{1,0:T(8,128)(2,1)}, bf16[8,96,128]{2,1,0:T(8,128)(2,1)}, bf16[576,128]{1,0:T(8,128)(2,1)S(1)}, bf...) custom-call(s32[4]{0:T(128)S(1)} %pad_add_fusion.info_ref, ...), custom_call_target="tpu_custom_call" | custom-call | tf_op jit(solution)/shard_map/middle/pallas_call | solution.py:520
  58.3 0.0 collective-permute-done.4.refs_7_
  58.3 0.0 collective-permute-done.3.refs_6_
  58.3 0.0 collective-permute-done.2.refs_5_
  58.3 3.4 %all-to-all-start.2 = ((bf16[8,96,128]{2,1,0:T(8,128)(2,1)}), bf16[8,96,128]{2,1,0:T(8,128)(2,1)S(1)}, u32[]{:S(2)}, u32[]{:S(2)}) async-start(bf16[8,96,128]{2,1,0:T(8,128)(2,1)} %get-tuple-element.58), calls=%async_computation.2 | async-start | bytes 393216 | tf_op jit(solution)/shard_map/all_to_all | solution.py:724
  61.8 0.5 collective-permute-start.5
  62.3 1.5 %collective-permute-start.6 = (bf16[576,128]{1,0:T(8,128)(2,1)S(1)}, bf16[576,128]{1,0:T(8,128)(2,1)S(1)}, u32[]{:S(2)}, u32[]{:S(2)}) collective-permute-start(bf16[576,128]{1,0:T(8,128)(2,1)S(1)} %get-tuple-element.61), channel_id=1, source_target_pairs={{0,2},{1,3},{2,0},{3,1},{4,6},{5,7},{6,4},{7,5},{8,10},{9,11},{10,... | collective-permute-start | bytes 442376 | tf_op jit(solution)/shard_map/ppermute | solution.py:718
  63.8 0.0 collective-permute-start.7
  63.8 3.1 %collective-permute-done.5.refs_1_ = bf16[576,128]{1,0:T(8,128)(2,1)S(1)} collective-permute-done((bf16[576,128]{1,0:T(8,128)(2,1)S(1)}, bf16[576,128]{1,0:T(8,128)(2,1)S(1)}, u32[]{:S(2)}, u32[]{:S(2)}) %collective-permute-start.5) | collective-permute-done | bytes 147488 | tf_op jit(solution)/shard_map/ppermute | solution.py:718
  66.9 2.1 %collective-permute-done.6.refs_2_ = bf16[576,128]{1,0:T(8,128)(2,1)S(1)} collective-permute-done((bf16[576,128]{1,0:T(8,128)(2,1)S(1)}, bf16[576,128]{1,0:T(8,128)(2,1)S(1)}, u32[]{:S(2)}, u32[]{:S(2)}) %collective-permute-start.6) | collective-permute-done | bytes 147488 | tf_op jit(solution)/shard_map/ppermute | solution.py:718
  69.0 0.2 collective-permute-done.7.refs_3_
  69.2 1.4 %all-to-all-done.2.grad_ref = bf16[8,96,128]{2,1,0:T(8,128)(2,1)S(1)} async-done(((bf16[8,96,128]{2,1,0:T(8,128)(2,1)}), bf16[8,96,128]{2,1,0:T(8,128)(2,1)S(1)}, u32[]{:S(2)}, u32[]{:S(2)}) %all-to-all-start.2) | async-done | bytes 196640 | tf_op jit(solution)/shard_map/all_to_all | solution.py:724
  70.6 1.6 %product.1 = bf16[8,312,128]{2,1,0:T(8,128)(2,1)} custom-call(bf16[576,128]{1,0:T(8,128)(2,1)S(1)} %get-tuple-element.63.refs_0_, bf16[576,128]{1,0:T(8,128)(2,1)S(1)} %collective-permute-done.5.refs_1_, bf16[576,128]{1,0:T(8,128)(2,1)S(1)} %collective-permute-done.6.refs_2_, bf16[576,128]{1,0:T(8,128)(2,1)S(1)} %collective-permute-done.7.refs_3_, ...), custom_call_target="tpu_custom_call" | custom-call | tf_op jit(solution)/shard_map/product/pallas_call | solution.py:616
  72.2 4.6 %all-to-all-start.3 = ((bf16[8,312,128]{2,1,0:T(8,128)(2,1)}), bf16[8,312,128]{2,1,0:T(8,128)(2,1)S(1)}, u32[]{:S(2)}, u32[]{:S(2)}) async-start(bf16[8,312,128]{2,1,0:T(8,128)(2,1)} %product.1), calls=%async_computation.3 | async-start | bytes 1277952 | tf_op jit(solution)/shard_map/all_to_all | solution.py:724
  76.8 2.6 %backward_heads.1 = (bf16[4,96,128]{2,1,0:T(8,128)(2,1)S(1)}, bf16[4,96,128]{2,1,0:T(8,128)(2,1)S(1)}) custom-call(s32[4]{0:T(128)S(1)} %pad_add_fusion.info_ref, bf16[8,288,128]{2,1,0:T(8,128)(2,1)S(1)} %all-to-all-done.x_ref, bf16[8,96,128]{2,1,0:T(8,128)(2,1)S(1)} %all-to-all-done.2.grad_ref, bf16[8,144,128]{2,1,0:T(8,128)(2,1)S(1)} %get-tuple-element.47.head_ref, ...), custom_call_target="tpu_custom_call" | custom-call | tf_op jit(solution)/shard_map/backward_heads/pallas_call | solution.py:371
  79.4 2.1 %collective-permute-start.8 = (bf16[4,96,128]{2,1,0:T(8,128)(2,1)S(1)}, bf16[4,96,128]{2,1,0:T(8,128)(2,1)S(1)}, u32[]{:S(2)}, u32[]{:S(2)}) collective-permute-start(bf16[4,96,128]{2,1,0:T(8,128)(2,1)S(1)} %get-tuple-element.75), channel_id=1, source_target_pairs={{0,4},{4,0},{8,12},{12,8},{16,20},{20,16},{24,28},{28,24},{1,5},{5... | collective-permute-start | bytes 294920 | tf_op jit(solution)/shard_map/ppermute | solution.py:774
  81.5 6.5 %collective-permute-done.8.other_ref = bf16[4,96,128]{2,1,0:T(8,128)(2,1)S(1)} collective-permute-done((bf16[4,96,128]{2,1,0:T(8,128)(2,1)S(1)}, bf16[4,96,128]{2,1,0:T(8,128)(2,1)S(1)}, u32[]{:S(2)}, u32[]{:S(2)}) %collective-permute-start.8) | collective-permute-done | bytes 98336 | tf_op jit(solution)/shard_map/ppermute | solution.py:774
  88.0 0.6 pair_heads.1
  88.5 0.1 collective-permute-start.9
  88.6 6.2 %collective-permute-start.10 = (bf16[2,96,128]{2,1,0:T(8,128)(2,1)S(1)}, bf16[2,96,128]{2,1,0:T(8,128)(2,1)S(1)}, u32[]{:S(2)}, u32[]{:S(2)}) collective-permute-start(bf16[2,96,128]{2,1,0:T(8,128)(2,1)S(1)} %get-tuple-element.78), channel_id=1, source_target_pairs={{0,16},{4,20},{8,24},{12,28},{16,0},{20,4},{24,8},{28,12},{1,17},{... | collective-permute-start | bytes 147464 | tf_op jit(solution)/shard_map/ppermute | solution.py:718
  94.8 0.0 collective-permute-start.11
  94.8 0.2 all-to-all-done.3.in_ref
  95.1 0.2 sum_shares.1
  95.3 8.2 %all-gather = bf16[1248,128]{1,0:T(8,128)(2,1)S(1)} all-gather(bf16[312,128]{1,0:T(8,128)(2,1)S(1)} %sum_shares.1), channel_id=2, replica_groups=mesh['seq'=8,'dp'=4] {'dp'}, dimensions={0}, use_global_device_ids=true | all-gather | bytes 399360 | tf_op jit(solution)/shard_map/all_gather | solution.py:776
  103.4 0.0 collective-permute-done.9.rest_1_
  103.4 0.0 collective-permute-done.10.rest_2_
  103.4 0.0 collective-permute-done.11.rest_3_
  103.4 1.7 %finish.1 = (f32[192,768]{1,0:T(8,128)}, f32[31,192]{1,0:T(8,128)}, f32[1,192]{1,0:T(1,128)}, bf16[128,768]{1,0:T(8,128)(2,1)}) custom-call(s32[4]{0:T(128)S(1)} %pad_add_fusion.info_ref, bf16[4,312,128]{2,1,0:T(8,128)(2,1)S(1)} %bitcast.21, bf16[2,96,128]{2,1,0:T(8,128)(2,1)S(1)} %get-tuple-element.76.rest_0_, ...), custom_call_target="tpu_custom_call" | custom-call | tf_op jit(solution)/shard_map/finish/pallas_call | solution.py:695
  (5 shorter events, 0.1 us)
Async XLA Ops:
  0.6 9.4 %copy-start = (bf16[1,128,1536]{2,1,0:T(8,128)(2,1)S(1)}, bf16[1,128,1536]{2,1,0:T(8,128)(2,1)}, u32[]{:S(2)}) copy-start(bf16[1,128,1536]{2,1,0:T(8,128)(2,1)} %param.9) | copy-start | bytes 1179652
  0.6 16.1 %copy-start.1 = (f32[1536]{0:T(1024)S(1)}, f32[1536]{0:T(1024)}, u32[]{:S(2)}) copy-start(f32[1536]{0:T(1024)} %param.16) | copy-start | bytes 18436
  2.7 24.6 %all-to-all-start = ((bf16[8,288,128]{2,1,0:T(8,128)(2,1)}), bf16[8,288,128]{2,1,0:T(8,128)(2,1)S(1)}, u32[]{:S(2)}, u32[]{:S(2)}) async-start(bf16[8,288,128]{2,1,0:T(8,128)(2,1)} %pack_heads.1), calls=%async_computation | async-start | bytes 1179648 | tf_op jit(solution)/shard_map/all_to_all | solution.py:724
  10.9 10.9 %collective-permute-start = (bf16[48,1536]{1,0:T(8,128)(2,1)S(1)}, bf16[48,1536]{1,0:T(8,128)(2,1)S(1)}, u32[]{:S(2)}, u32[]{:S(2)}) collective-permute-start(bf16[48,1536]{1,0:T(8,128)(2,1)S(1)} %pad_maximum_fusion), channel_id=1, source_target_pairs={{0,4},{4,8},{8,12},{12,16},{16,20},{20,24},{24,28},{1,5},{5,9},{9,... | collective-permute-start | bytes 442376 | tf_op jit(solution)/shard_map/ppermute | solution.py:743
  14.8 7.9 %collective-permute-start.1 = (bf16[48,1536]{1,0:T(8,128)(2,1)S(1)}, bf16[48,1536]{1,0:T(8,128)(2,1)S(1)}, u32[]{:S(2)}, u32[]{:S(2)}) collective-permute-start(bf16[48,1536]{1,0:T(8,128)(2,1)S(1)} %pad_maximum_fusion.1), channel_id=1, source_target_pairs={{4,0},{8,4},{12,8},{16,12},{20,16},{24,20},{28,24},{5,1},{9,5},{13... | collective-permute-start | bytes 442376 | tf_op jit(solution)/shard_map/ppermute | solution.py:744
  45.4 12.9 %collective-permute-start.4 = (bf16[8,96,128]{2,1,0:T(8,128)(2,1)S(1)}, bf16[8,96,128]{2,1,0:T(8,128)(2,1)S(1)}, u32[]{:S(2)}, u32[]{:S(2)}) collective-permute-start(bf16[8,96,128]{2,1,0:T(8,128)(2,1)S(1)} %slice.20), channel_id=1, source_target_pairs={{0,3},{1,0},{2,1},{3,2},{4,7},{5,4},{6,5},{7,6},{8,11},{9,8},{10,9... | collective-permute-start | bytes 589832 | tf_op jit(solution)/shard_map/ppermute | solution.py:718
  45.5 12.8 %collective-permute-start.3 = (bf16[8,96,128]{2,1,0:T(8,128)(2,1)S(1)}, bf16[8,96,128]{2,1,0:T(8,128)(2,1)S(1)}, u32[]{:S(2)}, u32[]{:S(2)}) collective-permute-start(bf16[8,96,128]{2,1,0:T(8,128)(2,1)S(1)} %slice.20), channel_id=1, source_target_pairs={{0,2},{1,3},{2,0},{3,1},{4,6},{5,7},{6,4},{7,5},{8,10},{9,11},{10,... | collective-permute-start | bytes 589832 | tf_op jit(solution)/shard_map/ppermute | solution.py:718
  47.0 11.3 %collective-permute-start.2 = (bf16[8,96,128]{2,1,0:T(8,128)(2,1)S(1)}, bf16[8,96,128]{2,1,0:T(8,128)(2,1)S(1)}, u32[]{:S(2)}, u32[]{:S(2)}) collective-permute-start(bf16[8,96,128]{2,1,0:T(8,128)(2,1)S(1)} %slice.20), channel_id=1, source_target_pairs={{0,1},{1,2},{2,3},{3,0},{4,5},{5,6},{6,7},{7,4},{8,9},{9,10},{10,1... | collective-permute-start | bytes 589832 | tf_op jit(solution)/shard_map/ppermute | solution.py:718
  58.3 12.2 %all-to-all-start.2 = ((bf16[8,96,128]{2,1,0:T(8,128)(2,1)}), bf16[8,96,128]{2,1,0:T(8,128)(2,1)S(1)}, u32[]{:S(2)}, u32[]{:S(2)}) async-start(bf16[8,96,128]{2,1,0:T(8,128)(2,1)} %get-tuple-element.58), calls=%async_computation.2 | async-start | bytes 393216 | tf_op jit(solution)/shard_map/all_to_all | solution.py:724
  61.8 5.1 %collective-permute-start.5 = (bf16[576,128]{1,0:T(8,128)(2,1)S(1)}, bf16[576,128]{1,0:T(8,128)(2,1)S(1)}, u32[]{:S(2)}, u32[]{:S(2)}) collective-permute-start(bf16[576,128]{1,0:T(8,128)(2,1)S(1)} %get-tuple-element.60), channel_id=1, source_target_pairs={{0,1},{1,2},{2,3},{3,0},{4,5},{5,6},{6,7},{7,4},{8,9},{9,10},{10,1... | collective-permute-start | bytes 442376 | tf_op jit(solution)/shard_map/ppermute | solution.py:718
  62.3 6.7 %collective-permute-start.6 = (bf16[576,128]{1,0:T(8,128)(2,1)S(1)}, bf16[576,128]{1,0:T(8,128)(2,1)S(1)}, u32[]{:S(2)}, u32[]{:S(2)}) collective-permute-start(bf16[576,128]{1,0:T(8,128)(2,1)S(1)} %get-tuple-element.61), channel_id=1, source_target_pairs={{0,2},{1,3},{2,0},{3,1},{4,6},{5,7},{6,4},{7,5},{8,10},{9,11},{10,... | collective-permute-start | bytes 442376 | tf_op jit(solution)/shard_map/ppermute | solution.py:718
  63.8 5.4 %collective-permute-start.7 = (bf16[576,128]{1,0:T(8,128)(2,1)S(1)}, bf16[576,128]{1,0:T(8,128)(2,1)S(1)}, u32[]{:S(2)}, u32[]{:S(2)}) collective-permute-start(bf16[576,128]{1,0:T(8,128)(2,1)S(1)} %get-tuple-element.62), channel_id=1, source_target_pairs={{0,3},{1,0},{2,1},{3,2},{4,7},{5,4},{6,5},{7,6},{8,11},{9,8},{10,9... | collective-permute-start | bytes 442376 | tf_op jit(solution)/shard_map/ppermute | solution.py:718
  72.2 22.9 %all-to-all-start.3 = ((bf16[8,312,128]{2,1,0:T(8,128)(2,1)}), bf16[8,312,128]{2,1,0:T(8,128)(2,1)S(1)}, u32[]{:S(2)}, u32[]{:S(2)}) async-start(bf16[8,312,128]{2,1,0:T(8,128)(2,1)} %product.1), calls=%async_computation.3 | async-start | bytes 1277952 | tf_op jit(solution)/shard_map/all_to_all | solution.py:724
  79.4 8.6 %collective-permute-start.8 = (bf16[4,96,128]{2,1,0:T(8,128)(2,1)S(1)}, bf16[4,96,128]{2,1,0:T(8,128)(2,1)S(1)}, u32[]{:S(2)}, u32[]{:S(2)}) collective-permute-start(bf16[4,96,128]{2,1,0:T(8,128)(2,1)S(1)} %get-tuple-element.75), channel_id=1, source_target_pairs={{0,4},{4,0},{8,12},{12,8},{16,20},{20,16},{24,28},{28,24},{1,5},{5... | collective-permute-start | bytes 294920 | tf_op jit(solution)/shard_map/ppermute | solution.py:774
  88.5 14.9 %collective-permute-start.9 = (bf16[2,96,128]{2,1,0:T(8,128)(2,1)S(1)}, bf16[2,96,128]{2,1,0:T(8,128)(2,1)S(1)}, u32[]{:S(2)}, u32[]{:S(2)}) collective-permute-start(bf16[2,96,128]{2,1,0:T(8,128)(2,1)S(1)} %get-tuple-element.77), channel_id=1, source_target_pairs={{0,8},{4,12},{8,16},{12,20},{16,24},{20,28},{24,0},{28,4},{1,9},{5... | collective-permute-start | bytes 147464 | tf_op jit(solution)/shard_map/ppermute | solution.py:718
  88.6 14.8 %collective-permute-start.10 = (bf16[2,96,128]{2,1,0:T(8,128)(2,1)S(1)}, bf16[2,96,128]{2,1,0:T(8,128)(2,1)S(1)}, u32[]{:S(2)}, u32[]{:S(2)}) collective-permute-start(bf16[2,96,128]{2,1,0:T(8,128)(2,1)S(1)} %get-tuple-element.78), channel_id=1, source_target_pairs={{0,16},{4,20},{8,24},{12,28},{16,0},{20,4},{24,8},{28,12},{1,17},{... | collective-permute-start | bytes 147464 | tf_op jit(solution)/shard_map/ppermute | solution.py:718
  94.8 8.6 %collective-permute-start.11 = (bf16[2,96,128]{2,1,0:T(8,128)(2,1)S(1)}, bf16[2,96,128]{2,1,0:T(8,128)(2,1)S(1)}, u32[]{:S(2)}, u32[]{:S(2)}) collective-permute-start(bf16[2,96,128]{2,1,0:T(8,128)(2,1)S(1)} %get-tuple-element.79), channel_id=1, source_target_pairs={{0,24},{4,28},{8,0},{12,4},{16,8},{20,12},{24,16},{28,20},{1,25},{... | collective-permute-start | bytes 147464 | tf_op jit(solution)/shard_map/ppermute | solution.py:718

commit v6 on v5

--- a/solution.py
+++ b/solution.py
@@ -339,9 +339,27 @@
     )(info, near(received))
 
 
-def backward_kernel(info_ref, x_ref, grad_ref, head_ref, lse_ref, *rest):
-    keep_ref, give_ref, keys_sc, values_sc, wide_sc, result_sc = rest
+def split_sides(place, blocks_ref, keep_ref, give_ref):
+    side = lax.rem(place, 2)
+    for layer in range(keep_ref.shape[0]):
+        keep_ref[layer] = blocks_ref[2 * layer + side]
+        give_ref[layer] = blocks_ref[2 * layer + 1 - side]
+
+
+def join_sides(place, pairs, blocks_ref):
+    count = len(pairs)
+    layer, side = lax.div(place, 2), lax.rem(place, 2)
+    for away, pair_ref in enumerate(pairs):
+        source = 2 * lax.rem(layer - away + count, count)
+        blocks_ref[source + side] = pair_ref[0]
+        blocks_ref[source + 1 - side] = pair_ref[1]
+
+
+def backward_kernel(info_ref, x_ref, head_ref, lse_ref, *rest):
+    pairs, rest = rest[:-7], rest[-7:]
+    keep_ref, give_ref, keys_sc, values_sc, wide_sc, result_sc, grad_ref = rest
     blocks, _, frames = x_ref.shape
+    join_sides(info_ref[3], pairs, grad_ref)
     key_rows(x_ref, info_ref[1], keys_sc)
     side_by_side(x_ref, KEYS, wide_sc)
     for block in range(blocks):
@@ -359,18 +377,15 @@
         result = jnp.dot(wide_sc[...], grad_score, preferred_element_type=F32) * SCORE_SCALE
         result_sc[first] = result[:, :frames].astype(BF16)
         result_sc[first + 1] = result[:, frames:].astype(BF16)
-    side = lax.rem(info_ref[3], 2)
-    for layer in range(blocks // 2):
-        keep_ref[layer] = result_sc[2 * layer + side]
-        give_ref[layer] = result_sc[2 * layer + 1 - side]
-
-
-def backward_heads(info, received, grads, heads, lse):
+    split_sides(info_ref[3], result_sc, keep_ref, give_ref)
+
+
+def backward_heads(info, received, heads, lse, pairs):
     blocks, _, frames = received.shape
     total = blocks * frames
     return pl.pallas_call(
         backward_kernel,
-        in_specs=[SCALARS] + here(4),
+        in_specs=[SCALARS] + here(3 + len(pairs)),
         out_specs=here(2),
         out_shape=[jax.ShapeDtypeStruct((blocks // 2, HS, frames), BF16)] * 2,
         scratch_shapes=[
@@ -378,10 +393,11 @@
             pltpu.VMEM((total, HS), BF16),
             pltpu.VMEM((HS, total), BF16),
             pltpu.VMEM((blocks, HS, frames), BF16),
+            pltpu.VMEM((blocks, HS, frames), BF16),
         ],
         compiler_params=params(),
         name="backward_heads",
-    )(info, near(received), near(grads), heads, lse)
+    )(info, near(received), heads, lse, pairs[0], *[near(pair) for pair in pairs[1:]])
 
 
 def shifted_sum(ref, tile, rows, weight_of, start):
@@ -407,11 +423,12 @@
     bias_ref,
     block_out_ref,
     grad_in_ref,
-    grad_heads_ref,
+    keep_ref,
+    give_ref,
     *rest,
 ):
-    piece_refs = rest[:-6]
-    att_sc, grad_sc, masked_sc, gate_sc, taps_sc, piece_sc = rest[-6:]
+    piece_refs = rest[:-7]
+    att_sc, grad_sc, masked_sc, gate_sc, taps_sc, piece_sc, heads_sc = rest[-7:]
     dp_count = len(piece_refs)
     step = pl.program_id(0)
     frames = input_ref.shape[0]
@@ -508,7 +525,8 @@
 
     @pl.when(step == pl.num_programs(0) - 1)
     def _():
-        grad_heads_ref[...] = grad_sc[...].T.astype(BF16).reshape(H, HS, frames)
+        heads_sc[...] = grad_sc[...].T.astype(BF16).reshape(H, HS, frames)
+        split_sides(info_ref[3], heads_sc, keep_ref, give_ref)
         for away, ref in enumerate(piece_refs):
             ref[...] = piece_sc[lax.rem(mine + away, dp_count)]
 
@@ -534,13 +552,15 @@
         out_specs=[
             column(frames),
             column(frames),
-            whole((H, HS, frames)),
+            whole((H // 2, HS, frames)),
+            whole((H // 2, HS, frames)),
         ]
         + [whole((piece_rows, frames))] * dp_count,
         out_shape=[
             jax.ShapeDtypeStruct((frames, D), BF16),
             jax.ShapeDtypeStruct((frames, D), BF16),
-            jax.ShapeDtypeStruct((H, HS, frames), BF16),
+            jax.ShapeDtypeStruct((H // 2, HS, frames), BF16),
+            jax.ShapeDtypeStruct((H // 2, HS, frames), BF16),
         ]
         + [jax.ShapeDtypeStruct((piece_rows, frames), BF16)] * dp_count,
         scratch_shapes=[
@@ -550,6 +570,7 @@
             pltpu.VMEM((CHUNK // LANES, frames + 2 * SIDE, LANES), F32),
             pltpu.VMEM((TAP_ROWS, 8, CHUNK), F32),
             pltpu.VMEM((dp_count, piece_rows, frames), BF16),
+            pltpu.VMEM((H, HS, frames), BF16),
         ],
         compiler_params=params(),
         name="middle",
@@ -679,12 +700,7 @@
     turned = jnp.concatenate(columns, axis=0).T
     tap_ref[...] = turned[:KW]
     bias_ref[...] = turned[KW : KW + 1]
-    count = len(pairs)
-    layer, side = lax.div(info_ref[3], 2), lax.rem(info_ref[3], 2)
-    for away, pair_ref in enumerate(pairs):
-        source = 2 * lax.rem(layer - away + count, count)
-        heads_sc[source + side] = pair_ref[0]
-        heads_sc[source + 1 - side] = pair_ref[1]
+    join_sides(info_ref[3], pairs, heads_sc)
     query_ref[...] = heads_sc[...].reshape(HD, heads_sc.shape[2]).T
 
 
@@ -724,6 +740,11 @@
     return lax.all_to_all(blocks, axis, split_axis=0, concat_axis=0, tiled=True)
 
 
+def first_stage(info, keep, give, count):
+    other = lax.ppermute(give, "seq", [(i, i ^ 1) for i in range(count)])
+    return pair_heads(info, keep, other)
+
+
 def fast_device(
     block_input, query_proj, key_proj, value_proj, lengths, out_proj, kernel, conv_bias, grad_output
 ):
@@ -750,7 +771,7 @@
     returned = exchange(sent, "seq")
     mine = returned[:, :HS]
     heads = send_round([mine] * dp_count, "dp")[1:]
-    block_output, grad_input, grad_heads, *pieces = middle(
+    block_output, grad_input, keep, give, *pieces = middle(
         info,
         returned,
         block_input[0],
@@ -762,17 +783,17 @@
         bias_row,
         dp_count,
     )
-    grad_heads, heads, pieces = lax.optimization_barrier((grad_heads, heads, pieces))
-
-    grads = exchange(grad_heads, "seq")
+    keep, give, heads, pieces = lax.optimization_barrier((keep, give, heads, pieces))
+
+    paired = first_stage(info, keep, give, seq_count)
     moved = send_round(pieces, "dp")
-    grads, moved = lax.optimization_barrier((grads, moved))
+    grads = send_round(paired, "seq", 2)
+    moved, grads = lax.optimization_barrier((moved, grads))
     shares = product(moved, heads, returned, seq_count)
-    shares, grads = lax.optimization_barrier((shares, grads))
+    later, _ = lax.optimization_barrier((lse, shares))
     shares = exchange(shares, "seq")
-    keep, give = backward_heads(info, received, grads, sent, lse)
-    other = lax.ppermute(give, "seq", [(i, i ^ 1) for i in range(seq_count)])
-    pairs = send_round(pair_heads(info, keep, other), "seq", 2)
+    keep, give = backward_heads(info, received, sent, later, grads)
+    pairs = send_round(first_stage(info, keep, give, seq_count), "seq", 2)
     gathered = lax.all_gather(sum_shares(shares), "dp")
     grad_proj, grad_kernel, grad_bias, grad_query = finish(info, gathered, pairs)
     return (block_output[None], grad_input[None], grad_query[None], grad_proj, grad_kernel, grad_bias[0])

time: 106 us -> 106 us (level)
  waiting for transfers between devices: 23.9 us -> 28.6 us
  starting transfers between devices: 32.8 us -> 29.5 us
  blocking collectives: 22.9 us -> 21 us
    all_to_all x3 -> x2, starting transfers between devices: 15.3 us -> 10.8 us  [exchange(): return lax.all_to_all(blocks, axis, split_axis=0, concat_axis=0, tiled=True)]
    ppermute x9 -> x12, waiting for transfers between devices: 5.37 us -> 7.67 us  [send_round(): lax.ppermute(blocks[away], axis, ring(count, away * stride))]
    all_gather x1, blocking collectives: 8.17 us -> 6.21 us  [fast_device(): gathered = lax.all_gather(sum_shares(shares), 'dp')]
    all_to_all x3 -> x2, waiting for transfers between devices: 6.24 us -> 7.88 us  [exchange(): return lax.all_to_all(blocks, axis, split_axis=0, concat_axis=0, tiled=True)]
    ppermute x1 -> x2, waiting for transfers between devices: 6.47 us -> 7.21 us  [first_stage(): other = lax.ppermute(give, 'seq', [(i, i ^ 1) for i in range(count)])]
    ppermute x1 -> x2, starting transfers between devices: 2.1 us -> 2.75 us  [first_stage(): other = lax.ppermute(give, 'seq', [(i, i ^ 1) for i in range(count)])]
    ppermute x9 -> x12, starting transfers between devices: 10.2 us -> 10.7 us  [send_round(): lax.ppermute(blocks[away], axis, ring(count, away * stride))]
  transfers between devices with their start and end apart: 15 -> 18, of which waited for: 9 -> 9; matrix products, arithmetic and copies ran while one was open for 1% -> 1% of each run, Pallas kernels for 14% -> 14%
where the time goes in v6:
time: 106 us; the launch traced here: 105 us
  starting transfers between devices  29.5 us (28%)
  waiting for transfers between devices  28.6 us (27%)
  Pallas kernels  23.7 us (22%)
  blocking collectives  21 us (20%)
  between operations  1.45 us (1%)
    all_to_all x1, blocking collectives, exchange(): return lax.all_to_all(blocks, axis, split_axis=0, concat_axis=0, tiled=True)  14.8 us
    pallas_call x1, Pallas kernels, middle(): pl.pallas_call(middle_kernel, grid=(D // CHUNK,), in_specs=[SCALARS, here...  11.1 us
    all_to_all x2, starting transfers between devices, exchange(): return lax.all_to_all(blocks, axis, split_axis=0, concat_axis=0, tiled=True)  10.8 us
    ppermute x12, starting transfers between devices, send_round(): lax.ppermute(blocks[away], axis, ring(count, away * stride))  10.7 us
    all_to_all x2, waiting for transfers between devices, exchange(): return lax.all_to_all(blocks, axis, split_axis=0, concat_axis=0, tiled=True)  7.88 us
    ppermute x12, waiting for transfers between devices, send_round(): lax.ppermute(blocks[away], axis, ring(count, away * stride))  7.67 us
    ppermute x2, waiting for transfers between devices, first_stage(): other = lax.ppermute(give, 'seq', [(i, i ^ 1) for i in range(count)])  7.21 us
    all_gather x1, blocking collectives, fast_device(): gathered = lax.all_gather(sum_shares(shares), 'dp')  6.21 us
  transfers between devices with their start and end apart: 18, of which 9 were waited for; matrix products, arithmetic and copies ran while one was open for 1% of the time, Pallas kernels for 14%

profile of v6, /device:TPU:0, one launch (start us, length us, event | category | flops | bytes accessed | tf_op | source)
XLA Modules:
  0.0 105.2 jit_solution(4958351886626758787)
XLA Ops:
  0.6 0.0 copy-start
  0.7 2.1 %pack_heads.1 = bf16[8,288,128]{2,1,0:T(8,128)(2,1)} custom-call(bf16[128,768]{1,0:T(8,128)(2,1)} %bitcast.24, bf16[128,768]{1,0:T(8,128)(2,1)} %bitcast.25, bf16[128,768]{1,0:T(8,128)(2,1)} %bitcast.26), custom_call_target="tpu_custom_call" | custom-call | tf_op jit(solution)/shard_map/pack_heads/pallas_call | solution.py:236
  2.7 7.3 %all-to-all-start = ((bf16[8,288,128]{2,1,0:T(8,128)(2,1)}), bf16[8,288,128]{2,1,0:T(8,128)(2,1)S(1)}, u32[]{:S(2)}, u32[]{:S(2)}) async-start(bf16[8,288,128]{2,1,0:T(8,128)(2,1)} %pack_heads.1), calls=%async_computation | async-start | bytes 1179648 | tf_op jit(solution)/shard_map/all_to_all | solution.py:740
  10.0 0.8 slice_bitcast_fusion.2
  10.9 3.9 %collective-permute-start = (bf16[48,1536]{1,0:T(8,128)(2,1)S(1)}, bf16[48,1536]{1,0:T(8,128)(2,1)S(1)}, u32[]{:S(2)}, u32[]{:S(2)}) collective-permute-start(bf16[48,1536]{1,0:T(8,128)(2,1)S(1)} %pad_maximum_fusion), channel_id=1, source_target_pairs={{0,4},{4,8},{8,12},{12,16},{16,20},{20,24},{24,28},{1,5},{5,9},{9,... | collective-permute-start | bytes 442376 | tf_op jit(solution)/shard_map/ppermute | solution.py:764
  14.8 1.3 %collective-permute-start.1 = (bf16[48,1536]{1,0:T(8,128)(2,1)S(1)}, bf16[48,1536]{1,0:T(8,128)(2,1)S(1)}, u32[]{:S(2)}, u32[]{:S(2)}) collective-permute-start(bf16[48,1536]{1,0:T(8,128)(2,1)S(1)} %pad_maximum_fusion.1), channel_id=1, source_target_pairs={{4,0},{8,4},{12,8},{16,12},{20,16},{24,20},{28,24},{5,1},{9,5},{13... | collective-permute-start | bytes 442376 | tf_op jit(solution)/shard_map/ppermute | solution.py:765
  16.8 0.1 pad_add_fusion.info_ref
  16.9 4.9 %collective-permute-done.before_ref = bf16[48,1536]{1,0:T(8,128)(2,1)S(1)} collective-permute-done((bf16[48,1536]{1,0:T(8,128)(2,1)S(1)}, bf16[48,1536]{1,0:T(8,128)(2,1)S(1)}, u32[]{:S(2)}, u32[]{:S(2)}) %collective-permute-start) | collective-permute-done | bytes 147488 | tf_op jit(solution)/shard_map/ppermute | solution.py:764
  21.8 0.9 collective-permute-done.1.after_ref
  22.7 4.6 %all-to-all-done.x_ref = bf16[8,288,128]{2,1,0:T(8,128)(2,1)S(1)} async-done(((bf16[8,288,128]{2,1,0:T(8,128)(2,1)}), bf16[8,288,128]{2,1,0:T(8,128)(2,1)S(1)}, u32[]{:S(2)}, u32[]{:S(2)}) %all-to-all-start) | async-done | bytes 589856 | tf_op jit(solution)/shard_map/all_to_all | solution.py:740
  27.4 3.3 %forward_heads.1 = (bf16[8,144,128]{2,1,0:T(8,128)(2,1)S(1)}, f32[1,1024]{1,0:T(1,128)S(1)}) custom-call(s32[4]{0:T(128)S(1)} %pad_add_fusion.info_ref, bf16[8,288,128]{2,1,0:T(8,128)(2,1)S(1)} %all-to-all-done.x_ref), custom_call_target="tpu_custom_call" | custom-call | tf_op jit(solution)/shard_map/forward_heads/pallas_call | solution.py:323
  30.6 14.8 %all_to_all.15.att_ref.refs_4_ = bf16[8,144,128]{2,1,0:T(8,128)(2,1)S(1)} all-to-all(bf16[8,144,128]{2,1,0:T(8,128)(2,1)S(1)} %get-tuple-element.55.head_ref), channel_id=1, replica_groups=mesh['seq'=8,'dp'=4] {'seq'}, dimensions={0} | all-to-all | bytes 589824 | tf_op jit(solution)/shard_map/all_to_all | solution.py:740
  45.4 0.1 collective-permute-start.4
  45.5 1.6 %collective-permute-start.3 = (bf16[8,96,128]{2,1,0:T(8,128)(2,1)S(1)}, bf16[8,96,128]{2,1,0:T(8,128)(2,1)S(1)}, u32[]{:S(2)}, u32[]{:S(2)}) collective-permute-start(bf16[8,96,128]{2,1,0:T(8,128)(2,1)S(1)} %slice.20), channel_id=1, source_target_pairs={{0,2},{1,3},{2,0},{3,1},{4,6},{5,7},{6,4},{7,5},{8,10},{9,11},{10,... | collective-permute-start | bytes 589832 | tf_op jit(solution)/shard_map/ppermute | solution.py:734
  47.0 0.2 collective-permute-start.2
  47.2 11.1 %middle.1 = (bf16[128,1536]{1,0:T(8,128)(2,1)}, bf16[128,1536]{1,0:T(8,128)(2,1)}, bf16[4,96,128]{2,1,0:T(8,128)(2,1)S(1)}, bf16[4,96,128]{2,1,0:T(8,128)(2,1)S(...) custom-call(s32[4]{0:T(128)S(1)} %pad_add_fusion.info_ref, ...), custom_call_target="tpu_custom_call" | custom-call | tf_op jit(solution)/shard_map/middle/pallas_call | solution.py:538
  58.3 0.0 collective-permute-done.4.refs_7_
  58.4 0.0 collective-permute-done.3.refs_6_
  58.4 0.0 collective-permute-done.2.refs_5_
  58.4 0.8 collective-permute-start.8
  59.1 0.2 collective-permute-start.5
  59.3 1.5 %collective-permute-start.6 = (bf16[576,128]{1,0:T(8,128)(2,1)S(1)}, bf16[576,128]{1,0:T(8,128)(2,1)S(1)}, u32[]{:S(2)}, u32[]{:S(2)}) collective-permute-start(bf16[576,128]{1,0:T(8,128)(2,1)S(1)} %get-tuple-element.69), channel_id=1, source_target_pairs={{0,2},{1,3},{2,0},{3,1},{4,6},{5,7},{6,4},{7,5},{8,10},{9,11},{10,... | collective-permute-start | bytes 442376 | tf_op jit(solution)/shard_map/ppermute | solution.py:734
  60.8 0.3 collective-permute-start.7
  61.1 2.5 %collective-permute-done.8.other_ref = bf16[4,96,128]{2,1,0:T(8,128)(2,1)S(1)} collective-permute-done((bf16[4,96,128]{2,1,0:T(8,128)(2,1)S(1)}, bf16[4,96,128]{2,1,0:T(8,128)(2,1)S(1)}, u32[]{:S(2)}, u32[]{:S(2)}) %collective-permute-start.8) | collective-permute-done | bytes 98336 | tf_op jit(solution)/shard_map/ppermute | solution.py:744
  63.6 0.6 pair_heads.2
  64.2 0.7 collective-permute-start.9
  64.9 1.7 %collective-permute-start.10 = (bf16[2,96,128]{2,1,0:T(8,128)(2,1)S(1)}, bf16[2,96,128]{2,1,0:T(8,128)(2,1)S(1)}, u32[]{:S(2)}, u32[]{:S(2)}) collective-permute-start(bf16[2,96,128]{2,1,0:T(8,128)(2,1)S(1)} %get-tuple-element.75), channel_id=1, source_target_pairs={{0,16},{4,20},{8,24},{12,28},{16,0},{20,4},{24,8},{28,12},{1,17},{... | collective-permute-start | bytes 147464 | tf_op jit(solution)/shard_map/ppermute | solution.py:734
  66.6 3.6 %collective-permute-done.9.rest_1_ = bf16[2,96,128]{2,1,0:T(8,128)(2,1)S(1)} collective-permute-done((bf16[2,96,128]{2,1,0:T(8,128)(2,1)S(1)}, bf16[2,96,128]{2,1,0:T(8,128)(2,1)S(1)}, u32[]{:S(2)}, u32[]{:S(2)}) %collective-permute-start.9) | collective-permute-done | bytes 49184 | tf_op jit(solution)/shard_map/ppermute | solution.py:734
  70.1 0.0 collective-permute-start.11
  70.1 1.2 %collective-permute-done.10.rest_2_ = bf16[2,96,128]{2,1,0:T(8,128)(2,1)S(1)} collective-permute-done((bf16[2,96,128]{2,1,0:T(8,128)(2,1)S(1)}, bf16[2,96,128]{2,1,0:T(8,128)(2,1)S(1)}, u32[]{:S(2)}, u32[]{:S(2)}) %collective-permute-start.10) | collective-permute-done | bytes 49184 | tf_op jit(solution)/shard_map/ppermute | solution.py:734
  71.3 2.9 %collective-permute-done.11.rest_3_ = bf16[2,96,128]{2,1,0:T(8,128)(2,1)S(1)} collective-permute-done((bf16[2,96,128]{2,1,0:T(8,128)(2,1)S(1)}, bf16[2,96,128]{2,1,0:T(8,128)(2,1)S(1)}, u32[]{:S(2)}, u32[]{:S(2)}) %collective-permute-start.11) | collective-permute-done | bytes 49184 | tf_op jit(solution)/shard_map/ppermute | solution.py:734
  74.2 0.0 collective-permute-done.5.refs_1_
  74.2 0.0 collective-permute-done.6.refs_2_
  74.2 1.6 %product.1 = bf16[8,312,128]{2,1,0:T(8,128)(2,1)} custom-call(bf16[576,128]{1,0:T(8,128)(2,1)S(1)} %get-tuple-element.77.refs_0_, bf16[576,128]{1,0:T(8,128)(2,1)S(1)} %collective-permute-done.5.refs_1_, bf16[576,128]{1,0:T(8,128)(2,1)S(1)} %collective-permute-done.6.refs_2_, bf16[576,128]{1,0:T(8,128)(2,1)S(1)} %collective-permute-done.7.refs_3_, ...), custom_call_target="tpu_custom_call" | custom-call | tf_op jit(solution)/shard_map/product/pallas_call | solution.py:637
  75.9 3.5 %all-to-all-start.2 = ((bf16[8,312,128]{2,1,0:T(8,128)(2,1)}), bf16[8,312,128]{2,1,0:T(8,128)(2,1)S(1)}, u32[]{:S(2)}, u32[]{:S(2)}) async-start(bf16[8,312,128]{2,1,0:T(8,128)(2,1)} %product.1), calls=%async_computation.2 | async-start | bytes 1277952 | tf_op jit(solution)/shard_map/all_to_all | solution.py:740
  79.4 2.6 %backward_heads.1 = (bf16[4,96,128]{2,1,0:T(8,128)(2,1)S(1)}, bf16[4,96,128]{2,1,0:T(8,128)(2,1)S(1)}) custom-call(s32[4]{0:T(128)S(1)} %pad_add_fusion.info_ref, bf16[8,288,128]{2,1,0:T(8,128)(2,1)S(1)} %all-to-all-done.x_ref, bf16[8,144,128]{2,1,0:T(8,128)(2,1)S(1)} %get-tuple-element.55.head_ref, f32[1,1024]{1,0:T(1,128)S(1)} %get-tuple-element.85.lse_ref, ...), custom_call_target="tpu_custom_call" | custom-call | tf_op jit(solution)/shard_map/backward_heads/pallas_call | solution.py:386
  82.0 2.0 %collective-permute-start.12 = (bf16[4,96,128]{2,1,0:T(8,128)(2,1)S(1)}, bf16[4,96,128]{2,1,0:T(8,128)(2,1)S(1)}, u32[]{:S(2)}, u32[]{:S(2)}) collective-permute-start(bf16[4,96,128]{2,1,0:T(8,128)(2,1)S(1)} %get-tuple-element.91), channel_id=1, source_target_pairs={{0,4},{4,0},{8,12},{12,8},{16,20},{20,16},{24,28},{28,24},{1,5},{5... | collective-permute-start | bytes 294920 | tf_op jit(solution)/shard_map/ppermute | solution.py:744
  84.0 4.7 %collective-permute-done.12.other_ref = bf16[4,96,128]{2,1,0:T(8,128)(2,1)S(1)} collective-permute-done((bf16[4,96,128]{2,1,0:T(8,128)(2,1)S(1)}, bf16[4,96,128]{2,1,0:T(8,128)(2,1)S(1)}, u32[]{:S(2)}, u32[]{:S(2)}) %collective-permute-start.12) | collective-permute-done | bytes 98336 | tf_op jit(solution)/shard_map/ppermute | solution.py:744
  88.7 0.6 pair_heads.3
  89.3 0.7 collective-permute-start.13
  89.9 3.9 %collective-permute-start.14 = (bf16[2,96,128]{2,1,0:T(8,128)(2,1)S(1)}, bf16[2,96,128]{2,1,0:T(8,128)(2,1)S(1)}, u32[]{:S(2)}, u32[]{:S(2)}) collective-permute-start(bf16[2,96,128]{2,1,0:T(8,128)(2,1)S(1)} %get-tuple-element.94), channel_id=1, source_target_pairs={{0,16},{4,20},{8,24},{12,28},{16,0},{20,4},{24,8},{28,12},{1,17},{... | collective-permute-start | bytes 147464 | tf_op jit(solution)/shard_map/ppermute | solution.py:734
  93.8 3.3 %all-to-all-done.2.in_ref = bf16[8,312,128]{2,1,0:T(8,128)(2,1)S(1)} async-done(((bf16[8,312,128]{2,1,0:T(8,128)(2,1)}), bf16[8,312,128]{2,1,0:T(8,128)(2,1)S(1)}, u32[]{:S(2)}, u32[]{:S(2)}) %all-to-all-start.2) | async-done | bytes 639008 | tf_op jit(solution)/shard_map/all_to_all | solution.py:740
  97.1 0.2 sum_shares.1
  97.3 6.2 %all-gather = bf16[1248,128]{1,0:T(8,128)(2,1)S(1)} all-gather(bf16[312,128]{1,0:T(8,128)(2,1)S(1)} %sum_shares.1), channel_id=2, replica_groups=mesh['seq'=8,'dp'=4] {'dp'}, dimensions={0}, use_global_device_ids=true | all-gather | bytes 399360 | tf_op jit(solution)/shard_map/all_gather | solution.py:797
  103.5 0.0 collective-permute-done.13.rest_1_
  103.5 0.0 collective-permute-done.14.rest_2_
  103.5 0.0 collective-permute-done.15.rest_3_
  103.5 1.7 %finish.1 = (f32[192,768]{1,0:T(8,128)}, f32[31,192]{1,0:T(8,128)}, f32[1,192]{1,0:T(1,128)}, bf16[128,768]{1,0:T(8,128)(2,1)}) custom-call(s32[4]{0:T(128)S(1)} %pad_add_fusion.info_ref, bf16[4,312,128]{2,1,0:T(8,128)(2,1)S(1)} %bitcast.21, bf16[2,96,128]{2,1,0:T(8,128)(2,1)S(1)} %get-tuple-element.92.rest_0_, ...), custom_call_target="tpu_custom_call" | custom-call | tf_op jit(solution)/shard_map/finish/pallas_call | solution.py:711
  (10 shorter events, 0.1 us)
Async XLA Ops:
  0.6 9.4 %copy-start = (bf16[1,128,1536]{2,1,0:T(8,128)(2,1)S(1)}, bf16[1,128,1536]{2,1,0:T(8,128)(2,1)}, u32[]{:S(2)}) copy-start(bf16[1,128,1536]{2,1,0:T(8,128)(2,1)} %param.9) | copy-start | bytes 1179652
  0.6 16.1 %copy-start.1 = (f32[1536]{0:T(1024)S(1)}, f32[1536]{0:T(1024)}, u32[]{:S(2)}) copy-start(f32[1536]{0:T(1024)} %param.16) | copy-start | bytes 18436
  2.7 24.6 %all-to-all-start = ((bf16[8,288,128]{2,1,0:T(8,128)(2,1)}), bf16[8,288,128]{2,1,0:T(8,128)(2,1)S(1)}, u32[]{:S(2)}, u32[]{:S(2)}) async-start(bf16[8,288,128]{2,1,0:T(8,128)(2,1)} %pack_heads.1), calls=%async_computation | async-start | bytes 1179648 | tf_op jit(solution)/shard_map/all_to_all | solution.py:740
  10.9 10.9 %collective-permute-start = (bf16[48,1536]{1,0:T(8,128)(2,1)S(1)}, bf16[48,1536]{1,0:T(8,128)(2,1)S(1)}, u32[]{:S(2)}, u32[]{:S(2)}) collective-permute-start(bf16[48,1536]{1,0:T(8,128)(2,1)S(1)} %pad_maximum_fusion), channel_id=1, source_target_pairs={{0,4},{4,8},{8,12},{12,16},{16,20},{20,24},{24,28},{1,5},{5,9},{9,... | collective-permute-start | bytes 442376 | tf_op jit(solution)/shard_map/ppermute | solution.py:764
  14.8 7.9 %collective-permute-start.1 = (bf16[48,1536]{1,0:T(8,128)(2,1)S(1)}, bf16[48,1536]{1,0:T(8,128)(2,1)S(1)}, u32[]{:S(2)}, u32[]{:S(2)}) collective-permute-start(bf16[48,1536]{1,0:T(8,128)(2,1)S(1)} %pad_maximum_fusion.1), channel_id=1, source_target_pairs={{4,0},{8,4},{12,8},{16,12},{20,16},{24,20},{28,24},{5,1},{9,5},{13... | collective-permute-start | bytes 442376 | tf_op jit(solution)/shard_map/ppermute | solution.py:765
  45.4 12.9 %collective-permute-start.4 = (bf16[8,96,128]{2,1,0:T(8,128)(2,1)S(1)}, bf16[8,96,128]{2,1,0:T(8,128)(2,1)S(1)}, u32[]{:S(2)}, u32[]{:S(2)}) collective-permute-start(bf16[8,96,128]{2,1,0:T(8,128)(2,1)S(1)} %slice.20), channel_id=1, source_target_pairs={{0,3},{1,0},{2,1},{3,2},{4,7},{5,4},{6,5},{7,6},{8,11},{9,8},{10,9... | collective-permute-start | bytes 589832 | tf_op jit(solution)/shard_map/ppermute | solution.py:734
  45.5 12.9 %collective-permute-start.3 = (bf16[8,96,128]{2,1,0:T(8,128)(2,1)S(1)}, bf16[8,96,128]{2,1,0:T(8,128)(2,1)S(1)}, u32[]{:S(2)}, u32[]{:S(2)}) collective-permute-start(bf16[8,96,128]{2,1,0:T(8,128)(2,1)S(1)} %slice.20), channel_id=1, source_target_pairs={{0,2},{1,3},{2,0},{3,1},{4,6},{5,7},{6,4},{7,5},{8,10},{9,11},{10,... | collective-permute-start | bytes 589832 | tf_op jit(solution)/shard_map/ppermute | solution.py:734
  47.0 11.3 %collective-permute-start.2 = (bf16[8,96,128]{2,1,0:T(8,128)(2,1)S(1)}, bf16[8,96,128]{2,1,0:T(8,128)(2,1)S(1)}, u32[]{:S(2)}, u32[]{:S(2)}) collective-permute-start(bf16[8,96,128]{2,1,0:T(8,128)(2,1)S(1)} %slice.20), channel_id=1, source_target_pairs={{0,1},{1,2},{2,3},{3,0},{4,5},{5,6},{6,7},{7,4},{8,9},{9,10},{10,1... | collective-permute-start | bytes 589832 | tf_op jit(solution)/shard_map/ppermute | solution.py:734
  58.4 5.3 %collective-permute-start.8 = (bf16[4,96,128]{2,1,0:T(8,128)(2,1)S(1)}, bf16[4,96,128]{2,1,0:T(8,128)(2,1)S(1)}, u32[]{:S(2)}, u32[]{:S(2)}) collective-permute-start(bf16[4,96,128]{2,1,0:T(8,128)(2,1)S(1)} %get-tuple-element.72), channel_id=1, source_target_pairs={{0,4},{4,0},{8,12},{12,8},{16,20},{20,16},{24,28},{28,24},{1,5},{5... | collective-permute-start | bytes 294920 | tf_op jit(solution)/shard_map/ppermute | solution.py:744
  59.1 15.1 %collective-permute-start.5 = (bf16[576,128]{1,0:T(8,128)(2,1)S(1)}, bf16[576,128]{1,0:T(8,128)(2,1)S(1)}, u32[]{:S(2)}, u32[]{:S(2)}) collective-permute-start(bf16[576,128]{1,0:T(8,128)(2,1)S(1)} %get-tuple-element.68), channel_id=1, source_target_pairs={{0,1},{1,2},{2,3},{3,0},{4,5},{5,6},{6,7},{7,4},{8,9},{9,10},{10,1... | collective-permute-start | bytes 442376 | tf_op jit(solution)/shard_map/ppermute | solution.py:734
  59.3 14.9 %collective-permute-start.6 = (bf16[576,128]{1,0:T(8,128)(2,1)S(1)}, bf16[576,128]{1,0:T(8,128)(2,1)S(1)}, u32[]{:S(2)}, u32[]{:S(2)}) collective-permute-start(bf16[576,128]{1,0:T(8,128)(2,1)S(1)} %get-tuple-element.69), channel_id=1, source_target_pairs={{0,2},{1,3},{2,0},{3,1},{4,6},{5,7},{6,4},{7,5},{8,10},{9,11},{10,... | collective-permute-start | bytes 442376 | tf_op jit(solution)/shard_map/ppermute | solution.py:734
  60.8 13.4 %collective-permute-start.7 = (bf16[576,128]{1,0:T(8,128)(2,1)S(1)}, bf16[576,128]{1,0:T(8,128)(2,1)S(1)}, u32[]{:S(2)}, u32[]{:S(2)}) collective-permute-start(bf16[576,128]{1,0:T(8,128)(2,1)S(1)} %get-tuple-element.70), channel_id=1, source_target_pairs={{0,3},{1,0},{2,1},{3,2},{4,7},{5,4},{6,5},{7,6},{8,11},{9,8},{10,9... | collective-permute-start | bytes 442376 | tf_op jit(solution)/shard_map/ppermute | solution.py:734
  64.2 5.9 %collective-permute-start.9 = (bf16[2,96,128]{2,1,0:T(8,128)(2,1)S(1)}, bf16[2,96,128]{2,1,0:T(8,128)(2,1)S(1)}, u32[]{:S(2)}, u32[]{:S(2)}) collective-permute-start(bf16[2,96,128]{2,1,0:T(8,128)(2,1)S(1)} %get-tuple-element.74), channel_id=1, source_target_pairs={{0,8},{4,12},{8,16},{12,20},{16,24},{20,28},{24,0},{28,4},{1,9},{5... | collective-permute-start | bytes 147464 | tf_op jit(solution)/shard_map/ppermute | solution.py:734
  64.9 6.4 %collective-permute-start.10 = (bf16[2,96,128]{2,1,0:T(8,128)(2,1)S(1)}, bf16[2,96,128]{2,1,0:T(8,128)(2,1)S(1)}, u32[]{:S(2)}, u32[]{:S(2)}) collective-permute-start(bf16[2,96,128]{2,1,0:T(8,128)(2,1)S(1)} %get-tuple-element.75), channel_id=1, source_target_pairs={{0,16},{4,20},{8,24},{12,28},{16,0},{20,4},{24,8},{28,12},{1,17},{... | collective-permute-start | bytes 147464 | tf_op jit(solution)/shard_map/ppermute | solution.py:734
  70.1 4.1 %collective-permute-start.11 = (bf16[2,96,128]{2,1,0:T(8,128)(2,1)S(1)}, bf16[2,96,128]{2,1,0:T(8,128)(2,1)S(1)}, u32[]{:S(2)}, u32[]{:S(2)}) collective-permute-start(bf16[2,96,128]{2,1,0:T(8,128)(2,1)S(1)} %get-tuple-element.76), channel_id=1, source_target_pairs={{0,24},{4,28},{8,0},{12,4},{16,8},{20,12},{24,16},{28,20},{1,25},{... | collective-permute-start | bytes 147464 | tf_op jit(solution)/shard_map/ppermute | solution.py:734
  75.9 21.2 %all-to-all-start.2 = ((bf16[8,312,128]{2,1,0:T(8,128)(2,1)}), bf16[8,312,128]{2,1,0:T(8,128)(2,1)S(1)}, u32[]{:S(2)}, u32[]{:S(2)}) async-start(bf16[8,312,128]{2,1,0:T(8,128)(2,1)} %product.1), calls=%async_computation.2 | async-start | bytes 1277952 | tf_op jit(solution)/shard_map/all_to_all | solution.py:740
  82.0 6.7 %collective-permute-start.12 = (bf16[4,96,128]{2,1,0:T(8,128)(2,1)S(1)}, bf16[4,96,128]{2,1,0:T(8,128)(2,1)S(1)}, u32[]{:S(2)}, u32[]{:S(2)}) collective-permute-start(bf16[4,96,128]{2,1,0:T(8,128)(2,1)S(1)} %get-tuple-element.91), channel_id=1, source_target_pairs={{0,4},{4,0},{8,12},{12,8},{16,20},{20,16},{24,28},{28,24},{1,5},{5... | collective-permute-start | bytes 294920 | tf_op jit(solution)/shard_map/ppermute | solution.py:744
  89.3 14.2 %collective-permute-start.13 = (bf16[2,96,128]{2,1,0:T(8,128)(2,1)S(1)}, bf16[2,96,128]{2,1,0:T(8,128)(2,1)S(1)}, u32[]{:S(2)}, u32[]{:S(2)}) collective-permute-start(bf16[2,96,128]{2,1,0:T(8,128)(2,1)S(1)} %get-tuple-element.93), channel_id=1, source_target_pairs={{0,8},{4,12},{8,16},{12,20},{16,24},{20,28},{24,0},{28,4},{1,9},{5... | collective-permute-start | bytes 147464 | tf_op jit(solution)/shard_map/ppermute | solution.py:734
  89.9 13.5 %collective-permute-start.14 = (bf16[2,96,128]{2,1,0:T(8,128)(2,1)S(1)}, bf16[2,96,128]{2,1,0:T(8,128)(2,1)S(1)}, u32[]{:S(2)}, u32[]{:S(2)}) collective-permute-start(bf16[2,96,128]{2,1,0:T(8,128)(2,1)S(1)} %get-tuple-element.94), channel_id=1, source_target_pairs={{0,16},{4,20},{8,24},{12,28},{16,0},{20,4},{24,8},{28,12},{1,17},{... | collective-permute-start | bytes 147464 | tf_op jit(solution)/shard_map/ppermute | solution.py:734
  93.8 9.7 %collective-permute-start.15 = (bf16[2,96,128]{2,1,0:T(8,128)(2,1)S(1)}, bf16[2,96,128]{2,1,0:T(8,128)(2,1)S(1)}, u32[]{:S(2)}, u32[]{:S(2)}) collective-permute-start(bf16[2,96,128]{2,1,0:T(8,128)(2,1)S(1)} %get-tuple-element.95), channel_id=1, source_target_pairs={{0,24},{4,28},{8,0},{12,4},{16,8},{20,12},{24,16},{28,20},{1,25},{... | collective-permute-start | bytes 147464 | tf_op jit(solution)/shard_map/ppermute | solution.py:734
